TPU v7x, 32 devices: a whole 2x2x4 slice. The times are simulated.
32 devices in a mesh: dp: 8 (over y, x, core), seq: 4 (over z).
Axes of the slice: x: 2, y: 2, z: 4, core: 2. Of those that a mesh axis runs over, the one named last changes fastest.
Arguments:
- layer_input: bfloat16 [16, 1024, 1536], P('dp', 'seq'), may hold values from -6 to 6
- attn_gain: bfloat16 [1536], P('dp'), may hold values from 0.099609375 to 1.8984375
- query_weight: bfloat16 [1536, 1536], P('dp'), may hold values from -0.15625 to 0.15625
- key_matrix: bfloat16 [1536, 768], P('dp'), may hold values from -0.15625 to 0.15625
- value_matrix: bfloat16 [1536, 768], P('dp'), may hold values from -0.15625 to 0.15625
- output_weight: bfloat16 [1536, 1536], P('dp'), may hold values from -2.5 to 2.5
- ffn_gain: bfloat16 [1536], P('dp'), may hold values from 0.099609375 to 1.8984375
- gate_weight: bfloat16 [1536, 4096], P('dp'), may hold values from -0.15625 to 0.15625
- up_weight: bfloat16 [1536, 4096], P('dp'), may hold values from -0.15625 to 0.15625
- down_weight: bfloat16 [4096, 1536], P('dp'), may hold values from -0.09375 to 0.09375
- cotangent: bfloat16 [16, 1024, 1536], P('dp', 'seq'), may hold values from -6 to 6
Outputs:
- layer_output: bfloat16 [16, 1024, 1536], P('dp', 'seq')
- input_grad: float32 [16, 1024, 1536], P('dp', 'seq')
- attn_gain_grad: float32 [1536], P('dp')
- query_weight_grad: float32 [1536, 1536], P('dp')
- key_weight_grad: float32 [1536, 768], P('dp')
- value_weight_grad: float32 [1536, 768], P('dp')
- output_weight_grad: float32 [1536, 1536], P('dp')
- ffn_gain_grad: float32 [1536], P('dp')
- gate_weight_grad: float32 [1536, 4096], P('dp')
- up_weight_grad: float32 [1536, 4096], P('dp')
- down_weight_grad: float32 [4096, 1536], P('dp')
All inputs are finite; a program needn't handle non-finite values.
Results may differ from a plain program's by a relative error of at most 0.019.
Values may be sent and summed in bfloat16 or wider, within the bound.
No kernel may reach another device: no remote copies, remote signals or barrier semaphores. Data moves between devices by JAX's collectives and lax.ppermute only.
A program may use at most 320 MiB of HBM per device.

v0:
```python
import jax
import jax.numpy as jnp
from jax import lax
from jax.sharding import PartitionSpec as P

QUERY_HEADS = 16
KEY_VALUE_HEADS = 8
HEAD_SIZE = 96


eps = 1e-06
theta_base = 100000.0


def rope_tables(count, start_offset, width):
    half = width // 2
    freq = theta_base ** (-(jnp.arange(half).astype(jnp.float32) * 2.0) / width)
    places = (start_offset + jnp.arange(count)).astype(jnp.float32)
    angle = places[:, None] * freq[None, :]
    angle = jnp.concatenate([angle, angle], axis=1)
    return (jnp.cos(angle), jnp.sin(angle))


def rotate(field):
    half = field.shape[-1] // 2
    return jnp.concatenate([-field[..., half:], field[..., :half]], axis=-1)


def rope_forward(field, cosine_table, sine_table):
    return field * cosine_table + rotate(field) * sine_table


def rotary_backward(field, cosine_table, sine_table):
    return field * cosine_table - rotate(field) * sine_table


def norm_backward(grad_norm, unit, gain, inverse):
    scaled = grad_norm * gain
    return inverse * (scaled - unit * jnp.mean(scaled * unit, axis=-1, keepdims=True))


def times_transposed(left, right):
    return lax.dot_general(
        left, right, (((1,), (1,)), ((), ())), preferred_element_type=jnp.float32
    )


def transposed_times(left, right):
    return lax.dot_general(
        left, right, (((0,), (0,)), ((), ())), preferred_element_type=jnp.float32
    )


def block_probs(query_block, key_block, start_offset, logsum_block):
    block = query_block.shape[1]
    stop = key_block.shape[1]
    scores = jnp.einsum(
        "sqgcd,skcd->sgcqk", query_block, key_block, preferred_element_type=jnp.float32
    ) * HEAD_SIZE ** (-0.5)
    causal = (start_offset + jnp.arange(block))[:, None] >= jnp.arange(stop)[None, :]
    if logsum_block is None:
        masked = jnp.where(causal, scores, -1e30)
        peak = jnp.max(masked, axis=-1, keepdims=True)
        logsum_block = peak + jnp.log(jnp.sum(jnp.exp(masked - peak), axis=-1, keepdims=True))
    probs = jnp.where(causal, jnp.exp(scores - logsum_block), 0.0)
    return (probs, logsum_block)


def body(
    layer_input,
    attn_gain,
    query_weight,
    key_matrix,
    value_matrix,
    output_weight,
    ffn_gain,
    gate_weight,
    up_weight,
    down_weight,
    cotangent,
):
    sequence_count, local_length, width = layer_input.shape
    token_rows = sequence_count * local_length
    shard_count = lax.axis_size("seq")
    length = local_length * shard_count
    query_group_count = QUERY_HEADS // KEY_VALUE_HEADS
    local_key_value = KEY_VALUE_HEADS // shard_count
    scale = HEAD_SIZE ** (-0.5)
    half_precision = jnp.bfloat16
    query_all, key_all, value_all, output_all, gain_one = (
        lax.all_gather(query_weight, "dp", axis=0, tiled=True),
        lax.all_gather(key_matrix, "dp", axis=0, tiled=True),
        lax.all_gather(value_matrix, "dp", axis=0, tiled=True),
        lax.all_gather(output_weight, "dp", axis=0, tiled=True),
        lax.all_gather(attn_gain, "dp", axis=0, tiled=True),
    )
    gate_all, up_all, down_all, gain_two = (
        lax.all_gather(gate_weight, "dp", axis=0, tiled=True),
        lax.all_gather(up_weight, "dp", axis=0, tiled=True),
        lax.all_gather(down_weight, "dp", axis=0, tiled=True),
        lax.all_gather(ffn_gain, "dp", axis=0, tiled=True),
    )
    gain_one = gain_one.astype(jnp.float32)
    gain_two = gain_two.astype(jnp.float32)
    resid_in = layer_input.reshape(token_rows, width).astype(jnp.float32)
    inv_one = lax.rsqrt(jnp.mean(resid_in * resid_in, axis=-1, keepdims=True) + eps)
    unit_one = resid_in * inv_one
    first_normed = (unit_one * gain_one).astype(half_precision)
    cosine_table, sine_table = rope_tables(
        local_length, lax.axis_index("seq") * local_length, HEAD_SIZE
    )
    query_rows = jnp.dot(first_normed, query_all, preferred_element_type=jnp.float32).reshape(
        sequence_count, local_length, QUERY_HEADS, HEAD_SIZE
    )
    key_rows = jnp.dot(first_normed, key_all, preferred_element_type=jnp.float32).reshape(
        sequence_count, local_length, KEY_VALUE_HEADS, HEAD_SIZE
    )
    value_rows = jnp.dot(first_normed, value_all, preferred_element_type=jnp.float32)
    query_rows = rope_forward(query_rows, cosine_table[:, None, :], sine_table[:, None, :]).astype(
        half_precision
    )
    key_rows = rope_forward(key_rows, cosine_table[:, None, :], sine_table[:, None, :]).astype(
        half_precision
    )
    query_rows = query_rows.reshape(
        sequence_count, local_length, query_group_count, KEY_VALUE_HEADS * HEAD_SIZE
    )
    paired = jnp.stack(
        [
            key_rows.reshape(sequence_count, local_length, KEY_VALUE_HEADS * HEAD_SIZE),
            value_rows.astype(half_precision).reshape(
                sequence_count, local_length, KEY_VALUE_HEADS * HEAD_SIZE
            ),
        ],
        axis=2,
    )
    query_heads, pair_heads = (
        lax.all_to_all(query_rows, "seq", split_axis=3, concat_axis=1, tiled=True),
        lax.all_to_all(paired, "seq", split_axis=3, concat_axis=1, tiled=True),
    )
    query_heads = query_heads.reshape(
        sequence_count, length, query_group_count, local_key_value, HEAD_SIZE
    )
    key_heads = pair_heads[:, :, 0].reshape(sequence_count, length, local_key_value, HEAD_SIZE)
    value_heads = pair_heads[:, :, 1].reshape(sequence_count, length, local_key_value, HEAD_SIZE)
    block = min(512, length)
    count = length // block
    attended_blocks = []
    logsums = []
    for index in range(count):
        start_offset = index * block
        stop = start_offset + block
        probs, logsum_block = block_probs(
            query_heads[:, start_offset:stop], key_heads[:, :stop], start_offset, None
        )
        logsums.append(logsum_block)
        probs_half = probs.astype(half_precision)
        attended_blocks.append(
            jnp.einsum(
                "sgcqk,skcd->sqgcd",
                probs_half,
                value_heads[:, :stop],
                preferred_element_type=jnp.float32,
            ).astype(half_precision)
        )
    attended_heads = jnp.concatenate(attended_blocks, axis=1)
    attended_tok = lax.all_to_all(
        attended_heads.reshape(
            sequence_count, length, query_group_count, local_key_value * HEAD_SIZE
        ),
        "seq",
        split_axis=1,
        concat_axis=3,
        tiled=True,
    )
    flat_att = attended_tok.reshape(token_rows, QUERY_HEADS * HEAD_SIZE)
    resid_mid = resid_in + jnp.dot(flat_att, output_all, preferred_element_type=jnp.float32)
    inv_two = lax.rsqrt(jnp.mean(resid_mid * resid_mid, axis=-1, keepdims=True) + eps)
    unit_two = resid_mid * inv_two
    normed_two = (unit_two * gain_two).astype(half_precision)
    gate = jnp.dot(normed_two, gate_all, preferred_element_type=jnp.float32)
    upward = jnp.dot(normed_two, up_all, preferred_element_type=jnp.float32)
    sigma = jax.nn.sigmoid(gate)
    silu_gate = gate * sigma
    hidden = (silu_gate * upward).astype(half_precision)
    layer_output = (
        resid_mid + jnp.dot(hidden, down_all, preferred_element_type=jnp.float32)
    ).astype(half_precision)
    upstream = cotangent.reshape(token_rows, width)
    grad_hidden = times_transposed(upstream, down_all)
    down_grad = transposed_times(hidden, upstream)
    grad_gate = (grad_hidden * upward * sigma * (1.0 + gate * (1.0 - sigma))).astype(half_precision)
    grad_up = (grad_hidden * silu_gate).astype(half_precision)
    gate_grad = transposed_times(normed_two, grad_gate)
    up_grad = transposed_times(normed_two, grad_up)
    grad_norm_two = times_transposed(grad_gate, gate_all) + times_transposed(grad_up, up_all)
    ffn_gain_grad = jnp.sum(grad_norm_two * unit_two, axis=0)
    gate_grad, up_grad, down_grad, ffn_gain_grad = (
        lax.psum_scatter(
            gate_grad.astype(jnp.bfloat16), "dp", scatter_dimension=0, tiled=True
        ).astype(jnp.float32),
        lax.psum_scatter(
            up_grad.astype(jnp.bfloat16), "dp", scatter_dimension=0, tiled=True
        ).astype(jnp.float32),
        lax.psum_scatter(
            down_grad.astype(jnp.bfloat16), "dp", scatter_dimension=0, tiled=True
        ).astype(jnp.float32),
        lax.psum_scatter(
            ffn_gain_grad.astype(jnp.bfloat16), "dp", scatter_dimension=0, tiled=True
        ).astype(jnp.float32),
    )
    gate_grad, up_grad, down_grad, ffn_gain_grad = (
        lax.psum(gate_grad.astype(jnp.bfloat16), "seq").astype(jnp.float32),
        lax.psum(up_grad.astype(jnp.bfloat16), "seq").astype(jnp.float32),
        lax.psum(down_grad.astype(jnp.bfloat16), "seq").astype(jnp.float32),
        lax.psum(ffn_gain_grad.astype(jnp.bfloat16), "seq").astype(jnp.float32),
    )
    grad_mid = upstream.astype(jnp.float32) + norm_backward(
        grad_norm_two, unit_two, gain_two, inv_two
    )
    grad_mid_half = grad_mid.astype(half_precision)
    out_grad = transposed_times(flat_att, grad_mid_half)
    grad_att = (
        times_transposed(grad_mid_half, output_all)
        .astype(half_precision)
        .reshape(sequence_count, local_length, query_group_count, KEY_VALUE_HEADS * HEAD_SIZE)
    )
    grad_heads = lax.all_to_all(grad_att, "seq", split_axis=3, concat_axis=1, tiled=True)
    grad_heads = grad_heads.reshape(
        sequence_count, length, query_group_count, local_key_value, HEAD_SIZE
    )
    query_grad_blocks = []
    key_gradient = jnp.zeros((sequence_count, length, local_key_value, HEAD_SIZE), jnp.float32)
    value_gradient = jnp.zeros((sequence_count, length, local_key_value, HEAD_SIZE), jnp.float32)
    for index in range(count):
        start_offset = index * block
        stop = start_offset + block
        query_block = query_heads[:, start_offset:stop]
        key_block = key_heads[:, :stop]
        value_block = value_heads[:, :stop]
        grad_block = grad_heads[:, start_offset:stop]
        probs, unused = block_probs(query_block, key_block, start_offset, logsums[index])
        probs_half = probs.astype(half_precision)
        grad_probs = jnp.einsum(
            "sqgcd,skcd->sgcqk", grad_block, value_block, preferred_element_type=jnp.float32
        )
        delta = jnp.sum(
            grad_block.astype(jnp.float32)
            * attended_heads[:, start_offset:stop].astype(jnp.float32),
            axis=-1,
        )
        delta = jnp.transpose(delta, (0, 2, 3, 1))[..., None]
        grad_scores = (probs * (grad_probs - delta)).astype(half_precision)
        query_grad_blocks.append(
            jnp.einsum(
                "sgcqk,skcd->sqgcd", grad_scores, key_block, preferred_element_type=jnp.float32
            )
            * scale
        )
        key_part = (
            jnp.einsum(
                "sgcqk,sqgcd->skcd", grad_scores, query_block, preferred_element_type=jnp.float32
            )
            * scale
        )
        value_part = jnp.einsum(
            "sgcqk,sqgcd->skcd", probs_half, grad_block, preferred_element_type=jnp.float32
        )
        padding = ((0, 0), (0, length - stop), (0, 0), (0, 0))
        key_gradient = key_gradient + jnp.pad(key_part, padding)
        value_gradient = value_gradient + jnp.pad(value_part, padding)
    grad_queries = jnp.concatenate(query_grad_blocks, axis=1)
    cos_full, sin_full = rope_tables(length, 0, HEAD_SIZE)
    queries_back = rotary_backward(
        grad_queries, cos_full[:, None, None, :], sin_full[:, None, None, :]
    ).astype(half_precision)
    key_rows_restored = rotary_backward(
        key_gradient, cos_full[:, None, :], sin_full[:, None, :]
    ).astype(half_precision)
    value_rows_restored = value_gradient.astype(half_precision)
    queries_back = queries_back.reshape(
        sequence_count, length, query_group_count, local_key_value * HEAD_SIZE
    )
    pair_back = jnp.stack(
        [
            key_rows_restored.reshape(sequence_count, length, local_key_value * HEAD_SIZE),
            value_rows_restored.reshape(sequence_count, length, local_key_value * HEAD_SIZE),
        ],
        axis=2,
    )
    queries_tok, paired_token_rows = (
        lax.all_to_all(queries_back, "seq", split_axis=1, concat_axis=3, tiled=True),
        lax.all_to_all(pair_back, "seq", split_axis=1, concat_axis=3, tiled=True),
    )
    queries_tok = queries_tok.reshape(token_rows, QUERY_HEADS * HEAD_SIZE)
    key_token_rows = paired_token_rows[:, :, 0].reshape(token_rows, KEY_VALUE_HEADS * HEAD_SIZE)
    value_token_rows = paired_token_rows[:, :, 1].reshape(token_rows, KEY_VALUE_HEADS * HEAD_SIZE)
    query_grad = transposed_times(first_normed, queries_tok)
    key_grad = transposed_times(first_normed, key_token_rows)
    value_grad = transposed_times(first_normed, value_token_rows)
    grad_norm_one = (
        times_transposed(queries_tok, query_all)
        + times_transposed(key_token_rows, key_all)
        + times_transposed(value_token_rows, value_all)
    )
    attn_gain_grad = jnp.sum(grad_norm_one * unit_one, axis=0)
    query_grad, key_grad, value_grad, out_grad, attn_gain_grad = (
        lax.psum_scatter(
            query_grad.astype(jnp.bfloat16), "dp", scatter_dimension=0, tiled=True
        ).astype(jnp.float32),
        lax.psum_scatter(
            key_grad.astype(jnp.bfloat16), "dp", scatter_dimension=0, tiled=True
        ).astype(jnp.float32),
        lax.psum_scatter(
            value_grad.astype(jnp.bfloat16), "dp", scatter_dimension=0, tiled=True
        ).astype(jnp.float32),
        lax.psum_scatter(
            out_grad.astype(jnp.bfloat16), "dp", scatter_dimension=0, tiled=True
        ).astype(jnp.float32),
        lax.psum_scatter(
            attn_gain_grad.astype(jnp.bfloat16), "dp", scatter_dimension=0, tiled=True
        ).astype(jnp.float32),
    )
    query_grad, key_grad, value_grad, out_grad, attn_gain_grad = (
        lax.psum(query_grad.astype(jnp.bfloat16), "seq").astype(jnp.float32),
        lax.psum(key_grad.astype(jnp.bfloat16), "seq").astype(jnp.float32),
        lax.psum(value_grad.astype(jnp.bfloat16), "seq").astype(jnp.float32),
        lax.psum(out_grad.astype(jnp.bfloat16), "seq").astype(jnp.float32),
        lax.psum(attn_gain_grad.astype(jnp.bfloat16), "seq").astype(jnp.float32),
    )
    input_grad = grad_mid + norm_backward(grad_norm_one, unit_one, gain_one, inv_one)
    return (
        layer_output.reshape(sequence_count, local_length, width),
        input_grad.reshape(sequence_count, local_length, width),
        attn_gain_grad,
        query_grad,
        key_grad,
        value_grad,
        out_grad,
        ffn_gain_grad,
        gate_grad,
        up_grad,
        down_grad,
    )


def solution(mesh):
    return jax.shard_map(
        body,
        mesh=mesh,
        in_specs=(
            P("dp", "seq", None),
            P("dp"),
            P("dp", None),
            P("dp", None),
            P("dp", None),
            P("dp", None),
            P("dp"),
            P("dp", None),
            P("dp", None),
            P("dp", None),
            P("dp", "seq", None),
        ),
        out_specs=(
            P("dp", "seq", None),
            P("dp", "seq", None),
            P("dp"),
            P("dp", None),
            P("dp", None),
            P("dp", None),
            P("dp", None),
            P("dp"),
            P("dp", None),
            P("dp", None),
            P("dp", None),
        ),
        check_vma=False,
    )
```

profile of v0, /device:TPU:0, one launch (start us, length us, event | category | flops | bytes accessed | tf_op | source)
XLA Modules:
  0.0 1285.3 jit_solution(7736904151588342376)
XLA Ops:
  13.7 15.4 %all-reduce.7 = (bf16[1536]{0:T(1024)(128)(2,1)S(1)}, bf16[1536]{0:T(1024)(128)(2,1)S(1)}) all-reduce(bf16[1536]{0:T(1024)(128)(2,1)S(1)} %dynamic-update-slice, bf16[1536]{0:T(1024)(128)(2,1)S(1)} %dynamic-update-slice.1), channel_id=1, replica_groups=mesh['dp'=8,'seq'=4] {'dp'}, use_global_device_ids=true, to_apply=%add.2 | all-reduce | flops 3072 | bytes 12288
  32.2 9.7 all-gather.8.cloned.1.call-done
  41.9 4.3 copy.92
  50.5 22.3 %all-gather.10.cloned.1.call-done = bf16[1536,768]{1,0:T(8,128)(2,1)} async-done(((bf16[192,768]{1,0:T(8,128)(2,1)}), bf16[1536,768]{1,0:T(8,128)(2,1)}) %all-gather.10.cloned.1.call-update) | async-done | bytes 2359312 | tf_op jit(solution)/shard_map/all_gather | solution.py:93
  72.8 4.4 convolution_convert_fusion.9
  79.5 3.2 pad_maximum_fusion.2
  82.7 4.8 all-to-all-start
  87.5 26.2 %all-gather.12.cloned.1.call-done = bf16[1536,1536]{1,0:T(8,128)(2,1)} async-done(((bf16[192,1536]{1,0:T(8,128)(2,1)}), bf16[1536,1536]{1,0:T(8,128)(2,1)}) %all-gather.12.cloned.1.call-update) | async-done | bytes 4718608 | tf_op jit(solution)/shard_map/all_gather | solution.py:91
  113.6 6.6 copy.96
  120.3 5.1 fusion.26
  129.2 4.5 all-to-all-start.1
  141.6 29.7 %all-to-all-done.1 = bf16[2,256,2,768]{1,2,0,3:T(2,128)(2,1)} async-done(((bf16[2,256,2,768]{1,2,0,3:T(2,128)(2,1)}), bf16[2,256,2,768]{1,2,0,3:T(2,128)(2,1)}, u32[]{:S(2)}, u32[]{:S(2)}) %all-to-all-start.1) | async-done | bytes 1572896 | tf_op jit(solution)/shard_map/all_to_all | solution.py:138
  184.4 9.2 fusion.4
  193.7 9.3 exponential_reduce_fusion
  203.1 5.1 fusion.30
  208.2 8.1 fusion.31
  217.3 4.0 copy.105
  221.3 4.6 all-to-all-start.2
  225.9 47.6 %all-to-all-done.2 = bf16[2,1024,2,192]{3,2,0,1:T(2,128)(2,1)} async-done(((bf16[2,1024,2,192]{3,2,0,1:T(2,128)(2,1)}), bf16[2,1024,2,192]{3,2,0,1:T(2,128)(2,1)}, u32[]{:S(2)}, u32[]{:S(2)}) %all-to-all-start.2) | async-done | bytes 1572896 | tf_op jit(solution)/shard_map/all_to_all | solution.py:167
  273.5 9.8 copy.106
  284.9 5.3 multiply_reduce_fusion.4
  292.2 12.3 fusion.60
  304.5 11.8 fusion.61
  316.3 59.9 %all-gather.20.cloned.1.call-done = bf16[4096,1536]{1,0:T(8,128)(2,1)} async-done(((bf16[512,1536]{1,0:T(8,128)(2,1)}), bf16[4096,1536]{1,0:T(8,128)(2,1)}) %all-gather.20.cloned.1.call-update) | async-done | bytes 12582928 | tf_op jit(solution)/shard_map/all_gather | solution.py:100
  376.2 22.0 %multiply_convert_fusion = (bf16[512,4096]{1,0:T(8,128)(2,1)}, bf16[512,4096]{1,0:T(8,128)(2,1)}, bf16[512,4096]{1,0:T(8,128)(2,1)}) fusion(f32[512,4096]{1,0:T(8,128)} %fusion.60, f32[512,4096]{1,0:T(8,128)} %fusion.61, bf16[512,1536]{1,0:T(8,128)(2,1)S(1)} %bitcast.276, bf16[4096,1536]{1,0:T(8,128)(2,1)} %all-gather.20.cloned.1.call-done), kind=kOutput, calls=%fused_computation.20 | convolution fusion | flops 6473908224 | bytes 43515904 | tf_op jit(solution)/shard_map/dot_general | solution.py:43
  398.2 10.9 fusion.62
  409.2 12.0 multiply_reduce_fusion
  422.1 3.8 convolution_convert_fusion.7
  425.9 4.6 reshape.358
  430.5 6.2 copy.107
  436.7 4.6 all-to-all-start.3
  443.5 5.7 convolution_convert_fusion.3
  449.3 29.5 %all-to-all-done.3 = bf16[2,256,2,768]{1,2,0,3:T(2,128)(2,1)} async-done(((bf16[2,256,2,768]{1,2,0,3:T(2,128)(2,1)}), bf16[2,256,2,768]{1,2,0,3:T(2,128)(2,1)}, u32[]{:S(2)}, u32[]{:S(2)}) %all-to-all-start.3) | async-done | bytes 1572896 | tf_op jit(solution)/shard_map/all_to_all | solution.py:228
  483.5 3.1 multiply_reduce_fusion.6
  486.6 9.7 fusion.1
  496.4 5.2 fusion.7
  511.1 5.5 convolution_bitcast_fusion
  516.6 8.8 fusion.25
  525.4 5.9 copy.124
  531.3 6.3 pad_maximum_fusion.1
  537.6 50.2 %all_to_all.96 = bf16[2,1024,2,192]{3,2,0,1:T(2,128)(2,1)S(1)} all-to-all(bf16[2,1024,2,192]{3,2,0,1:T(2,128)(2,1)S(1)} %pad_maximum_fusion.1), channel_id=1, replica_groups=mesh['dp'=8,'seq'=4] {'seq'}, dimensions={1} | all-to-all | bytes 3145728 | tf_op jit(solution)/shard_map/all_to_all | solution.py:293
  587.8 4.6 copy.146
  595.4 4.5 convolution_convert_fusion.6
  603.1 5.2 multiply_bitcast_fusion
  610.6 4.5 convolution_convert_fusion.5
  619.5 4.7 copy.117
  624.3 50.8 %all_to_all.97 = bf16[2,1024,2,192]{3,2,0,1:T(2,128)(2,1)} all-to-all(bf16[2,1024,2,192]{3,2,0,1:T(2,128)(2,1)S(1)} %copy.117), channel_id=1, replica_groups=mesh['dp'=8,'seq'=4] {'seq'}, dimensions={1} | all-to-all | bytes 3145728 | tf_op jit(solution)/shard_map/all_to_all | solution.py:292
  675.0 10.0 copy.118
  686.5 4.4 convolution_convert_fusion.4
  692.3 11.9 convolution_convert_fusion.2
  704.3 12.0 convolution_convert_fusion.1
  717.7 12.1 convolution_convert_fusion
  730.0 14.9 %reduce-scatter.8.cloned.1.call-done = bf16[192,1536]{1,0:T(8,128)(2,1)} async-done(((bf16[1536,1536]{1,0:T(8,128)(2,1)}), bf16[192,1536]{1,0:T(8,128)(2,1)}) %reduce-scatter.8.cloned.1.call-update) | async-done | bytes 589840 | tf_op jit(solution)/shard_map/reduce_scatter | solution.py:308
  744.9 95.8 %reduce-scatter.16.cloned.1.call-done = bf16[192,4096]{1,0:T(8,128)(2,1)} async-done(((bf16[1536,4096]{1,0:T(8,128)(2,1)}), bf16[192,4096]{1,0:T(8,128)(2,1)}) %reduce-scatter.16.cloned.1.call-update) | async-done | bytes 1572880 | tf_op jit(solution)/shard_map/reduce_scatter | solution.py:199
  840.7 95.9 %reduce-scatter.18.cloned.1.call-done = bf16[192,4096]{1,0:T(8,128)(2,1)} async-done(((bf16[1536,4096]{1,0:T(8,128)(2,1)}), bf16[192,4096]{1,0:T(8,128)(2,1)}) %reduce-scatter.18.cloned.1.call-update) | async-done | bytes 1572880 | tf_op jit(solution)/shard_map/reduce_scatter | solution.py:202
  936.6 95.8 %reduce-scatter.20.cloned.1.call-done = bf16[512,1536]{1,0:T(8,128)(2,1)} async-done(((bf16[4096,1536]{1,0:T(8,128)(2,1)}), bf16[512,1536]{1,0:T(8,128)(2,1)}) %reduce-scatter.20.cloned.1.call-update) | async-done | bytes 1572880 | tf_op jit(solution)/shard_map/reduce_scatter | solution.py:205
  1034.3 11.8 fusion.18
  1046.1 4.8 fusion.63
  1053.4 3.4 multiply_reduce_fusion.1
  1056.8 13.7 %all-reduce.6 = (bf16[1536]{0:T(1024)(128)(2,1)S(1)}, bf16[1536]{0:T(1024)(128)(2,1)S(1)}) all-reduce(bf16[1536]{0:T(1024)(128)(2,1)S(1)} %get-tuple-element.13, bf16[1536]{0:T(1024)(128)(2,1)S(1)} %copy-done.56), channel_id=2, replica_groups=mesh['dp'=8,'seq'=4] {'dp'}, use_global_device_ids=true, to_apply=%region_11.12.clone | all-reduce | flops 3072 | bytes 12288
  1070.7 12.4 all-reduce.8
  1084.2 5.4 multiply_add_fusion
  1089.7 177.0 %all-reduce.12.cloned.1.call-done = (bf16[192,1536]{1,0:T(8,128)(2,1)}, bf16[192,768]{1,0:T(8,128)(2,1)}, bf16[192,768]{1,0:T(8,128)(2,1)}, bf16[192,1536]{1,0:T...) async-done(((bf16[192,1536]{1,0:T(8,128)(2,1)}, bf16[192,768]{1,0:T(8,128)(2,1)}, bf16[192,768]{1,0:T(8,128)(2,1)}, ...) | async-done | bytes 6488080 | tf_op jit(solution)/shard_map/psum | solution.py:325
  1266.7 3.5 convert_element_type.266
  (256 shorter events, 91.6 us)
Async XLA Ops:
  7.2 34.7 %all-gather.8.cloned.1.call-start = ((), (), s32[]{:S(2)}) async-start(), calls=%async_computation.13 | async-start | bytes 2654208 | tf_op jit(solution)/shard_map/all_gather | solution.py:92
  7.9 4.0 copy-start.59
  7.9 5.3 copy-start.61
  7.9 5.5 copy-start.62
  7.9 21.3 %copy-start.1 = (bf16[2,256,1536]{2,1,0:T(8,128)(2,1)S(1)}, bf16[2,256,1536]{2,1,0:T(8,128)(2,1)}, u32[]{:S(2)}) copy-start(bf16[2,256,1536]{2,1,0:T(8,128)(2,1)} %param.11) | copy-start | bytes 4718596
  8.0 64.8 %all-gather.10.cloned.1.call-start = ((), (), s32[]{:S(2)}) async-start(), calls=%async_computation.14 | async-start | bytes 2654208 | tf_op jit(solution)/shard_map/all_gather | solution.py:93
  8.7 104.9 %all-gather.12.cloned.1.call-start = ((), (), s32[]{:S(2)}) async-start(), calls=%async_computation.15 | async-start | bytes 5308416 | tf_op jit(solution)/shard_map/all_gather | solution.py:91
  9.4 275.4 %all-gather.14.cloned.1.call-start = ((), (), s32[]{:S(2)}) async-start(), calls=%async_computation.16 | async-start | bytes 5308416 | tf_op jit(solution)/shard_map/all_gather | solution.py:94
  10.0 282.1 %all-gather.16.cloned.1.call-start = ((), (), s32[]{:S(2)}) async-start(), calls=%async_computation.17 | async-start | bytes 14155776 | tf_op jit(solution)/shard_map/all_gather | solution.py:98
  10.6 293.9 %all-gather.18.cloned.1.call-start = ((), (), s32[]{:S(2)}) async-start(), calls=%async_computation.18 | async-start | bytes 14155776 | tf_op jit(solution)/shard_map/all_gather | solution.py:99
  11.2 365.0 %all-gather.20.cloned.1.call-start = ((), (), s32[]{:S(2)}) async-start(), calls=%async_computation.19 | async-start | bytes 14155776 | tf_op jit(solution)/shard_map/all_gather | solution.py:100
  29.2 3.0 copy-start.47
  30.5 15.6 %copy-start.30 = (bf16[2,256,1536]{2,1,0:T(8,128)(2,1)}, bf16[2,256,1536]{2,1,0:T(8,128)(2,1)S(1)}, u32[]{:S(2)}) copy-start(bf16[2,256,1536]{2,1,0:T(8,128)(2,1)S(1)} %multiply_convert_fusion.5) | copy-start | bytes 4718596
  82.7 46.6 %all-to-all-start = ((bf16[2,256,2,768]{1,0,2,3:T(2,128)(2,1)}), bf16[2,256,2,768]{1,0,2,3:T(2,128)(2,1)S(1)}, u32[]{:S(2)}, u32[]{:S(2)}) async-start(bf16[2,256,2,768]{1,0,2,3:T(2,128)(2,1)} %pad_maximum_fusion.2), calls=%async_computation | async-start | bytes 3145728 | tf_op jit(solution)/shard_map/all_to_all | solution.py:139
  129.2 42.1 %all-to-all-start.1 = ((bf16[2,256,2,768]{1,2,0,3:T(2,128)(2,1)}), bf16[2,256,2,768]{1,2,0,3:T(2,128)(2,1)}, u32[]{:S(2)}, u32[]{:S(2)}) async-start(bf16[2,256,2,768]{1,2,0,3:T(2,128)(2,1)} %copy.97), calls=%async_computation.1 | async-start | bytes 3145728 | tf_op jit(solution)/shard_map/all_to_all | solution.py:138
  133.8 69.2 %copy-start.39 = (pred[512,512]{0,1:T(8,128)(4,1)}, pred[512,512]{0,1:T(8,128)(4,1)S(1)}, u32[]{:S(2)}) copy-start(pred[512,512]{0,1:T(8,128)(4,1)S(1)} %iota_compare_fusion.1) | copy-start | bytes 786436
  178.3 6.1 copy-start.17
  181.1 3.3 copy-start.9
  181.1 3.4 copy-start.26
  184.4 18.6 %copy-start.51 = (f32[2,2,2,512]{3,1,2,0:T(2,128)}, f32[2,2,2,512]{3,1,2,0:T(2,128)S(1)}, u32[]{:S(2)}) copy-start(f32[2,2,2,512]{3,1,2,0:T(2,128)S(1)} %log_add_fusion.1) | copy-start | bytes 49156
  193.6 9.4 copy-start.42
  203.0 5.2 copy-start.54
  208.2 8.2 copy-start.19
  221.3 52.3 %all-to-all-start.2 = ((bf16[2,1024,2,192]{3,2,0,1:T(2,128)(2,1)}), bf16[2,1024,2,192]{3,2,0,1:T(2,128)(2,1)}, u32[]{:S(2)}, u32[]{:S(2)}) async-start(bf16[2,1024,2,192]{3,2,0,1:T(2,128)(2,1)} %copy.105), calls=%async_computation.2 | async-start | bytes 4194304 | tf_op jit(solution)/shard_map/all_to_all | solution.py:167
  292.1 12.4 copy-start.32
  304.5 71.7 %copy-start.36 = (bf16[2,256,1536]{2,1,0:T(8,128)(2,1)S(1)}, bf16[2,256,1536]{2,1,0:T(8,128)(2,1)}, u32[]{:S(2)}) copy-start(bf16[2,256,1536]{2,1,0:T(8,128)(2,1)} %param.21) | copy-start | bytes 4718596
  398.2 11.0 copy-start.6
  398.2 23.9 %slice-start.2 = ((s8[4718592]{0:T(1024)(128)(4,1)}), s8[4194304]{0:T(1024)(128)(4,1)S(1)}, s32[]{:S(2)}) async-start(s8[4718592]{0:T(1024)(128)(4,1)} %bitcast.291), calls=%async_computation.30 | async-start | bytes 8388608
  409.2 12.0 copy-start.37
  409.2 12.9 %slice-start.3 = ((s8[4718592]{0:T(1024)(128)(4,1)}), s8[524288]{0:T(1024)(128)(4,1)S(1)}, s32[]{:S(2)}) async-start(s8[4718592]{0:T(1024)(128)(4,1)} %bitcast.291), calls=%async_computation.31 | async-start | bytes 1048576
  422.1 21.4 %copy-start.4 = (f32[512,1536]{1,0:T(8,128)}, f32[512,1536]{1,0:T(8,128)S(1)}, u32[]{:S(2)}) copy-start(f32[512,1536]{1,0:T(8,128)S(1)} %multiply_add_fusion.1) | copy-start | bytes 9437188
  430.5 10.8 copy-start.58
  436.7 42.1 %all-to-all-start.3 = ((bf16[2,256,2,768]{1,2,0,3:T(2,128)(2,1)}), bf16[2,256,2,768]{1,2,0,3:T(2,128)(2,1)}, u32[]{:S(2)}, u32[]{:S(2)}) async-start(bf16[2,256,2,768]{1,2,0,3:T(2,128)(2,1)} %copy.107), calls=%async_computation.3 | async-start | bytes 3145728 | tf_op jit(solution)/shard_map/all_to_all | solution.py:228
  441.3 288.6 %reduce-scatter.14.cloned.1.call-start = ((), (), s32[]{:S(2)}) async-start(), calls=%async_computation.23 | async-start | bytes 5308416 | tf_op jit(solution)/shard_map/reduce_scatter | solution.py:317
  449.2 280.8 %reduce-scatter.10.cloned.1.call-start = ((), (), s32[]{:S(2)}) async-start(), calls=%async_computation.21 | async-start | bytes 2654208 | tf_op jit(solution)/shard_map/reduce_scatter | solution.py:311
  483.2 13.1 %slice-start = ((s8[8388608]{0:T(1024)(128)(4,1)}), s8[4194304]{0:T(1024)(128)(4,1)S(1)}, s32[]{:S(2)}) async-start(s8[8388608]{0:T(1024)(128)(4,1)} %bitcast.242), calls=%async_computation.28 | async-start | bytes 8388608
  483.4 3.2 copy-start.21
  483.4 3.2 copy-start.23
  486.6 9.8 slice-start.1
  486.6 9.8 copy-start.40
  486.6 9.8 copy-start.52
  496.4 8.7 copy-start
  496.4 7.2 copy-start.25
  511.1 5.5 copy-start.22
  511.1 5.5 copy-start.27
  511.1 5.5 copy-start.55
  595.4 4.6 copy-start.15
  595.4 4.6 copy-start.11
  600.0 130.0 %reduce-scatter.12.cloned.1.call-start = ((), (), s32[]{:S(2)}) async-start(), calls=%async_computation.22 | async-start | bytes 2654208 | tf_op jit(solution)/shard_map/reduce_scatter | solution.py:314
  600.0 3.1 copy-start.12
  615.1 129.7 %reduce-scatter.8.cloned.1.call-start = ((), (), s32[]{:S(2)}) async-start(), calls=%async_computation.20 | async-start | bytes 5308416 | tf_op jit(solution)/shard_map/reduce_scatter | solution.py:308
  675.0 11.5 copy-start.31
  691.0 149.7 %reduce-scatter.16.cloned.1.call-start = ((), (), s32[]{:S(2)}) async-start(), calls=%async_computation.24 | async-start | bytes 14155776 | tf_op jit(solution)/shard_map/reduce_scatter | solution.py:199
  704.3 232.3 %reduce-scatter.18.cloned.1.call-start = ((), (), s32[]{:S(2)}) async-start(), calls=%async_computation.25 | async-start | bytes 14155776 | tf_op jit(solution)/shard_map/reduce_scatter | solution.py:202
  716.3 316.0 %reduce-scatter.20.cloned.1.call-start = ((), (), s32[]{:S(2)}) async-start(), calls=%async_computation.26 | async-start | bytes 14155776 | tf_op jit(solution)/shard_map/reduce_scatter | solution.py:205
  729.9 536.8 %all-reduce.12.cloned.1.call-start = ((), (), s32[]{:S(2)}) async-start(), calls=%async_computation.27 | async-start | bytes 12976128 | tf_op jit(solution)/shard_map/psum | solution.py:325
  1034.3 11.9 copy-start.29
  1046.1 4.8 copy-start.8
  1046.1 4.8 copy-start.16
  1053.3 3.4 copy-start.56
  1266.7 3.6 copy-start.35
  1272.2 3.2 copy-start.43
  1272.2 4.4 copy-start.46
  1274.3 3.2 copy-start.45
  (22 other events, 38.1 us)
Sparse Core Ops, SparseCore 0:
  9.9 31.9 all-gather.7
  43.8 29.0 all-gather.9
  74.7 38.9 all-gather.11
  115.4 38.9 all-gather.13
  156.1 72.1 all-gather.15
  230.0 72.1 all-gather.17
  304.0 72.1 all-gather.19
  449.3 54.3 reduce-scatter.13
  600.1 40.6 reduce-scatter.9
  644.6 42.4 reduce-scatter.11
  691.1 53.7 reduce-scatter.7
  748.2 92.3 reduce-scatter.15
  844.2 92.3 reduce-scatter.17
  939.9 92.3 reduce-scatter.19
  1035.2 231.4 all-reduce.11
where the time goes:
time: 1290 us
  waiting for transfers between devices  709 us (55%)
  matrix products  233 us (18%)
  blocking collectives  143 us (11%)
  local copies, waits for them, and re-layouts  110 us (9%)
  other arithmetic  54.6 us (4%)
  starting transfers between devices  19.1 us (1%)
  between operations  17 us (1%)
    psum x1, waiting for transfers between devices, body(): lax.psum(query_grad.astype(jnp.bfloat16), 'seq').astype(jnp.float32)  177 us
    reduce_scatter x1, waiting for transfers between devices, body(): lax.psum_scatter(up_grad.astype(jnp.bfloat16), 'dp', scatter_dimension=0,...  95.9 us
    reduce_scatter x1, waiting for transfers between devices, body(): lax.psum_scatter(down_grad.astype(jnp.bfloat16), 'dp', scatter_dimension=...  95.8 us
    reduce_scatter x1, waiting for transfers between devices, body(): lax.psum_scatter(gate_grad.astype(jnp.bfloat16), 'dp', scatter_dimension=...  95.8 us
    all_gather x1, waiting for transfers between devices, body(): lax.all_gather(down_weight, 'dp', axis=0, tiled=True)  59.9 us
    dot_general x7, matrix products, times_transposed(): lax.dot_general(left, right, (((1,), (1,)), ((), ())), preferred_element_...  58.3 us
    dot_general x7, matrix products, transposed_times(): lax.dot_general(left, right, (((0,), (0,)), ((), ())), preferred_element_...  55.2 us
    all_to_all x1, blocking collectives, body(): lax.all_to_all(queries_back, 'seq', split_axis=1, concat_axis=3, tiled=True)  50.8 us
  transfers between devices with their start and end apart: 19, of which 12 were waited for; matrix products, arithmetic and copies ran while one was open for 24% of the time, Pallas kernels for 0%

commit v1 on v0

--- a/solution.py
+++ b/solution.py
@@ -1,6 +1,8 @@
 import jax
 import jax.numpy as jnp
 from jax import lax
+from jax.experimental import pallas as pl
+from jax.experimental.pallas import tpu as pltpu
 from jax.sharding import PartitionSpec as P
 
 QUERY_HEADS = 16
@@ -344,9 +346,854 @@
     )
 
 
+SAME_CORE = [[0, 2, 4, 6], [1, 3, 5, 7]]
+VMEM_BYTES = 48 * 1024 * 1024
+
+
+def flip(field, bit):
+    count = lax.axis_size("dp")
+    return lax.ppermute(field, "dp", [(i, i ^ bit) for i in range(count)])
+
+
+def cross(field, bit):
+    return lax.ppermute(field, "seq", [(i, i ^ bit) for i in range(4)])
+
+
+def column_swap(field, turn, back):
+    pairs = []
+    for dp in range(8):
+        for place in range(4):
+            chip, core, high, low = dp // 2, dp % 2, place // 2, place % 2
+            target = (2 * chip + (high ^ 1)) * 4 + 2 * core + (low ^ turn)
+            pairs.append((target, dp * 4 + place) if back else (dp * 4 + place, target))
+    return lax.ppermute(field, ("dp", "seq"), pairs)
+
+
+def pick_order(swapped, first, second, axis=0):
+    return jnp.where(
+        swapped,
+        jnp.concatenate([second, first], axis=axis),
+        jnp.concatenate([first, second], axis=axis),
+    )
+
+
+def sequence_parts(field, low):
+    return [
+        column_swap(lax.dynamic_index_in_dim(field, low ^ turn, 0, keepdims=False), turn, False)
+        for turn in range(2)
+    ]
+
+
+def slice_parts(half, low):
+    rows = half.shape[0] // 2
+    return [
+        column_swap(lax.dynamic_slice_in_dim(half, (low ^ turn) * rows, rows, 0), turn, True)
+        for turn in range(2)
+    ]
+
+
+def join_slices(parts, low):
+    return jnp.where(low == 1, jnp.stack(parts[::-1]), jnp.stack(parts))
+
+
+def both_cores(half, core):
+    return pick_order(core == 0, half, flip(half, 1))
+
+
+def relative_columns(field, chip):
+    width = field.shape[-1] // 4
+    return jnp.concatenate(
+        [lax.dynamic_slice_in_dim(field, (chip ^ r) * width, width, field.ndim - 1) for r in range(4)],
+        axis=-1,
+    )
+
+
+def gather_chips(block):
+    half = block.shape[0] // 2
+    from_x = flip(block, 2)
+    from_y = flip(block, 4)
+    corner_x = flip(from_y[:half], 2)
+    corner_y = flip(from_x[half:], 4)
+    return block, from_x, from_y, corner_x, corner_y
+
+
+def add_half(*terms):
+    total = terms[0].astype(jnp.float32)
+    for term in terms[1:]:
+        total = total + term.astype(jnp.float32)
+    return total.astype(jnp.bfloat16)
+
+
+def scatter_first(field):
+    half = field.shape[0] // 8
+    corner = field[6 * half :]
+    return flip(corner[:half], 2), flip(corner[half:], 4)
+
+
+def scatter_second(field, got_x, got_y):
+    rows = field.shape[0] // 4
+    half = rows // 2
+    over_x, over_y = field[rows : 2 * rows], field[2 * rows : 3 * rows]
+    send_x = jnp.concatenate([over_x[:half], add_half(over_x[half:], got_y)], axis=0)
+    send_y = jnp.concatenate([add_half(over_y[:half], got_x), over_y[half:]], axis=0)
+    return flip(send_x, 2), flip(send_y, 4)
+
+
+def halve(field, bit_value, bit):
+    size = field.shape[0] // 2
+    own = lax.dynamic_slice_in_dim(field, bit_value * size, size, 0)
+    other = lax.dynamic_slice_in_dim(field, (1 - bit_value) * size, size, 0)
+    return add_half(own, cross(other, bit))
+
+
+def join(field, bit_value, bit):
+    return pick_order(bit_value == 1, field, cross(field, bit))
+
+
+def prepare_kernel(core_ref, gate_mine, gate_theirs, up_mine, up_theirs, mine_ref, theirs_ref):
+    for gate, up, out in ((gate_mine, up_mine, mine_ref), (gate_theirs, up_theirs, theirs_ref)):
+        part = gate.shape[1] // 2
+        for group in range(2):
+            out[group, :, :part] = gate[:, group * part : (group + 1) * part]
+            out[group, :, part:] = up[:, group * part : (group + 1) * part]
+
+
+def prepare_ffn(gate_weight, up_weight, core):
+    rows, columns = gate_weight.shape
+    piece = columns // 8
+    mine = pl.BlockSpec((rows, piece), lambda j, c: (0, 2 * j + c[0]))
+    theirs = pl.BlockSpec((rows, piece), lambda j, c: (0, 2 * j + 1 - c[0]))
+    out = pl.BlockSpec((2, rows, piece), lambda j, c: (0, 0, j))
+    shape = jax.ShapeDtypeStruct((2, rows, columns // 2), jnp.bfloat16)
+    return pl.pallas_call(
+        prepare_kernel,
+        out_shape=(shape, shape),
+        grid_spec=pltpu.PrefetchScalarGridSpec(
+            num_scalar_prefetch=1,
+            grid=(4,),
+            in_specs=[mine, theirs, mine, theirs],
+            out_specs=(out, out),
+        ),
+        name="prepare_ffn",
+    )(core.reshape(1), gate_weight, gate_weight, up_weight, up_weight)
+
+
+def merge_kernel(core_ref, own_0, other_0, own_1, other_1, gate_ref, up_ref):
+    part = own_0.shape[1] // 2
+    mine = core_ref[0] == pl.program_id(1)
+    first = jnp.where(mine, own_0[...].astype(jnp.float32), other_0[...].astype(jnp.float32))
+    second = jnp.where(mine, own_1[...].astype(jnp.float32), other_1[...].astype(jnp.float32))
+    gate_ref[:, :part] = first[:, :part]
+    gate_ref[:, part:] = second[:, :part]
+    up_ref[:, :part] = first[:, part:]
+    up_ref[:, part:] = second[:, part:]
+
+
+def merge_ffn(own_0, other_0, own_1, other_1, core):
+    rows, columns = own_0.shape
+    piece = columns // 4
+    part = pl.BlockSpec((rows, piece), lambda j, i, c: (0, j))
+    out = pl.BlockSpec((rows, piece), lambda j, i, c: (0, 2 * j + i))
+    shape = jax.ShapeDtypeStruct((rows, columns * 2), jnp.float32)
+    return pl.pallas_call(
+        merge_kernel,
+        out_shape=(shape, shape),
+        grid_spec=pltpu.PrefetchScalarGridSpec(
+            num_scalar_prefetch=1,
+            grid=(4, 2),
+            in_specs=[part] * 4,
+            out_specs=(out, out),
+        ),
+        name="merge_ffn",
+    )(core.reshape(1), own_0, other_0, own_1, other_1)
+
+
+def hint(flops, bytes_accessed, transcendentals=0):
+    return pl.CostEstimate(
+        flops=flops // 8, transcendentals=transcendentals // 8, bytes_accessed=bytes_accessed // 8
+    )
+
+
+def stacked(pieces, rows):
+    own, from_x, from_y, corner_x, corner_y = pieces
+    rest = rows - corner_x.shape[0]
+    return jnp.concatenate(
+        [own[:rows, :], from_x[:rows, :], from_y[:rows, :], corner_x[...], corner_y[:rest, :]],
+        axis=0,
+    )
+
+
+def hidden_kernel(rows, normed, upstream, *refs):
+    down, hidden, grads = refs[5:]
+    part = grads.shape[1] // 2
+    weight = stacked(refs[:5], rows)
+    tile = 256
+    for start in range(0, normed.shape[0], tile):
+        lines = pl.ds(start, tile)
+        total = jnp.dot(normed[lines, :], weight, preferred_element_type=jnp.float32)
+        grad_hidden = lax.dot_general(
+            upstream[lines, :], down[...], (((1,), (1,)), ((), ())), preferred_element_type=jnp.float32
+        )
+        gate, upward = total[:, :part], total[:, part:]
+        sigma = jax.nn.sigmoid(gate)
+        silu_gate = gate * sigma
+        hidden[lines, :] = (silu_gate * upward).astype(jnp.bfloat16)
+        grads[lines, :part] = (
+            grad_hidden * upward * sigma * (1.0 + gate * (1.0 - sigma))
+        ).astype(jnp.bfloat16)
+        grads[lines, part:] = (grad_hidden * silu_gate).astype(jnp.bfloat16)
+
+
+def hidden_stage(normed, upstream, pieces, down):
+    length, width = normed.shape
+    columns = pieces[0].shape[1]
+    piece = columns // 4
+    whole = pl.BlockSpec((length, width), lambda j: (0, 0), pipeline_mode=pl.Buffered(1))
+    return pl.pallas_call(
+        lambda *refs: hidden_kernel(width // 4, *refs),
+        out_shape=(
+            jax.ShapeDtypeStruct((length, columns // 2), jnp.bfloat16),
+            jax.ShapeDtypeStruct((length, columns), jnp.bfloat16),
+        ),
+        grid=(4,),
+        in_specs=[whole, whole]
+        + [pl.BlockSpec((p.shape[0], piece), lambda j: (0, j)) for p in pieces]
+        + [pl.BlockSpec((piece // 2, width), lambda j: (j, 0))],
+        out_specs=(
+            pl.BlockSpec((length, piece // 2), lambda j: (0, j)),
+            pl.BlockSpec((length, piece), lambda j: (0, j)),
+        ),
+        compiler_params=pltpu.CompilerParams(vmem_limit_bytes=VMEM_BYTES),
+        cost_estimate=hint(
+            3 * length * width * columns,
+            4 * length * width + 3 * width * columns + 3 * length * columns,
+            length * columns // 2,
+        ),
+        name="hidden_stage",
+    )(normed, upstream, *pieces, down)
+
+
+NEGATIVE = -1e30
+LANES = 128
+
+
+def turned(field, cos, sin_low, sin_high, sign):
+    half = HEAD_SIZE // 2
+    spun = pltpu.roll(field, LANES - half, 1) * sin_low + pltpu.roll(field, half, 1) * sin_high
+    return field * cos + sign * spun
+
+
+def project_kernel(rows, heads, normed, cos, sin_low, sin_high, *refs):
+    out, weight = refs[5:]
+    own, from_x, from_y, corner_x, corner_y = refs[:5]
+    rest = rows - corner_x.shape[0]
+
+    @pl.when(pl.program_id(0) == 0)
+    def _():
+        start = 0
+        for piece, count in (
+            (own, rows), (from_x, rows), (from_y, rows), (corner_x, rows - rest), (corner_y, rest)
+        ):
+            lines = pl.ds(start, count)
+            for head in range(heads):
+                weight[lines, pl.ds(head * LANES, HEAD_SIZE)] = piece[
+                    :count, pl.ds(head * HEAD_SIZE, HEAD_SIZE)
+                ]
+                weight[lines, pl.ds(head * LANES + HEAD_SIZE, LANES - HEAD_SIZE)] = jnp.zeros(
+                    (count, LANES - HEAD_SIZE), jnp.bfloat16
+                )
+            start += count
+
+    part = jnp.dot(normed[...], weight[...], preferred_element_type=jnp.float32)
+    for head in range(heads):
+        columns = slice(head * LANES, (head + 1) * LANES)
+        field = part[:, columns]
+        if head < heads * 3 // 4:
+            field = turned(field, cos[...], sin_low[...], sin_high[...], 1.0)
+        out[:, columns] = field.astype(jnp.bfloat16)
+
+
+def project_stage(normed, pieces, tables):
+    length, width = normed.shape
+    columns = pieces[0].shape[1]
+    heads = columns // HEAD_SIZE
+    tile = 256
+    table = pl.BlockSpec((tile, LANES), lambda i: (i, 0))
+    return pl.pallas_call(
+        lambda *refs: project_kernel(width // 4, heads, *refs),
+        out_shape=(
+            jax.ShapeDtypeStruct((length, heads * LANES), jnp.bfloat16),
+            jax.ShapeDtypeStruct((width, heads * LANES), jnp.bfloat16),
+        ),
+        grid=(length // tile,),
+        in_specs=[pl.BlockSpec((tile, width), lambda i: (i, 0)), table, table, table]
+        + [
+            pl.BlockSpec(p.shape, lambda i: (0, 0), pipeline_mode=pl.Buffered(1)) for p in pieces
+        ],
+        out_specs=(
+            pl.BlockSpec((tile, heads * LANES), lambda i: (i, 0)),
+            pl.BlockSpec((width, heads * LANES), lambda i: (0, 0), pipeline_mode=pl.Buffered(1)),
+        ),
+        compiler_params=pltpu.CompilerParams(vmem_limit_bytes=VMEM_BYTES),
+        cost_estimate=hint(
+            2 * length * width * heads * LANES,
+            2 * length * width + 4 * width * columns + 2 * length * columns,
+        ),
+        name="project_stage",
+    )(normed, *tables, *pieces)
+
+
+def block_softmax(query, key, tile, index):
+    scale = HEAD_SIZE ** (-0.5)
+    lines = pl.ds(index * tile, tile)
+    before = index * tile
+
+    def scores(which):
+        return scale * lax.dot_general(
+            query[lines, :], key[which, :], (((1,), (1,)), ((), ())),
+            preferred_element_type=jnp.float32,
+        )
+
+    last = scores(lines)
+    seen = lax.broadcasted_iota(jnp.int32, (tile, tile), 0) >= lax.broadcasted_iota(
+        jnp.int32, (tile, tile), 1
+    )
+    last = jnp.where(seen, last, NEGATIVE)
+    peak = jnp.max(last, axis=1, keepdims=True)
+    if before:
+        earlier = scores(pl.ds(0, before))
+        peak = jnp.maximum(peak, jnp.max(earlier, axis=1, keepdims=True))
+    last = jnp.exp(last - peak)
+    total = jnp.sum(last, axis=1, keepdims=True)
+    if before:
+        earlier = jnp.exp(earlier - peak)
+        total = total + jnp.sum(earlier, axis=1, keepdims=True)
+    inverse = 1.0 / total
+    parts = [(lines, last * inverse)]
+    if before:
+        parts.append((pl.ds(0, before), earlier * inverse))
+    return lines, parts
+
+
+def attention_kernel(tile, query, key, value, out):
+    for index in range(query.shape[0] // tile):
+        lines, parts = block_softmax(query, key, tile, index)
+        total = 0.0
+        for which, probs in parts:
+            total = total + jnp.dot(
+                probs.astype(jnp.bfloat16), value[which, :], preferred_element_type=jnp.float32
+            )
+        out[lines, :] = total.astype(jnp.bfloat16)
+
+
+def attention_stage(fields, heads, kv_heads):
+    length = fields.shape[0]
+    tile = min(256, length)
+    spec = lambda start, count: pl.BlockSpec((length, LANES), lambda h: (0, start + h % count))
+    return pl.pallas_call(
+        lambda *refs: attention_kernel(tile, *refs),
+        out_shape=jax.ShapeDtypeStruct((length, heads * LANES), jnp.bfloat16),
+        grid=(heads,),
+        in_specs=[spec(0, heads), spec(heads, kv_heads), spec(heads + kv_heads, kv_heads)],
+        out_specs=spec(0, heads),
+        compiler_params=pltpu.CompilerParams(vmem_limit_bytes=VMEM_BYTES),
+        cost_estimate=hint(
+            2 * heads * length * length * LANES,
+            6 * heads * length * LANES,
+            heads * length * length // 2,
+        ),
+        name="attention_stage",
+    )(fields, fields, fields)
+
+
+def attention_back_kernel(tile, *refs):
+    query_0, query_1, key, value, out_0, out_1, grad_0, grad_1 = refs[:8]
+    cos, sin_low, sin_high, back_0, back_1, key_back, value_back, key_sum, value_sum = refs[8:]
+    scale = HEAD_SIZE ** (-0.5)
+    key_sum[...] = jnp.zeros_like(key_sum)
+    value_sum[...] = jnp.zeros_like(value_sum)
+    for query, out, grad, back in (
+        (query_0, out_0, grad_0, back_0),
+        (query_1, out_1, grad_1, back_1),
+    ):
+        for index in range(query.shape[0] // tile):
+            lines, parts = block_softmax(query, key, tile, index)
+            upstream = grad[lines, :]
+            delta = jnp.sum(
+                upstream.astype(jnp.float32) * out[lines, :].astype(jnp.float32),
+                axis=1,
+                keepdims=True,
+            )
+            total = 0.0
+            for which, probs in parts:
+                grad_probs = lax.dot_general(
+                    upstream, value[which, :], (((1,), (1,)), ((), ())),
+                    preferred_element_type=jnp.float32,
+                )
+                grad_scores = (probs * (grad_probs - delta)).astype(jnp.bfloat16)
+                total = total + jnp.dot(
+                    grad_scores, key[which, :], preferred_element_type=jnp.float32
+                )
+                key_sum[which, :] += lax.dot_general(
+                    grad_scores, query[lines, :], (((0,), (0,)), ((), ())),
+                    preferred_element_type=jnp.float32,
+                )
+                value_sum[which, :] += lax.dot_general(
+                    probs.astype(jnp.bfloat16), upstream, (((0,), (0,)), ((), ())),
+                    preferred_element_type=jnp.float32,
+                )
+            back[lines, :] = turned(
+                total * scale, cos[lines, :], sin_low[lines, :], sin_high[lines, :], -1.0
+            ).astype(jnp.bfloat16)
+    key_back[...] = turned(
+        key_sum[...] * scale, cos[...], sin_low[...], sin_high[...], -1.0
+    ).astype(jnp.bfloat16)
+    value_back[...] = value_sum[...].astype(jnp.bfloat16)
+
+
+def attention_back_stage(fields, attended, grads, tables, kv_heads):
+    length = fields.shape[0]
+    tile = min(256, length)
+    spec = lambda start: pl.BlockSpec((length, LANES), lambda h: (0, start + h))
+    table = pl.BlockSpec((length, LANES), lambda h: (0, 0))
+    shape = jax.ShapeDtypeStruct((length, kv_heads * LANES), jnp.bfloat16)
+    first, second = spec(0), spec(kv_heads)
+    return pl.pallas_call(
+        lambda *refs: attention_back_kernel(tile, *refs),
+        out_shape=(shape,) * 4,
+        grid=(kv_heads,),
+        in_specs=[first, second, spec(2 * kv_heads), spec(3 * kv_heads)]
+        + [first, second] * 2
+        + [table] * 3,
+        out_specs=(first,) * 4,
+        scratch_shapes=[pltpu.VMEM((length, LANES), jnp.float32)] * 2,
+        compiler_params=pltpu.CompilerParams(vmem_limit_bytes=VMEM_BYTES),
+        cost_estimate=hint(
+            10 * kv_heads * length * length * LANES,
+            30 * kv_heads * length * LANES,
+            kv_heads * length * length,
+        ),
+        name="attention_back_stage",
+    )(fields, fields, fields, fields, attended, attended, grads, grads, *tables)
+
+
+def inputs_back_kernel(rows, chip_ref, *refs):
+    weight, out = refs[-2:]
+    columns = refs[0].shape[1]
+    part = 0.0
+    for j, grad in enumerate(refs[:-2]):
+        part = part + lax.dot_general(
+            grad[...], weight[:, j * columns : (j + 1) * columns], (((1,), (1,)), ((), ())),
+            preferred_element_type=jnp.float32,
+        )
+    for r in range(4):
+        where = pl.ds(pl.multiple_of((chip_ref[0] ^ r) * rows, 128), rows)
+        out[:, where] = part[:, r * rows : (r + 1) * rows]
+
+
+def inputs_back_stage(backs, weight, chip):
+    length, columns = backs[0].shape
+    width = weight.shape[0]
+    tile = 256
+    return pl.pallas_call(
+        lambda *refs: inputs_back_kernel(width // 4, *refs),
+        out_shape=jax.ShapeDtypeStruct((length, width), jnp.float32),
+        grid_spec=pltpu.PrefetchScalarGridSpec(
+            num_scalar_prefetch=1,
+            grid=(length // tile,),
+            in_specs=[pl.BlockSpec((tile, columns), lambda i, c: (i, 0))] * len(backs)
+            + [pl.BlockSpec(weight.shape, lambda i, c: (0, 0), pipeline_mode=pl.Buffered(1))],
+            out_specs=pl.BlockSpec((tile, width), lambda i, c: (i, 0)),
+        ),
+        compiler_params=pltpu.CompilerParams(vmem_limit_bytes=VMEM_BYTES),
+        cost_estimate=hint(
+            2 * length * width * weight.shape[1], 2 * width * weight.shape[1] + 8 * length * width
+        ),
+        name="inputs_back_stage",
+    )(chip.reshape(1), *backs, weight)
+
+
+def weight_kernel(normed, *refs):
+    gains, out = refs[-2:]
+    rows = normed.shape[1]
+    heads = refs[0].shape[1] // LANES
+    for j, back in enumerate(refs[:-2]):
+        part = lax.dot_general(
+            normed[...], back[...], (((0,), (0,)), ((), ())), preferred_element_type=jnp.float32
+        ).astype(jnp.bfloat16)
+        for head in range(heads):
+            out[:rows, pl.ds((j * heads + head) * HEAD_SIZE, HEAD_SIZE)] = part[
+                :, head * LANES : head * LANES + HEAD_SIZE
+            ]
+    out[rows:, :] = gains[...]
+
+
+def weight_stage(normed, backs, gains):
+    length, width = normed.shape
+    columns = gains.shape[1]
+    rows, extra = width // 4, gains.shape[0] // 4
+    whole = pl.BlockSpec(backs[0].shape, lambda i: (0, 0), pipeline_mode=pl.Buffered(1))
+    return pl.pallas_call(
+        weight_kernel,
+        out_shape=jax.ShapeDtypeStruct((width + 4 * extra, columns), jnp.bfloat16),
+        grid=(4,),
+        in_specs=[pl.BlockSpec((length, rows), lambda i: (0, i))]
+        + [whole] * len(backs)
+        + [pl.BlockSpec((extra, columns), lambda i: (i, 0))],
+        out_specs=pl.BlockSpec((rows + extra, columns), lambda i: (i, 0)),
+        compiler_params=pltpu.CompilerParams(vmem_limit_bytes=VMEM_BYTES),
+        cost_estimate=hint(
+            2 * length * width * columns,
+            2 * length * width + 2 * width * columns + 2 * length * columns,
+        ),
+        name="weight_stage",
+    )(normed, *backs, gains)
+
+
+def back_kernel(rows, with_base, chip_ref, grads, *rest):
+    weight, out = rest[-1], rest[-2]
+
+    @pl.when(pl.program_id(0) == 0)
+    def _():
+        weight[...] = stacked(rest[:5], rows)
+
+    part = lax.dot_general(
+        grads[...], weight[...], (((1,), (1,)), ((), ())), preferred_element_type=jnp.float32
+    )
+    for r in range(4):
+        columns = pl.ds(pl.multiple_of((chip_ref[0] ^ r) * rows, 128), rows)
+        block = part[:, r * rows : (r + 1) * rows]
+        if with_base:
+            block = block + rest[5][:, columns]
+        out[:, columns] = block
+
+
+def back_stage(grads, pieces, chip, base=None):
+    length, columns = grads.shape
+    width = (pieces[0].shape[0] // 128 * 128) * 4
+    tile = 256
+    line = pl.BlockSpec((tile, width), lambda i, c: (i, 0))
+    inputs = [grads, *pieces] + ([] if base is None else [base])
+    return pl.pallas_call(
+        lambda *refs: back_kernel(width // 4, base is not None, *refs),
+        out_shape=jax.ShapeDtypeStruct((length, width), jnp.float32),
+        grid_spec=pltpu.PrefetchScalarGridSpec(
+            num_scalar_prefetch=1,
+            grid=(length // tile,),
+            in_specs=[pl.BlockSpec((tile, columns), lambda i, c: (i, 0))]
+            + [
+                pl.BlockSpec(p.shape, lambda i, c: (0, 0), pipeline_mode=pl.Buffered(1))
+                for p in pieces
+            ]
+            + ([] if base is None else [line]),
+            out_specs=line,
+            scratch_shapes=[pltpu.VMEM((width, columns), jnp.bfloat16)],
+        ),
+        compiler_params=pltpu.CompilerParams(vmem_limit_bytes=VMEM_BYTES),
+        cost_estimate=hint(
+            2 * length * width * columns,
+            2 * length * columns + 2 * width * columns + 4 * length * width,
+        ),
+        name="back_stage",
+    )(chip.reshape(1), *inputs)
+
+
+def split_cores(field, chips):
+    piece = field.shape[1] // (2 * chips)
+    cuts = [field[:, i * piece : (i + 1) * piece] for i in range(2 * chips)]
+    return cuts[::2], cuts[1::2]
+
+
+def interleave(own, other, chips, core):
+    piece = own.shape[1] // chips
+    parts = []
+    for i in range(chips):
+        a, b = own[:, i * piece : (i + 1) * piece], other[:, i * piece : (i + 1) * piece]
+        parts += [jnp.where(core == 0, a, b), jnp.where(core == 0, b, a)]
+    return jnp.concatenate(parts, axis=1).astype(jnp.float32)
+
+
+def paired_body(
+    layer_input,
+    attn_gain,
+    query_weight,
+    key_matrix,
+    value_matrix,
+    output_weight,
+    ffn_gain,
+    gate_weight,
+    up_weight,
+    down_weight,
+    cotangent,
+):
+    f32, bf16 = jnp.float32, jnp.bfloat16
+    sequence_count, local_length, width = layer_input.shape
+    place = lax.axis_index("seq")
+    dp = lax.axis_index("dp")
+    core, chip, low = dp % 2, dp // 2, place % 2
+    length = local_length * 4
+    tokens = length // 2
+    kv_heads = KEY_VALUE_HEADS // 2
+    groups = QUERY_HEADS // KEY_VALUE_HEADS
+    kv_width = kv_heads * HEAD_SIZE
+
+    def half_rows(field):
+        return lax.dynamic_slice_in_dim(field, (1 - core) * tokens, tokens, 0)
+
+    def other_rows(field):
+        return lax.dynamic_slice_in_dim(field, core * tokens, tokens, 0)
+
+    def chain(token, *fields):
+        return lax.optimization_barrier((token,) + fields)
+
+    token = layer_input[0, 0, :8]
+    core_rows = query_weight.shape[0]
+    chip_rows = 2 * core_rows
+
+    own_gains = jnp.concatenate(
+        [attn_gain, ffn_gain, jnp.zeros((width - 2 * core_rows,), bf16)]
+    )
+    own_gains = jnp.pad(own_gains[None], ((0, 7), (0, 0)))
+    even, odd = [], []
+    for field, chips in ((query_weight, 4), (key_matrix, 2), (value_matrix, 2)):
+        first, second = split_cores(field, chips)
+        even, odd = even + first, odd + second
+    even, odd = jnp.concatenate(even, axis=1), jnp.concatenate(odd, axis=1)
+    mine, theirs = jnp.where(core == 0, even, odd), jnp.where(core == 0, odd, even)
+    theirs = flip(jnp.concatenate([theirs, own_gains], axis=0), 1)
+    inputs_parts = sequence_parts(layer_input, low)
+    theirs, their_gains = theirs[:core_rows], theirs[core_rows:]
+    attn_block = jnp.where(
+        core == 0,
+        jnp.concatenate([mine, theirs, own_gains, their_gains], axis=0),
+        jnp.concatenate([theirs, mine, their_gains, own_gains], axis=0),
+    )
+    attn_x, attn_y = flip(attn_block, 2), flip(attn_block, 4)
+    ffn_mine, ffn_theirs = prepare_ffn(gate_weight, up_weight, core)
+    ffn_other = flip(ffn_theirs, 1)
+    ffn_blocks = [pick_order(core == 1, ffn_mine[g], ffn_other[g]) for g in range(2)]
+    inputs_full = both_cores(pick_order(low == 1, *inputs_parts), core)
+    resid_in = inputs_full.astype(f32)
+    inv_one = lax.rsqrt(jnp.mean(resid_in * resid_in, axis=-1, keepdims=True) + eps)
+    unit_one = resid_in * inv_one
+    token, attn_x, attn_y = chain(token, attn_x, attn_y)
+    corner_x, corner_y = flip(attn_y[:core_rows], 2), flip(attn_x[core_rows:], 4)
+    token, corner_x, corner_y, ffn_0, down_in, upstream_in, output_in = chain(
+        token, corner_x, corner_y, ffn_blocks[0], down_weight, cotangent, output_weight
+    )
+    sides_0 = (flip(ffn_0, 2), flip(ffn_0, 4))
+
+    def gather_rows(field):
+        return lax.all_gather(field, "dp", axis=0, tiled=True, axis_index_groups=SAME_CORE)
+
+    part_rows = down_weight.shape[0] // 2
+    output_all = gather_rows(output_in)
+    down_0 = gather_rows(down_in[:part_rows])
+    upstream_parts = sequence_parts(upstream_in, low)
+
+    attn_pieces = (attn_block, attn_x, attn_y, corner_x, corner_y)
+    gain_lines = [p[-16:] for p in (attn_block, attn_x, attn_y, corner_y)]
+    gains = jnp.concatenate(
+        [g[i, :chip_rows].reshape(2, core_rows) for g in gain_lines for i in (0, 8)], axis=1
+    )
+    gains = relative_columns(gains, chip).astype(f32)
+    gain_one, gain_two = gains[0], gains[1]
+    first_normed = relative_columns((unit_one * gain_one).astype(bf16), chip)
+    cosine_table, sine_table = rope_tables(length, 0, HEAD_SIZE)
+    rest = ((0, 0), (0, LANES - HEAD_SIZE))
+    first_half = jnp.arange(HEAD_SIZE)[None, :] < HEAD_SIZE // 2
+    tables = (
+        jnp.pad(cosine_table, rest),
+        jnp.pad(jnp.where(first_half, -sine_table, 0.0), rest),
+        jnp.pad(jnp.where(first_half, 0.0, sine_table), rest),
+    )
+    heads = groups * kv_heads
+    fields, attn_weight = project_stage(first_normed, attn_pieces, tables)
+    token, fields, *sides_0 = chain(token, fields, *sides_0)
+    half = ffn_0.shape[0] // 2
+    corners_0 = (flip(sides_0[1][:half], 2), flip(sides_0[0][half:], 4))
+    attended = attention_stage(fields, heads, kv_heads)
+    token, attended, ffn_1, down_in, corner_0x, corner_0y, *upstream_parts = chain(
+        token, attended, ffn_blocks[1], down_in, *corners_0, *upstream_parts
+    )
+    sides_1 = (flip(ffn_1, 2), flip(ffn_1, 4))
+    down_1 = gather_rows(down_in[part_rows:])
+    output_all = jnp.pad(
+        output_all.reshape(heads, HEAD_SIZE, width), ((0, 0), (0, LANES - HEAD_SIZE), (0, 0))
+    ).reshape(heads * LANES, width)
+    attn_part = jnp.dot(attended, output_all, preferred_element_type=f32)
+    attn_flip = flip(attn_part.astype(bf16), 1)
+    upstream = both_cores(pick_order(low == 1, *upstream_parts), core)
+    resid_mid = resid_in + attn_part + attn_flip.astype(f32)
+    inv_two = lax.rsqrt(jnp.mean(resid_mid * resid_mid, axis=-1, keepdims=True) + eps)
+    unit_two = resid_mid * inv_two
+    normed_two = relative_columns((unit_two * gain_two).astype(bf16), chip)
+    ffn_pieces_0 = (ffn_0, *sides_0, corner_0x, corner_0y)
+
+    def scatter_down(field):
+        return lax.psum_scatter(
+            field, "dp", scatter_dimension=0, tiled=True, axis_index_groups=SAME_CORE
+        )
+
+    token, normed_two, down_0 = chain(token, normed_two, down_0)
+    hidden_0, grads_0 = hidden_stage(normed_two, upstream, ffn_pieces_0, down_0)
+    token, grads_0, hidden_0, *sides_1 = chain(token, grads_0, hidden_0, *sides_1)
+    corners_1 = (flip(sides_1[1][:half], 2), flip(sides_1[0][half:], 4))
+    ffn_grad_0 = transposed_times(normed_two, grads_0).astype(bf16)
+    token, grads_0, ffn_grad_0 = chain(token, grads_0, ffn_grad_0)
+    first_0 = scatter_first(ffn_grad_0)
+    grad_norm = back_stage(grads_0, ffn_pieces_0, chip)
+    token, grad_norm, hidden_0 = chain(token, grad_norm, hidden_0)
+    down_grad_0 = transposed_times(hidden_0, upstream).astype(bf16)
+    token, down_grad_0, normed_two, *first_0 = chain(token, down_grad_0, normed_two, *first_0)
+    second_0 = scatter_second(ffn_grad_0, *first_0)
+    down_grad_0 = scatter_down(down_grad_0)
+    token, normed_two, down_1, *corners_1 = chain(token, normed_two, down_1, *corners_1)
+    ffn_pieces_1 = (ffn_1, *sides_1, *corners_1)
+    hidden_1, grads_1 = hidden_stage(normed_two, upstream, ffn_pieces_1, down_1)
+    token, grads_1, hidden_1 = chain(token, grads_1, hidden_1)
+    ffn_grad_1 = transposed_times(normed_two, grads_1).astype(bf16)
+    token, grads_1, ffn_grad_1 = chain(token, grads_1, ffn_grad_1)
+    first_1 = scatter_first(ffn_grad_1)
+    grad_norm = back_stage(grads_1, ffn_pieces_1, chip, grad_norm)
+    token, grad_norm, hidden_1, down_grad_0, *second_0 = chain(
+        token, grad_norm, hidden_1, down_grad_0, *second_0
+    )
+    ffn_sum_0 = add_half(ffn_grad_0[:chip_rows], *second_0)
+    low_high = place % 2, place // 2
+    ffn_pair_0 = halve(ffn_sum_0, low_high[0], 1)
+    norm_flip = flip(grad_norm.astype(bf16), 1)
+    down_grad_1 = transposed_times(hidden_1, upstream).astype(bf16)
+    token, down_grad_1, grad_norm, norm_flip, *first_1 = chain(
+        token, down_grad_1, grad_norm, norm_flip, *first_1
+    )
+    second_1 = scatter_second(ffn_grad_1, *first_1)
+    down_grad_1 = scatter_down(down_grad_1)
+    grad_norm_two = grad_norm + norm_flip.astype(f32)
+    ffn_gain_grad = jnp.sum(grad_norm * unit_two, axis=0)
+    grad_mid = upstream.astype(f32) + norm_backward(grad_norm_two, unit_two, gain_two, inv_two)
+    grad_mid_half = grad_mid.astype(bf16)
+    token, grad_mid_half, ffn_pair_0 = chain(token, grad_mid_half, ffn_pair_0)
+    ffn_total_0 = halve(ffn_pair_0, low_high[1], 2)
+    grad_att = times_transposed(grad_mid_half, output_all).astype(bf16)
+    out_grad = transposed_times(attended, grad_mid_half).astype(bf16)
+    out_grad = out_grad.reshape(heads, LANES, width)[:, :HEAD_SIZE].reshape(-1, width)
+    token, grad_att, out_grad, ffn_total_0 = chain(token, grad_att, out_grad, ffn_total_0)
+    out_grad = scatter_down(out_grad)
+    ffn_pair_0 = join(ffn_total_0, low_high[1], 2)
+    backs = attention_back_stage(fields, attended, grad_att, tables, kv_heads)
+    token, down_grad_1, ffn_pair_0, *rest = chain(
+        token, down_grad_1, ffn_pair_0, *second_1, *backs
+    )
+    second_1, backs = rest[:2], rest[2:]
+    ffn_sum_1 = add_half(ffn_grad_1[:chip_rows], *second_1)
+    ffn_sum_0 = join(ffn_pair_0, low_high[0], 1)
+    ffn_pair = halve(ffn_sum_1, low_high[0], 1)
+    part_one = inputs_back_stage(backs, attn_weight, chip)
+    attn_gain_grad = jnp.sum(part_one * unit_one, axis=0)
+    gain_grads = relative_columns(jnp.stack([attn_gain_grad, ffn_gain_grad]), chip).astype(bf16)
+    gain_grads = jnp.transpose(gain_grads.reshape(2, 8, core_rows), (1, 0, 2))
+    gain_grads = jnp.pad(
+        gain_grads.reshape(8, 1, chip_rows), ((0, 0), (0, 7), (0, width - chip_rows))
+    ).reshape(64, width)
+    token, gain_grads, part_one, out_grad, ffn_pair, ffn_sum_0 = chain(
+        token, gain_grads, part_one, out_grad, ffn_pair, ffn_sum_0
+    )
+    row_grad = lax.psum(jnp.concatenate([down_grad_0, down_grad_1, out_grad], axis=0), "seq")
+    ffn_total = halve(ffn_pair, low_high[1], 2)
+    attn_grad = weight_stage(first_normed, backs, gain_grads)
+    token, attn_grad, part_one, hidden_0, hidden_1, ffn_total = chain(
+        token, attn_grad, part_one, hidden_0, hidden_1, ffn_total
+    )
+    first_2 = scatter_first(attn_grad)
+    ffn_pair = join(ffn_total, low_high[1], 2)
+    part_flip = flip(other_rows(part_one).astype(bf16), 1)
+    down_total = jnp.dot(hidden_0, down_0, preferred_element_type=f32) + jnp.dot(
+        hidden_1, down_1, preferred_element_type=f32
+    )
+    token, down_total, part_flip, *first_2 = chain(token, down_total, part_flip, *first_2)
+    second_2 = scatter_second(attn_grad, *first_2)
+    down_flip = flip(other_rows(down_total).astype(bf16), 1)
+    grad_norm_one = half_rows(part_one) + part_flip.astype(f32)
+    unit_half = half_rows(unit_one)
+    input_grad = half_rows(grad_mid) + norm_backward(
+        grad_norm_one, unit_half, gain_one, half_rows(inv_one)
+    )
+    input_parts = slice_parts(input_grad.astype(bf16), low)
+    layer_half = (half_rows(resid_mid + down_total) + down_flip.astype(f32)).astype(bf16)
+    layer_parts = slice_parts(layer_half, low)
+    token, ffn_pair, *second_2 = chain(token, ffn_pair, *second_2)
+    attn_grad = add_half(attn_grad[: chip_rows + 16], *second_2)
+    ffn_sum_1 = join(ffn_pair, low_high[0], 1)
+    tail = halve(attn_grad, low_high[0], 1)
+    token, tail, ffn_sum_1 = chain(token, tail, ffn_sum_1)
+    tail = halve(tail, low_high[1], 2)
+
+    def settle(field, size, extra=None):
+        own = lax.dynamic_slice_in_dim(field, core * size, size, 0)
+        other = lax.dynamic_slice_in_dim(field, (1 - core) * size, size, 0)
+        if extra is not None:
+            lines = extra.shape[0] // 2
+            own = (own, lax.dynamic_slice_in_dim(extra, core * lines, lines, 0))
+            other = jnp.concatenate(
+                [other, lax.dynamic_slice_in_dim(extra, (1 - core) * lines, lines, 0)], axis=0
+            )
+        return own, flip(other, 1)
+
+    settled = settle(ffn_sum_0, core_rows) + settle(ffn_sum_1, core_rows)
+    token, tail, *settled = chain(token, tail, *settled)
+    tail = join(tail, low_high[1], 2)
+    gate_grad, up_grad = merge_ffn(*settled, core)
+    token, tail, gate_grad, up_grad = chain(token, tail, gate_grad, up_grad)
+    tail = join(tail, low_high[0], 1)
+    layer_output = join_slices(layer_parts, low)
+    input_grad = join_slices(input_parts, low).astype(f32)
+    row_grad = row_grad.astype(f32)
+    down_grad, out_grad = row_grad[: 2 * part_rows], row_grad[2 * part_rows :]
+    token, tail, layer_output, input_grad, down_grad, out_grad = chain(
+        token, tail, layer_output, input_grad, down_grad, out_grad
+    )
+    (attn_own, gains_own), attn_other = settle(
+        tail[:chip_rows], core_rows, tail[chip_rows:]
+    )
+    gain_sums = (
+        0.0 * token[0].astype(f32)
+        + gains_own[0, :chip_rows].astype(f32)
+        + attn_other[core_rows, :chip_rows].astype(f32)
+    )
+    attn_other = attn_other[:core_rows]
+    cuts = (0, groups * kv_width, (groups + 1) * kv_width, (groups + 2) * kv_width)
+    query_grad, key_grad, value_grad = [
+        interleave(
+            attn_own[:, cuts[i] : cuts[i + 1]], attn_other[:, cuts[i] : cuts[i + 1]], chips, core
+        )
+        for i, chips in enumerate((4, 2, 2))
+    ]
+    return (
+        layer_output,
+        input_grad,
+        gain_sums[:core_rows],
+        query_grad,
+        key_grad,
+        value_grad,
+        out_grad,
+        gain_sums[core_rows:],
+        gate_grad,
+        up_grad,
+        down_grad,
+    )
+
+
+def any_body(layer_input, *rest):
+    paired = (
+        lax.axis_size("dp") == 8 and lax.axis_size("seq") == 4 and layer_input.shape[0] == 2
+    )
+    return (paired_body if paired else body)(layer_input, *rest)
+
+
 def solution(mesh):
     return jax.shard_map(
-        body,
+        any_body,
         mesh=mesh,
         in_specs=(
             P("dp", "seq", None),

time: 1290 us -> 789 us (0.61)
  waiting for transfers between devices: 709 us -> 285 us
  matrix products: 233 us -> 55.5 us
  Pallas kernels: 0 us -> 157 us
  blocking collectives: 143 us -> 0 us
  other arithmetic: 54.6 us -> 115 us
  starting transfers between devices: 19.1 us -> 66.9 us
  local copies, waits for them, and re-layouts: 110 us -> 87.3 us
    reduce_scatter x7 -> x3, waiting for transfers between devices: 302 us -> 0.02 us  [scatter_down(): lax.psum_scatter(field, 'dp', scatter_dimension=0, tiled=True, axis_index...]
    ppermute x0 -> x55, waiting for transfers between devices: none -> 285 us  [the longest x35 150 us: flip(): return lax.ppermute(field, 'dp', [(i, i ^ bit) for i in range(count)])]
    psum x1, waiting for transfers between devices: 177 us -> 0.02 us  [paired_body(): lax.psum(jnp.concatenate([down_grad_0, down_grad_1, out_grad], axis=0), '...]
    pallas_call x0 -> x11, Pallas kernels: none -> 157 us  [the longest x2 32.3 us: hidden_stage(): pl.pallas_call(lambda *refs: hidden_kernel(width // 4, *refs), out_shape=...]
    all_gather x7 -> x3, waiting for transfers between devices: 118 us -> 0.01 us  [gather_rows(): lax.all_gather(field, 'dp', axis=0, tiled=True, axis_index_groups=SAME_CORE)]
    all_to_all x4 -> x0, waiting for transfers between devices: 107 us -> none  [the longest x1 47.6 us: body(): lax.all_to_all(attended_heads.reshape(sequence_count, length, query_group...]
    dot_general x19 -> x3, matrix products: 119 us -> 16.9 us  [the longest x1 5.77 us: paired_body(): jnp.dot(hidden_1, down_1, preferred_element_type=f32)]
    all_to_all x2 -> x0, blocking collectives: 101 us -> none  [the longest x1 50.8 us: body(): lax.all_to_all(queries_back, 'seq', split_axis=1, concat_axis=3, tiled=True)]
  transfers between devices with their start and end apart: 19 -> 62, of which waited for: 12 -> 32; matrix products, arithmetic and copies ran while one was open for 24% -> 28% of each run, Pallas kernels for 0% -> 20%
where the time goes in v1:
time: 789 us; the launch traced here: 782 us
  waiting for transfers between devices  285 us (36%)
  Pallas kernels  157 us (20%)
  other arithmetic  115 us (15%)
  local copies, waits for them, and re-layouts  87.3 us (11%)
  starting transfers between devices  66.9 us (8%)
  matrix products  55.5 us (7%)
  between operations  16 us (2%)
    ppermute x35, waiting for transfers between devices, flip(): return lax.ppermute(field, 'dp', [(i, i ^ bit) for i in range(count)])  150 us
    ppermute x12, waiting for transfers between devices, cross(): return lax.ppermute(field, 'seq', [(i, i ^ bit) for i in range(4)])  127 us
    dot_general x5, matrix products, transposed_times(): lax.dot_general(left, right, (((0,), (0,)), ((), ())), preferred_element_...  34 us
    pallas_call x2, Pallas kernels, hidden_stage(): pl.pallas_call(lambda *refs: hidden_kernel(width // 4, *refs), out_shape=...  32.3 us
    pallas_call x1, Pallas kernels, attention_back_stage(): pl.pallas_call(lambda *refs: attention_back_kernel(tile, *refs), out_shap...  31.6 us
    ppermute x35, starting transfers between devices, flip(): return lax.ppermute(field, 'dp', [(i, i ^ bit) for i in range(count)])  27.5 us
    ppermute x12, starting transfers between devices, cross(): return lax.ppermute(field, 'seq', [(i, i ^ bit) for i in range(4)])  25.5 us
    select_n x11, other arithmetic, pick_order(): jnp.where(swapped, jnp.concatenate([second, first], axis=axis), jnp.conca...  25.3 us
  transfers between devices with their start and end apart: 62, of which 32 were waited for; matrix products, arithmetic and copies ran while one was open for 28% of the time, Pallas kernels for 20%

profile of v1, /device:TPU:0, one launch (start us, length us, event | category | flops | bytes accessed | tf_op | source)
XLA Modules:
  0.0 782.2 jit_solution(12461734069675925478)
XLA Ops:
  13.1 4.2 prepare_ffn.1
  17.9 3.0 collective-permute-start.2
  31.5 16.8 %collective-permute-done.2.refs_6_ = bf16[400,1536]{1,0:T(8,128)(2,1)} collective-permute-done((bf16[400,1536]{1,0:T(8,128)(2,1)S(1)}, bf16[400,1536]{1,0:T(8,128)(2,1)}, u32[]{:S(2)}, u32[]{:S(2)}) %collective-permute-start.2) | collective-permute-done | bytes 1228832 | tf_op jit(solution)/shard_map/ppermute | solution.py:355
  56.4 9.1 %collective-permute-done.3.refs_7_ = bf16[192,1536]{1,0:T(8,128)(2,1)S(1)} collective-permute-done((bf16[192,1536]{1,0:T(8,128)(2,1)S(1)}, bf16[192,1536]{1,0:T(8,128)(2,1)S(1)}, u32[]{:S(2)}, u32[]{:S(2)}) %collective-permute-start.3) | collective-permute-done | bytes 589856 | tf_op jit(solution)/shard_map/ppermute | solution.py:355
  68.0 3.5 maximum_select_fusion.3
  78.4 3.5 fusion
  92.4 5.3 convert_multiply_fusion
  101.5 15.3 %project_stage.1 = (bf16[1024,2048]{1,0:T(8,128)(2,1)}, bf16[1536,2048]{1,0:T(8,128)(2,1)}) custom-call(bf16[1024,1536]{1,0:T(8,128)(2,1)} %pad_maximum_fusion.refs_0_.normed, f32[1024,128]{1,0:T(8,128)S(1)} %copy-done.11, f32[1024,128]{1,0:T(8,128)S(1)} %copy-done.9, f32[1024,128]{1,0:T(8,128)S(1)} %copy-done.7, bf16[400,1536]{1,0:T(8,128)(2,1)S(1)} %copy-done.6, ...), custom_call_target="tpu_custom_call" | custom-call | flops 805306368 | bytes 1966080 | tf_op jit(solution)/shard_map/project_stage/pallas_call | solution.py:622
  116.8 16.1 %collective-permute-done.10.refs_4_ = bf16[384,2048]{1,0:T(8,128)(2,1)} collective-permute-done((bf16[384,2048]{1,0:T(8,128)(2,1)S(1)}, bf16[384,2048]{1,0:T(8,128)(2,1)}, u32[]{:S(2)}, u32[]{:S(2)}) %collective-permute-start.10) | collective-permute-done | bytes 1572896 | tf_op jit(solution)/shard_map/ppermute | solution.py:355
  139.7 19.1 %attention_stage.1.refs_4_.refs_5_ = bf16[1024,1024]{1,0:T(8,128)(2,1)S(1)} custom-call(bf16[1024,2048]{1,0:T(8,128)(2,1)} %get-tuple-element.156.refs_0_.refs_1_.refs_2_.refs_3_, bf16[1024,2048]{1,0:T(8,128)(2,1)} %get-tuple-element.156.refs_0_.refs_1_.refs_2_.refs_3_, bf16[1024,2048]{1,0:T(8,128)(2,1)} %get-tuple-element.156.refs_0_.refs_1_.refs_2_.refs_3_), custom_call_target="tpu_custom_call" | custom-call | flops 268435456 | bytes 786432 | tf_op jit(solution)/shard_map/attention_stage/pallas_call | solution.py:693
  158.9 5.4 collective-permute-done.12.refs_6_
  168.0 5.7 fusion.28
  173.8 3.5 maximum_select_fusion.5
  182.0 4.8 maximum_select_fusion.1.refs_1_
  186.8 5.5 multiply_reduce_fusion.3
  201.1 15.6 %hidden_stage.2 = (bf16[1024,1024]{1,0:T(8,128)(2,1)}, bf16[1024,2048]{1,0:T(8,128)(2,1)}) custom-call(bf16[1024,1536]{1,0:T(8,128)(2,1)} %pad_maximum_fusion.1.refs_0_, bf16[1024,1536]{1,0:T(8,128)(2,1)} %maximum_select_fusion.1.refs_1_, bf16[384,2048]{1,0:T(8,128)(2,1)S(1)} %copy-done.2, bf16[384,2048]{1,0:T(8,128)(2,1)S(1)} %copy-done.4, ...), custom_call_target="tpu_custom_call" | custom-call | flops 1207959552 | bytes 2752512 | tf_op jit(solution)/shard_map/hidden_stage/pallas_call | solution.py:552
  216.7 12.8 %collective-permute-done.18.refs_4_ = bf16[384,2048]{1,0:T(8,128)(2,1)} collective-permute-done((bf16[384,2048]{1,0:T(8,128)(2,1)}, bf16[384,2048]{1,0:T(8,128)(2,1)}, u32[]{:S(2)}, u32[]{:S(2)}) %collective-permute-start.18) | collective-permute-done | bytes 1572896 | tf_op jit(solution)/shard_map/ppermute | solution.py:355
  231.7 9.3 %convolution_convert_fusion.1 = bf16[1536,2048]{1,0:T(8,128)(2,1)S(1)} fusion(bf16[1024,1536]{1,0:T(8,128)(2,1)S(1)} %copy-done.33, bf16[1024,2048]{1,0:T(8,128)(2,1)} %get-tuple-element.177.refs_1_), kind=kOutput, calls=%fused_computation.4 | convolution fusion | flops 6445596672 | bytes 13631488 | tf_op jit(solution)/shard_map/dot_general | solution.py:51
  245.8 11.0 %back_stage.2.refs_7_ = f32[1024,1536]{1,0:T(8,128)} custom-call(s32[1]{0:T(128)} %bitcast.12.refs_0_, bf16[1024,2048]{1,0:T(8,128)(2,1)} %get-tuple-element.177.refs_1_, bf16[384,2048]{1,0:T(8,128)(2,1)S(1)} %copy-done.2, bf16[384,2048]{1,0:T(8,128)(2,1)S(1)} %copy-done.4, bf16[384,2048]{1,0:T(8,128)(2,1)} %collective-permute-done.10.refs_4_, ...), custom_call_target="tpu_custom_call" | custom-call | flops 805306368 | bytes 2097152 | tf_op jit(solution)/shard_map/back_stage/pallas_call | solution.py:877
  256.8 5.1 convolution_convert_fusion.4
  269.1 29.9 %collective-permute-done.22.refs_6_ = bf16[192,2048]{1,0:T(8,128)(2,1)S(1)} collective-permute-done((bf16[192,2048]{1,0:T(8,128)(2,1)}, bf16[192,2048]{1,0:T(8,128)(2,1)S(1)}, u32[]{:S(2)}, u32[]{:S(2)}) %collective-permute-start.22) | collective-permute-done | bytes 786464 | tf_op jit(solution)/shard_map/ppermute | solution.py:355
  298.9 3.7 collective-permute-done.21.refs_5_
  307.8 16.7 %hidden_stage.3 = (bf16[1024,1024]{1,0:T(8,128)(2,1)}, bf16[1024,2048]{1,0:T(8,128)(2,1)}) custom-call(bf16[1024,1536]{1,0:T(8,128)(2,1)} %pad_maximum_fusion.1.refs_0_, bf16[1024,1536]{1,0:T(8,128)(2,1)} %maximum_select_fusion.1.refs_1_, bf16[384,2048]{1,0:T(8,128)(2,1)} %maximum_select_fusion.4.refs_2_, bf16[384,2048]{1,0:T(8,128)(2,1)} %collective-permute-done.17.refs_3_, ...), custom_call_target="tpu_custom_call" | custom-call | flops 1207959552 | bytes 2752512 | tf_op jit(solution)/shard_map/hidden_stage/pallas_call | solution.py:552
  324.5 10.8 %convolution_convert_fusion = bf16[1536,2048]{1,0:T(8,128)(2,1)} fusion(bf16[1024,1536]{1,0:T(8,128)(2,1)S(1)} %copy-done.34, bf16[1024,2048]{1,0:T(8,128)(2,1)} %get-tuple-element.197.refs_1_), kind=kOutput, calls=%fused_computation.3 | convolution fusion | flops 6445596672 | bytes 13631488 | tf_op jit(solution)/shard_map/dot_general | solution.py:51
  335.3 13.1 %back_stage.3 = f32[1024,1536]{1,0:T(8,128)} custom-call(s32[1]{0:T(128)} %bitcast.12.refs_0_, bf16[1024,2048]{1,0:T(8,128)(2,1)} %get-tuple-element.197.refs_1_, bf16[384,2048]{1,0:T(8,128)(2,1)} %maximum_select_fusion.4.refs_2_, bf16[384,2048]{1,0:T(8,128)(2,1)} %collective-permute-done.17.refs_3_, bf16[384,2048]{1,0:T(8,128)(2,1)} %collective-permute-done.18.refs_4_, ...), custom_call_target="tpu_custom_call" | custom-call | flops 805306368 | bytes 2097152 | tf_op jit(solution)/shard_map/back_stage/pallas_call | solution.py:877
  349.6 4.8 convert_element_type.285
  354.4 3.4 fusion.21
  359.6 2.9 add_convert_fusion.2
  366.4 5.0 convolution_convert_fusion.3
  371.5 6.6 collective-permute-done.27
  379.7 5.0 collective-permute-done.28
  386.9 7.7 multiply_reduce_fusion
  396.5 5.4 fusion.19
  401.9 2.8 collective-permute-start.29
  404.7 3.8 convolution_convert_fusion.2
  411.3 4.6 convolution_convert_fusion.5.refs_6_.refs_7_
  415.9 3.8 add_convert_fusion.5
  428.3 31.6 %attention_back_stage.1 = (bf16[1024,512]{1,0:T(8,128)(2,1)S(1)}, bf16[1024,512]{1,0:T(8,128)(2,1)S(1)}, bf16[1024,512]{1,0:T(8,128)(2,1)S(1)}, bf16[1024,512]{1,0:T(8,128)(2,1)S(1)}) custom-call(bf16[1024,2048]{1,0:T(8,128)(2,1)} %get-tuple-element.156.refs_0_.refs_1_.refs_2_.refs_3_, bf16[1024,2048]{1,0:T(8,128)(2,1)} %get-tuple-element.156.refs_0_.refs_1_.refs_2_.refs_3_, ...), custom_call_target="tpu_custom_call" | custom-call | flops 671088640 | bytes 1966080 | tf_op jit(solution)/shard_map/attention_back_stage/pallas_call | solution.py:761
  464.2 15.5 %collective-permute-done.31 = bf16[384,2048]{1,0:T(8,128)(2,1)} collective-permute-done((bf16[384,2048]{1,0:T(8,128)(2,1)}, bf16[384,2048]{1,0:T(8,128)(2,1)}, u32[]{:S(2)}, u32[]{:S(2)}) %collective-permute-start.31) | collective-permute-done | bytes 1572896 | tf_op jit(solution)/shard_map/ppermute | solution.py:355
  482.0 3.4 add_convert_fusion.1
  489.6 11.4 %inputs_back_stage.1 = f32[1024,1536]{1,0:T(8,128)} custom-call(s32[1]{0:T(128)} %bitcast.12.refs_0_, bf16[1024,512]{1,0:T(8,128)(2,1)S(1)} %get-tuple-element.226.refs_1_.refs_0_, bf16[1024,512]{1,0:T(8,128)(2,1)S(1)} %copy-done.14, bf16[1024,512]{1,0:T(8,128)(2,1)S(1)} %copy-done.16, bf16[1024,512]{1,0:T(8,128)(2,1)S(1)} %copy-done.19, ...), custom_call_target="tpu_custom_call" | custom-call | flops 805306368 | bytes 2359296 | tf_op jit(solution)/shard_map/inputs_back_stage/pallas_call | solution.py:798
  501.1 5.6 multiply_reduce_fusion.1
  507.3 14.6 %collective-permute-done.34 = bf16[192,2048]{1,0:T(8,128)(2,1)} collective-permute-done((bf16[192,2048]{1,0:T(8,128)(2,1)S(1)}, bf16[192,2048]{1,0:T(8,128)(2,1)}, u32[]{:S(2)}, u32[]{:S(2)}) %collective-permute-start.34) | collective-permute-done | bytes 786464 | tf_op jit(solution)/shard_map/ppermute | solution.py:359
  521.9 3.2 maximum_select_fusion.6
  527.3 4.4 collective-permute-start.35
  532.3 3.0 pad_maximum_fusion.2
  537.8 10.4 %weight_stage.1 = bf16[1600,1536]{1,0:T(8,128)(2,1)} custom-call(bf16[1024,1536]{1,0:T(8,128)(2,1)} %pad_maximum_fusion.refs_0_.normed, bf16[1024,512]{1,0:T(8,128)(2,1)S(1)} %get-tuple-element.226.refs_1_.refs_0_, bf16[1024,512]{1,0:T(8,128)(2,1)S(1)} %copy-done.14, bf16[1024,512]{1,0:T(8,128)(2,1)S(1)} %copy-done.17, bf16[1024,512]{1,0:T(8,128)(2,1)S(1)} %copy-done.20, ...), custom_call_target="tpu_custom_call" | custom-call | flops 603979776 | bytes 1376256 | tf_op jit(solution)/shard_map/weight_stage/pallas_call | solution.py:836
  548.2 18.7 %collective-permute-done.35 = bf16[96,2048]{1,0:T(8,128)(2,1)S(1)} collective-permute-done((bf16[96,2048]{1,0:T(8,128)(2,1)}, bf16[96,2048]{1,0:T(8,128)(2,1)S(1)}, u32[]{:S(2)}, u32[]{:S(2)}) %collective-permute-start.35) | collective-permute-done | bytes 393248 | tf_op jit(solution)/shard_map/ppermute | solution.py:359
  572.2 5.4 fusion.29
  577.6 5.8 convolution_add_fusion
  583.3 4.3 collective-permute-done.38
  593.5 6.1 collective-permute-done.39
  603.3 14.6 %collective-permute-done.40 = bf16[400,1536]{1,0:T(8,128)(2,1)S(1)} collective-permute-done((bf16[400,1536]{1,0:T(8,128)(2,1)}, bf16[400,1536]{1,0:T(8,128)(2,1)S(1)}, u32[]{:S(2)}, u32[]{:S(2)}) %collective-permute-start.40) | collective-permute-done | bytes 1228832 | tf_op jit(solution)/shard_map/ppermute | solution.py:355
  622.4 14.0 %collective-permute-start.42 = (bf16[200,1536]{1,0:T(8,128)(2,1)}, bf16[200,1536]{1,0:T(8,128)(2,1)S(1)}, u32[]{:S(2)}, u32[]{:S(2)}) collective-permute-start(bf16[200,1536]{1,0:T(8,128)(2,1)} %constant_dynamic-slice_fusion.16), channel_id=1, source_target_pairs={{0,1},{1,0},{2,3},{3,2},{4,5},{5,4},{6,7},{7,6},{8,9},{9,8},{10,11... | collective-permute-start | bytes 1843208 | tf_op jit(solution)/shard_map/ppermute | solution.py:359
  641.7 14.9 %collective-permute-done.42 = bf16[200,1536]{1,0:T(8,128)(2,1)S(1)} collective-permute-done((bf16[200,1536]{1,0:T(8,128)(2,1)}, bf16[200,1536]{1,0:T(8,128)(2,1)S(1)}, u32[]{:S(2)}, u32[]{:S(2)}) %collective-permute-start.42) | collective-permute-done | bytes 614432 | tf_op jit(solution)/shard_map/ppermute | solution.py:359
  656.6 2.8 collective-permute-start.53
  659.5 29.9 %collective-permute-done.43 = bf16[192,2048]{1,0:T(8,128)(2,1)} collective-permute-done((bf16[192,2048]{1,0:T(8,128)(2,1)}, bf16[192,2048]{1,0:T(8,128)(2,1)}, u32[]{:S(2)}, u32[]{:S(2)}) %collective-permute-start.43) | collective-permute-done | bytes 786464 | tf_op jit(solution)/shard_map/ppermute | solution.py:359
  693.3 3.2 fusion.3
  696.5 17.5 %collective-permute-done.44 = bf16[100,1536]{1,0:T(8,128)(2,1)S(1)} collective-permute-done((bf16[100,1536]{1,0:T(8,128)(2,1)S(1)}, bf16[100,1536]{1,0:T(8,128)(2,1)S(1)}, u32[]{:S(2)}, u32[]{:S(2)}) %collective-permute-start.44) | collective-permute-done | bytes 307232 | tf_op jit(solution)/shard_map/ppermute | solution.py:359
  718.1 8.2 %merge_ffn.1 = (f32[192,4096]{1,0:T(8,128)}, f32[192,4096]{1,0:T(8,128)}) custom-call(s32[1]{0:T(128)} %bitcast.1.core_ref, bf16[192,2048]{1,0:T(8,128)(2,1)} %get-tuple-element.258.own_0, bf16[192,2048]{1,0:T(8,128)(2,1)} %collective-permute-done.45.other_0, bf16[192,2048]{1,0:T(8,128)(2,1)} %get-tuple-element.260.own_1, bf16[192,2048]{1,0:T(8,128)(2,1)} %copy-done.59), custom_call_target="tpu_custom_call" | custom-call | tf_op jit(solution)/shard_map/merge_ffn/pallas_call | solution.py:498
  726.3 10.9 %collective-permute-done.47 = bf16[100,1536]{1,0:T(8,128)(2,1)} collective-permute-done((bf16[100,1536]{1,0:T(8,128)(2,1)S(1)}, bf16[100,1536]{1,0:T(8,128)(2,1)}, u32[]{:S(2)}, u32[]{:S(2)}) %collective-permute-start.47) | collective-permute-done | bytes 307232 | tf_op jit(solution)/shard_map/ppermute | solution.py:359
  745.0 8.4 %collective-permute-done.51 = bf16[256,1536]{1,0:T(8,128)(2,1)} collective-permute-done((bf16[256,1536]{1,0:T(8,128)(2,1)S(1)}, bf16[256,1536]{1,0:T(8,128)(2,1)}, u32[]{:S(2)}, u32[]{:S(2)}) %collective-permute-start.51) | collective-permute-done | bytes 786464 | tf_op jit(solution)/shard_map/ppermute | solution.py:369
  753.4 3.3 maximum_select_fusion.8
  756.7 7.1 collective-permute-done.48
  (401 shorter events, 183.5 us)
Async XLA Ops:
  7.2 158.9 %all-gather.4.cloned.1.call-start = ((), (), s32[]{:S(2)}) async-start(), calls=%async_computation.3 | async-start | bytes 2949120 | tf_op jit(solution)/shard_map/all_gather | solution.py:987
  12.6 4.8 collective-permute-start
  17.4 35.9 %collective-permute-start.5 = (bf16[2,192,2048]{2,1,0:T(8,128)(2,1)}, bf16[2,192,2048]{2,1,0:T(8,128)(2,1)}, u32[]{:S(2)}, u32[]{:S(2)}) collective-permute-start(bf16[2,192,2048]{2,1,0:T(8,128)(2,1)} %get-tuple-element.148), channel_id=1, source_target_pairs={{0,4},{4,0},{8,12},{12,8},{16,20},{20,16},{24,28},{28,24},{1,5},{5... | collective-permute-start | bytes 4718600 | tf_op jit(solution)/shard_map/ppermute | solution.py:355
  17.9 30.4 %collective-permute-start.2 = (bf16[400,1536]{1,0:T(8,128)(2,1)S(1)}, bf16[400,1536]{1,0:T(8,128)(2,1)}, u32[]{:S(2)}, u32[]{:S(2)}) collective-permute-start(bf16[400,1536]{1,0:T(8,128)(2,1)S(1)} %maximum_select_fusion.10.refs_4_), channel_id=1, source_target_pairs={{0,16},{4,20},{8,24},{12,28},{16,0},{20,4},{24,8},{28,12},{1,17},{... | collective-permute-start | bytes 3686408 | tf_op jit(solution)/shard_map/ppermute | solution.py:355
  20.9 28.7 %collective-permute-start.1 = (bf16[400,1536]{1,0:T(8,128)(2,1)S(1)}, bf16[400,1536]{1,0:T(8,128)(2,1)S(1)}, u32[]{:S(2)}, u32[]{:S(2)}) collective-permute-start(bf16[400,1536]{1,0:T(8,128)(2,1)S(1)} %maximum_select_fusion.10.refs_4_), channel_id=1, source_target_pairs={{0,8},{4,12},{8,0},{12,4},{16,24},{20,28},{24,16},{28,20},{1,9},{5... | collective-permute-start | bytes 3686408 | tf_op jit(solution)/shard_map/ppermute | solution.py:355
  25.0 43.0 %collective-permute-start.6 = (bf16[256,1536]{1,0:T(8,128)(2,1)}, bf16[256,1536]{1,0:T(8,128)(2,1)}, u32[]{:S(2)}, u32[]{:S(2)}) collective-permute-start(bf16[256,1536]{1,0:T(8,128)(2,1)} %get-tuple-element.353), channel_id=1, source_target_pairs={{0,5},{1,4},{2,1},{3,0},{4,7},{5,6},{6,3},{7,2},{8,13},{9,12},{10,... | collective-permute-start | bytes 2359304 | tf_op jit(solution)/shard_map/ppermute | solution.py:369
  25.7 42.3 %collective-permute-start.7 = (bf16[256,1536]{1,0:T(8,128)(2,1)}, bf16[256,1536]{1,0:T(8,128)(2,1)}, u32[]{:S(2)}, u32[]{:S(2)}) collective-permute-start(bf16[256,1536]{1,0:T(8,128)(2,1)} %get-tuple-element.354), channel_id=1, source_target_pairs={{0,4},{1,5},{2,0},{3,1},{4,6},{5,7},{6,2},{7,3},{8,12},{9,13},{10,... | collective-permute-start | bytes 2359304 | tf_op jit(solution)/shard_map/ppermute | solution.py:369
  51.1 14.3 %collective-permute-start.3 = (bf16[192,1536]{1,0:T(8,128)(2,1)S(1)}, bf16[192,1536]{1,0:T(8,128)(2,1)S(1)}, u32[]{:S(2)}, u32[]{:S(2)}) collective-permute-start(bf16[192,1536]{1,0:T(8,128)(2,1)S(1)} %slice.354), channel_id=1, source_target_pairs={{0,8},{4,12},{8,0},{12,4},{16,24},{20,28},{24,16},{28,20},{1,9},{5... | collective-permute-start | bytes 1769480 | tf_op jit(solution)/shard_map/ppermute | solution.py:355
  52.7 15.2 %collective-permute-start.4 = (bf16[208,1536]{1,0:T(8,128)(2,1)S(1)}, bf16[208,1536]{1,0:T(8,128)(2,1)}, u32[]{:S(2)}, u32[]{:S(2)}) collective-permute-start(bf16[208,1536]{1,0:T(8,128)(2,1)S(1)} %slice.355), channel_id=1, source_target_pairs={{0,16},{4,20},{8,24},{12,28},{16,0},{20,4},{24,8},{28,12},{1,17},{... | collective-permute-start | bytes 1916936 | tf_op jit(solution)/shard_map/ppermute | solution.py:355
  67.9 129.2 %all-gather.6.cloned.1.call-start = ((), (), s32[]{:S(2)}) async-start(), calls=%async_computation.4 | async-start | bytes 3932160 | tf_op jit(solution)/shard_map/all_gather | solution.py:987
  71.5 6.9 collective-permute-start.8
  81.9 51.0 %collective-permute-start.10 = (bf16[384,2048]{1,0:T(8,128)(2,1)S(1)}, bf16[384,2048]{1,0:T(8,128)(2,1)}, u32[]{:S(2)}, u32[]{:S(2)}) collective-permute-start(bf16[384,2048]{1,0:T(8,128)(2,1)S(1)} %maximum_select_fusion.2.refs_2_), channel_id=1, source_target_pairs={{0,16},{4,20},{8,24},{12,28},{16,0},{20,4},{24,8},{28,12},{1,17},{... | collective-permute-start | bytes 4718600 | tf_op jit(solution)/shard_map/ppermute | solution.py:355
  82.6 51.6 %collective-permute-start.9 = (bf16[384,2048]{1,0:T(8,128)(2,1)S(1)}, bf16[384,2048]{1,0:T(8,128)(2,1)S(1)}, u32[]{:S(2)}, u32[]{:S(2)}) collective-permute-start(bf16[384,2048]{1,0:T(8,128)(2,1)S(1)} %maximum_select_fusion.2.refs_2_), channel_id=1, source_target_pairs={{0,8},{4,12},{8,0},{12,4},{16,24},{20,28},{24,16},{28,20},{1,9},{5... | collective-permute-start | bytes 4718600 | tf_op jit(solution)/shard_map/ppermute | solution.py:355
  88.8 70.1 %collective-permute-start.14 = (bf16[256,1536]{1,0:T(8,128)(2,1)}, bf16[256,1536]{1,0:T(8,128)(2,1)}, u32[]{:S(2)}, u32[]{:S(2)}) collective-permute-start(bf16[256,1536]{1,0:T(8,128)(2,1)} %get-tuple-element.347), channel_id=1, source_target_pairs={{0,5},{1,4},{2,1},{3,0},{4,7},{5,6},{6,3},{7,2},{8,13},{9,12},{10,... | collective-permute-start | bytes 2359304 | tf_op jit(solution)/shard_map/ppermute | solution.py:369
  89.8 69.0 %collective-permute-start.13 = (bf16[256,1536]{1,0:T(8,128)(2,1)}, bf16[256,1536]{1,0:T(8,128)(2,1)}, u32[]{:S(2)}, u32[]{:S(2)}) collective-permute-start(bf16[256,1536]{1,0:T(8,128)(2,1)} %get-tuple-element.348), channel_id=1, source_target_pairs={{0,4},{1,5},{2,0},{3,1},{4,6},{5,7},{6,2},{7,3},{8,12},{9,13},{10,... | collective-permute-start | bytes 2359304 | tf_op jit(solution)/shard_map/ppermute | solution.py:369
  92.0 177.1 %all-gather.8.cloned.1.call-start = ((), (), s32[]{:S(2)}) async-start(), calls=%async_computation.5 | async-start | bytes 3932160 | tf_op jit(solution)/shard_map/all_gather | solution.py:987
  136.0 28.3 %collective-permute-start.12 = (bf16[192,2048]{1,0:T(8,128)(2,1)S(1)}, bf16[192,2048]{1,0:T(8,128)(2,1)S(1)}, u32[]{:S(2)}, u32[]{:S(2)}) collective-permute-start(bf16[192,2048]{1,0:T(8,128)(2,1)S(1)} %slice.370), channel_id=1, source_target_pairs={{0,16},{4,20},{8,24},{12,28},{16,0},{20,4},{24,8},{28,12},{1,17},{... | collective-permute-start | bytes 2359304 | tf_op jit(solution)/shard_map/ppermute | solution.py:355
  137.4 27.8 %collective-permute-start.11 = (bf16[192,2048]{1,0:T(8,128)(2,1)S(1)}, bf16[192,2048]{1,0:T(8,128)(2,1)S(1)}, u32[]{:S(2)}, u32[]{:S(2)}) collective-permute-start(bf16[192,2048]{1,0:T(8,128)(2,1)S(1)} %slice.369), channel_id=1, source_target_pairs={{0,8},{4,12},{8,0},{12,4},{16,24},{20,28},{24,16},{28,20},{1,9},{5... | collective-permute-start | bytes 2359304 | tf_op jit(solution)/shard_map/ppermute | solution.py:355
  158.8 245.9 %copy-start = (bf16[1024,1024]{1,0:T(8,128)(2,1)}, bf16[1024,1024]{1,0:T(8,128)(2,1)S(1)}, u32[]{:S(2)}) copy-start(bf16[1024,1024]{1,0:T(8,128)(2,1)S(1)} %attention_stage.1.refs_4_.refs_5_) | copy-start | bytes 6291460
  173.8 13.1 %collective-permute-start.15 = (bf16[1024,1536]{1,0:T(8,128)(2,1)}, bf16[1024,1536]{1,0:T(8,128)(2,1)}, u32[]{:S(2)}, u32[]{:S(2)}) collective-permute-start(bf16[1024,1536]{1,0:T(8,128)(2,1)} %get-tuple-element.386), channel_id=1, source_target_pairs={{0,4},{4,0},{8,12},{12,8},{16,20},{20,16},{24,28},{28,24},{1,5},{5... | collective-permute-start | bytes 9437192 | tf_op jit(solution)/shard_map/ppermute | solution.py:355
  177.3 4.7 collective-permute-start.16
  177.8 51.8 %collective-permute-start.18 = (bf16[384,2048]{1,0:T(8,128)(2,1)}, bf16[384,2048]{1,0:T(8,128)(2,1)}, u32[]{:S(2)}, u32[]{:S(2)}) collective-permute-start(bf16[384,2048]{1,0:T(8,128)(2,1)} %maximum_select_fusion.4.refs_2_), channel_id=1, source_target_pairs={{0,16},{4,20},{8,24},{12,28},{16,0},{20,4},{24,8},{28,12},{1,17},{... | collective-permute-start | bytes 4718600 | tf_op jit(solution)/shard_map/ppermute | solution.py:355
  179.0 52.7 %collective-permute-start.17 = (bf16[384,2048]{1,0:T(8,128)(2,1)}, bf16[384,2048]{1,0:T(8,128)(2,1)}, u32[]{:S(2)}, u32[]{:S(2)}) collective-permute-start(bf16[384,2048]{1,0:T(8,128)(2,1)} %maximum_select_fusion.4.refs_2_), channel_id=1, source_target_pairs={{0,8},{4,12},{8,0},{12,4},{16,24},{20,28},{24,16},{28,20},{1,9},{5... | collective-permute-start | bytes 4718600 | tf_op jit(solution)/shard_map/ppermute | solution.py:355
  180.6 169.0 %reduce-scatter.4.cloned.1.call-start = ((), (), s32[]{:S(2)}) async-start(), calls=%async_computation.6 | async-start | bytes 3932160 | tf_op jit(solution)/shard_map/reduce_scatter | solution.py:1034
  244.7 17.2 %collective-permute-start.20 = (bf16[192,2048]{1,0:T(8,128)(2,1)}, bf16[192,2048]{1,0:T(8,128)(2,1)}, u32[]{:S(2)}, u32[]{:S(2)}) collective-permute-start(bf16[192,2048]{1,0:T(8,128)(2,1)} %get-tuple-element.305), channel_id=1, source_target_pairs={{0,16},{4,20},{8,24},{12,28},{16,0},{20,4},{24,8},{28,12},{1,17},{... | collective-permute-start | bytes 2359304 | tf_op jit(solution)/shard_map/ppermute | solution.py:355
  244.8 17.1 %collective-permute-start.19 = (bf16[192,2048]{1,0:T(8,128)(2,1)}, bf16[192,2048]{1,0:T(8,128)(2,1)}, u32[]{:S(2)}, u32[]{:S(2)}) collective-permute-start(bf16[192,2048]{1,0:T(8,128)(2,1)} %get-tuple-element.306), channel_id=1, source_target_pairs={{0,8},{4,12},{8,0},{12,4},{16,24},{20,28},{24,16},{28,20},{1,9},{5... | collective-permute-start | bytes 2359304 | tf_op jit(solution)/shard_map/ppermute | solution.py:355
  261.9 220.1 %reduce-scatter.6.cloned.1.call-start = ((), (), s32[]{:S(2)}) async-start(), calls=%async_computation.7 | async-start | bytes 3932160 | tf_op jit(solution)/shard_map/reduce_scatter | solution.py:1034
  266.1 32.8 %collective-permute-start.22 = (bf16[192,2048]{1,0:T(8,128)(2,1)}, bf16[192,2048]{1,0:T(8,128)(2,1)S(1)}, u32[]{:S(2)}, u32[]{:S(2)}) collective-permute-start(bf16[192,2048]{1,0:T(8,128)(2,1)} %slice.377), channel_id=1, source_target_pairs={{0,16},{4,20},{8,24},{12,28},{16,0},{20,4},{24,8},{28,12},{1,17},{... | collective-permute-start | bytes 2359304 | tf_op jit(solution)/shard_map/ppermute | solution.py:355
  267.8 34.8 %collective-permute-start.21 = (bf16[192,2048]{1,0:T(8,128)(2,1)}, bf16[192,2048]{1,0:T(8,128)(2,1)}, u32[]{:S(2)}, u32[]{:S(2)}) collective-permute-start(bf16[192,2048]{1,0:T(8,128)(2,1)} %slice.376), channel_id=1, source_target_pairs={{0,8},{4,12},{8,0},{12,4},{16,24},{20,28},{24,16},{28,20},{1,9},{5... | collective-permute-start | bytes 2359304 | tf_op jit(solution)/shard_map/ppermute | solution.py:355
  305.2 43.2 %collective-permute-start.23 = (bf16[384,2048]{1,0:T(8,128)(2,1)S(1)}, bf16[384,2048]{1,0:T(8,128)(2,1)S(1)}, u32[]{:S(2)}, u32[]{:S(2)}) collective-permute-start(bf16[384,2048]{1,0:T(8,128)(2,1)S(1)} %pad_maximum_fusion.3), channel_id=1, source_target_pairs={{0,8},{4,12},{8,0},{12,4},{16,24},{20,28},{24,16},{28,20},{1,9},{5... | collective-permute-start | bytes 4718600 | tf_op jit(solution)/shard_map/ppermute | solution.py:355
  307.7 41.9 %collective-permute-start.24 = (bf16[384,2048]{1,0:T(8,128)(2,1)S(1)}, bf16[384,2048]{1,0:T(8,128)(2,1)}, u32[]{:S(2)}, u32[]{:S(2)}) collective-permute-start(bf16[384,2048]{1,0:T(8,128)(2,1)S(1)} %pad_maximum_fusion.4), channel_id=1, source_target_pairs={{0,16},{4,20},{8,24},{12,28},{16,0},{20,4},{24,8},{28,12},{1,17},{... | collective-permute-start | bytes 4718600 | tf_op jit(solution)/shard_map/ppermute | solution.py:355
  354.4 25.2 %collective-permute-start.25 = (bf16[1024,1536]{1,0:T(8,128)(2,1)}, bf16[1024,1536]{1,0:T(8,128)(2,1)}, u32[]{:S(2)}, u32[]{:S(2)}) collective-permute-start(bf16[1024,1536]{1,0:T(8,128)(2,1)} %convert_element_type.285), channel_id=1, source_target_pairs={{0,4},{4,0},{8,12},{12,8},{16,20},{20,16},{24,28},{28,24},{1,5},{5... | collective-permute-start | bytes 9437192 | tf_op jit(solution)/shard_map/ppermute | solution.py:355
  357.8 20.3 %collective-permute-start.27 = (bf16[192,2048]{1,0:T(8,128)(2,1)}, bf16[192,2048]{1,0:T(8,128)(2,1)}, u32[]{:S(2)}, u32[]{:S(2)}) collective-permute-start(bf16[192,2048]{1,0:T(8,128)(2,1)} %get-tuple-element.299), channel_id=1, source_target_pairs={{0,16},{4,20},{8,24},{12,28},{16,0},{20,4},{24,8},{28,12},{1,17},{... | collective-permute-start | bytes 2359304 | tf_op jit(solution)/shard_map/ppermute | solution.py:355
  359.6 20.0 %collective-permute-start.26 = (bf16[192,2048]{1,0:T(8,128)(2,1)}, bf16[192,2048]{1,0:T(8,128)(2,1)}, u32[]{:S(2)}, u32[]{:S(2)}) collective-permute-start(bf16[192,2048]{1,0:T(8,128)(2,1)} %get-tuple-element.300), channel_id=1, source_target_pairs={{0,8},{4,12},{8,0},{12,4},{16,24},{20,28},{24,16},{28,20},{1,9},{5... | collective-permute-start | bytes 2359304 | tf_op jit(solution)/shard_map/ppermute | solution.py:355
  364.6 20.1 %collective-permute-start.28 = (bf16[192,2048]{1,0:T(8,128)(2,1)}, bf16[192,2048]{1,0:T(8,128)(2,1)}, u32[]{:S(2)}, u32[]{:S(2)}) collective-permute-start(bf16[192,2048]{1,0:T(8,128)(2,1)} %constant_dynamic-slice_fusion.24), channel_id=1, source_target_pairs={{0,1},{1,0},{2,3},{3,2},{4,5},{5,4},{6,7},{7,6},{8,9},{9,8},{10,11... | collective-permute-start | bytes 2359304 | tf_op jit(solution)/shard_map/ppermute | solution.py:359
  379.6 146.9 %reduce-scatter.8.cloned.1.call-start = ((), (), s32[]{:S(2)}) async-start(), calls=%async_computation.8 | async-start | bytes 2949120 | tf_op jit(solution)/shard_map/reduce_scatter | solution.py:1034
  401.9 19.9 %collective-permute-start.29 = (bf16[96,2048]{1,0:T(8,128)(2,1)S(1)}, bf16[96,2048]{1,0:T(8,128)(2,1)S(1)}, u32[]{:S(2)}, u32[]{:S(2)}) collective-permute-start(bf16[96,2048]{1,0:T(8,128)(2,1)S(1)} %constant_dynamic-slice_fusion.23), channel_id=1, source_target_pairs={{0,2},{1,3},{2,0},{3,1},{4,6},{5,7},{6,4},{7,5},{8,10},{9,11},{10,... | collective-permute-start | bytes 1179656 | tf_op jit(solution)/shard_map/ppermute | solution.py:359
  422.7 315.9 %all-reduce.8.cloned.1.call-start = ((), (), s32[]{:S(2)}) async-start(), calls=%async_computation.9 | async-start | bytes 4325376 | tf_op jit(solution)/shard_map/psum | solution.py:1102
  425.4 54.3 %collective-permute-start.31 = (bf16[384,2048]{1,0:T(8,128)(2,1)}, bf16[384,2048]{1,0:T(8,128)(2,1)}, u32[]{:S(2)}, u32[]{:S(2)}) collective-permute-start(bf16[384,2048]{1,0:T(8,128)(2,1)} %pad_maximum_fusion.5), channel_id=1, source_target_pairs={{0,8},{4,12},{8,0},{12,4},{16,24},{20,28},{24,16},{28,20},{1,9},{5... | collective-permute-start | bytes 4718600 | tf_op jit(solution)/shard_map/ppermute | solution.py:355
  427.9 54.2 %collective-permute-start.32 = (bf16[384,2048]{1,0:T(8,128)(2,1)}, bf16[384,2048]{1,0:T(8,128)(2,1)}, u32[]{:S(2)}, u32[]{:S(2)}) collective-permute-start(bf16[384,2048]{1,0:T(8,128)(2,1)} %pad_maximum_fusion.6), channel_id=1, source_target_pairs={{0,16},{4,20},{8,24},{12,28},{16,0},{20,4},{24,8},{28,12},{1,17},{... | collective-permute-start | bytes 4718600 | tf_op jit(solution)/shard_map/ppermute | solution.py:355
  428.2 34.6 %collective-permute-start.30 = (bf16[96,2048]{1,0:T(8,128)(2,1)}, bf16[96,2048]{1,0:T(8,128)(2,1)S(1)}, u32[]{:S(2)}, u32[]{:S(2)}) collective-permute-start(bf16[96,2048]{1,0:T(8,128)(2,1)} %add_convert_fusion.14), channel_id=1, source_target_pairs={{0,2},{1,3},{2,0},{3,1},{4,6},{5,7},{6,4},{7,5},{8,10},{9,11},{10,... | collective-permute-start | bytes 1179656 | tf_op jit(solution)/shard_map/ppermute | solution.py:359
  487.6 37.5 %collective-permute-start.33 = (bf16[192,2048]{1,0:T(8,128)(2,1)}, bf16[192,2048]{1,0:T(8,128)(2,1)}, u32[]{:S(2)}, u32[]{:S(2)}) collective-permute-start(bf16[192,2048]{1,0:T(8,128)(2,1)} %constant_dynamic-slice_fusion.18), channel_id=1, source_target_pairs={{0,1},{1,0},{2,3},{3,2},{4,5},{5,4},{6,7},{7,6},{8,9},{9,8},{10,11... | collective-permute-start | bytes 2359304 | tf_op jit(solution)/shard_map/ppermute | solution.py:359
  489.3 32.6 %collective-permute-start.34 = (bf16[192,2048]{1,0:T(8,128)(2,1)S(1)}, bf16[192,2048]{1,0:T(8,128)(2,1)}, u32[]{:S(2)}, u32[]{:S(2)}) collective-permute-start(bf16[192,2048]{1,0:T(8,128)(2,1)S(1)} %maximum_select_fusion.12), channel_id=1, source_target_pairs={{0,1},{1,0},{2,3},{3,2},{4,5},{5,4},{6,7},{7,6},{8,9},{9,8},{10,11... | collective-permute-start | bytes 2359304 | tf_op jit(solution)/shard_map/ppermute | solution.py:359
  527.3 39.6 %collective-permute-start.35 = (bf16[96,2048]{1,0:T(8,128)(2,1)}, bf16[96,2048]{1,0:T(8,128)(2,1)S(1)}, u32[]{:S(2)}, u32[]{:S(2)}) collective-permute-start(bf16[96,2048]{1,0:T(8,128)(2,1)} %constant_dynamic-slice_fusion.17), channel_id=1, source_target_pairs={{0,2},{1,3},{2,0},{3,1},{4,6},{5,7},{6,4},{7,5},{8,10},{9,11},{10,... | collective-permute-start | bytes 1179656 | tf_op jit(solution)/shard_map/ppermute | solution.py:359
  567.0 32.6 %collective-permute-start.39 = (bf16[96,2048]{1,0:T(8,128)(2,1)S(1)}, bf16[96,2048]{1,0:T(8,128)(2,1)S(1)}, u32[]{:S(2)}, u32[]{:S(2)}) collective-permute-start(bf16[96,2048]{1,0:T(8,128)(2,1)S(1)} %add_convert_fusion.13), channel_id=1, source_target_pairs={{0,2},{1,3},{2,0},{3,1},{4,6},{5,7},{6,4},{7,5},{8,10},{9,11},{10,... | collective-permute-start | bytes 1179656 | tf_op jit(solution)/shard_map/ppermute | solution.py:359
  569.4 18.3 %collective-permute-start.36 = (bf16[512,1536]{1,0:T(8,128)(2,1)S(1)}, bf16[512,1536]{1,0:T(8,128)(2,1)S(1)}, u32[]{:S(2)}, u32[]{:S(2)}) collective-permute-start(bf16[512,1536]{1,0:T(8,128)(2,1)S(1)} %dynamic-slice_convert_fusion.1), channel_id=1, source_target_pairs={{0,4},{4,0},{8,12},{12,8},{16,20},{20,16},{24,28},{28,24},{1,5},{5... | collective-permute-start | bytes 4718600 | tf_op jit(solution)/shard_map/ppermute | solution.py:355
  571.5 16.1 %collective-permute-start.38 = (bf16[200,1536]{1,0:T(8,128)(2,1)S(1)}, bf16[200,1536]{1,0:T(8,128)(2,1)S(1)}, u32[]{:S(2)}, u32[]{:S(2)}) collective-permute-start(bf16[200,1536]{1,0:T(8,128)(2,1)S(1)} %get-tuple-element.311), channel_id=1, source_target_pairs={{0,16},{4,20},{8,24},{12,28},{16,0},{20,4},{24,8},{28,12},{1,17},{... | collective-permute-start | bytes 1843208 | tf_op jit(solution)/shard_map/ppermute | solution.py:355
  571.6 16.1 %collective-permute-start.37 = (bf16[200,1536]{1,0:T(8,128)(2,1)S(1)}, bf16[200,1536]{1,0:T(8,128)(2,1)S(1)}, u32[]{:S(2)}, u32[]{:S(2)}) collective-permute-start(bf16[200,1536]{1,0:T(8,128)(2,1)S(1)} %get-tuple-element.312), channel_id=1, source_target_pairs={{0,8},{4,12},{8,0},{12,4},{16,24},{20,28},{24,16},{28,20},{1,9},{5... | collective-permute-start | bytes 1843208 | tf_op jit(solution)/shard_map/ppermute | solution.py:355
  589.2 28.8 %collective-permute-start.40 = (bf16[400,1536]{1,0:T(8,128)(2,1)}, bf16[400,1536]{1,0:T(8,128)(2,1)S(1)}, u32[]{:S(2)}, u32[]{:S(2)}) collective-permute-start(bf16[400,1536]{1,0:T(8,128)(2,1)} %pad_maximum_fusion.7), channel_id=1, source_target_pairs={{0,8},{4,12},{8,0},{12,4},{16,24},{20,28},{24,16},{28,20},{1,9},{5... | collective-permute-start | bytes 3686408 | tf_op jit(solution)/shard_map/ppermute | solution.py:355
  590.6 28.9 %collective-permute-start.41 = (bf16[400,1536]{1,0:T(8,128)(2,1)}, bf16[400,1536]{1,0:T(8,128)(2,1)}, u32[]{:S(2)}, u32[]{:S(2)}) collective-permute-start(bf16[400,1536]{1,0:T(8,128)(2,1)} %pad_maximum_fusion.8), channel_id=1, source_target_pairs={{0,16},{4,20},{8,24},{12,28},{16,0},{20,4},{24,8},{28,12},{1,17},{... | collective-permute-start | bytes 3686408 | tf_op jit(solution)/shard_map/ppermute | solution.py:355
  593.5 120.6 %collective-permute-start.45 = (bf16[192,2048]{1,0:T(8,128)(2,1)}, bf16[192,2048]{1,0:T(8,128)(2,1)}, u32[]{:S(2)}, u32[]{:S(2)}) collective-permute-start(bf16[192,2048]{1,0:T(8,128)(2,1)} %get-tuple-element.345), channel_id=1, source_target_pairs={{0,4},{4,0},{8,12},{12,8},{16,20},{20,16},{24,28},{28,24},{1,5},{5... | collective-permute-start | bytes 2359304 | tf_op jit(solution)/shard_map/ppermute | solution.py:355
  602.0 91.3 %collective-permute-start.49 = (bf16[512,1536]{1,0:T(8,128)(2,1)}, bf16[512,1536]{1,0:T(8,128)(2,1)}, u32[]{:S(2)}, u32[]{:S(2)}) collective-permute-start(bf16[512,1536]{1,0:T(8,128)(2,1)} %dynamic-slice_convert_fusion), channel_id=1, source_target_pairs={{0,4},{4,0},{8,12},{12,8},{16,20},{20,16},{24,28},{28,24},{1,5},{5... | collective-permute-start | bytes 4718600 | tf_op jit(solution)/shard_map/ppermute | solution.py:355
  619.5 73.8 %slice-start.2 = ((s8[6291456]{0:T(1024)(128)(4,1)}), s8[4194304]{0:T(1024)(128)(4,1)S(1)}, s32[]{:S(2)}) async-start(s8[6291456]{0:T(1024)(128)(4,1)} %bitcast.56), calls=%async_computation.12 | async-start | bytes 8388608
  622.4 34.2 %collective-permute-start.42 = (bf16[200,1536]{1,0:T(8,128)(2,1)}, bf16[200,1536]{1,0:T(8,128)(2,1)S(1)}, u32[]{:S(2)}, u32[]{:S(2)}) collective-permute-start(bf16[200,1536]{1,0:T(8,128)(2,1)} %constant_dynamic-slice_fusion.16), channel_id=1, source_target_pairs={{0,1},{1,0},{2,3},{3,2},{4,5},{5,4},{6,7},{7,6},{8,9},{9,8},{10,11... | collective-permute-start | bytes 1843208 | tf_op jit(solution)/shard_map/ppermute | solution.py:359
  636.4 53.0 %collective-permute-start.43 = (bf16[192,2048]{1,0:T(8,128)(2,1)}, bf16[192,2048]{1,0:T(8,128)(2,1)}, u32[]{:S(2)}, u32[]{:S(2)}) collective-permute-start(bf16[192,2048]{1,0:T(8,128)(2,1)} %maximum_select_fusion.13), channel_id=1, source_target_pairs={{0,1},{1,0},{2,3},{3,2},{4,5},{5,4},{6,7},{7,6},{8,9},{9,8},{10,11... | collective-permute-start | bytes 2359304 | tf_op jit(solution)/shard_map/ppermute | solution.py:359
  640.1 102.9 %collective-permute-start.52 = (bf16[256,1536]{1,0:T(8,128)(2,1)}, bf16[256,1536]{1,0:T(8,128)(2,1)S(1)}, u32[]{:S(2)}, u32[]{:S(2)}) collective-permute-start(bf16[256,1536]{1,0:T(8,128)(2,1)} %get-tuple-element.339), channel_id=1, source_target_pairs={{5,0},{4,1},{1,2},{0,3},{7,4},{6,5},{3,6},{2,7},{13,8},{12,9},{9,1... | collective-permute-start | bytes 2359304 | tf_op jit(solution)/shard_map/ppermute | solution.py:369
  656.6 86.5 %collective-permute-start.53 = (bf16[256,1536]{1,0:T(8,128)(2,1)}, bf16[256,1536]{1,0:T(8,128)(2,1)S(1)}, u32[]{:S(2)}, u32[]{:S(2)}) collective-permute-start(bf16[256,1536]{1,0:T(8,128)(2,1)} %get-tuple-element.340), channel_id=1, source_target_pairs={{4,0},{5,1},{0,2},{1,3},{6,4},{7,5},{2,6},{3,7},{12,8},{13,9},{8,1... | collective-permute-start | bytes 2359304 | tf_op jit(solution)/shard_map/ppermute | solution.py:369
  692.1 21.9 %collective-permute-start.44 = (bf16[100,1536]{1,0:T(8,128)(2,1)S(1)}, bf16[100,1536]{1,0:T(8,128)(2,1)S(1)}, u32[]{:S(2)}, u32[]{:S(2)}) collective-permute-start(bf16[100,1536]{1,0:T(8,128)(2,1)S(1)} %constant_dynamic-slice_fusion.15), channel_id=1, source_target_pairs={{0,2},{1,3},{2,0},{3,1},{4,6},{5,7},{6,4},{7,5},{8,10},{9,11},{10,... | collective-permute-start | bytes 921608 | tf_op jit(solution)/shard_map/ppermute | solution.py:359
  693.3 20.8 %collective-permute-start.46 = (bf16[192,2048]{1,0:T(8,128)(2,1)S(1)}, bf16[192,2048]{1,0:T(8,128)(2,1)S(1)}, u32[]{:S(2)}, u32[]{:S(2)}) collective-permute-start(bf16[192,2048]{1,0:T(8,128)(2,1)S(1)} %get-tuple-element.343), channel_id=1, source_target_pairs={{0,4},{4,0},{8,12},{12,8},{16,20},{20,16},{24,28},{28,24},{1,5},{5... | collective-permute-start | bytes 2359304 | tf_op jit(solution)/shard_map/ppermute | solution.py:355
  714.1 23.0 %collective-permute-start.47 = (bf16[100,1536]{1,0:T(8,128)(2,1)S(1)}, bf16[100,1536]{1,0:T(8,128)(2,1)}, u32[]{:S(2)}, u32[]{:S(2)}) collective-permute-start(bf16[100,1536]{1,0:T(8,128)(2,1)S(1)} %add_convert_fusion.15), channel_id=1, source_target_pairs={{0,2},{1,3},{2,0},{3,1},{4,6},{5,7},{6,4},{7,5},{8,10},{9,11},{10,... | collective-permute-start | bytes 921608 | tf_op jit(solution)/shard_map/ppermute | solution.py:359
  715.3 29.7 %collective-permute-start.50 = (bf16[256,1536]{1,0:T(8,128)(2,1)}, bf16[256,1536]{1,0:T(8,128)(2,1)}, u32[]{:S(2)}, u32[]{:S(2)}) collective-permute-start(bf16[256,1536]{1,0:T(8,128)(2,1)} %get-tuple-element.341), channel_id=1, source_target_pairs={{5,0},{4,1},{1,2},{0,3},{7,4},{6,5},{3,6},{2,7},{13,8},{12,9},{9,1... | collective-permute-start | bytes 2359304 | tf_op jit(solution)/shard_map/ppermute | solution.py:369
  715.9 37.5 %collective-permute-start.51 = (bf16[256,1536]{1,0:T(8,128)(2,1)S(1)}, bf16[256,1536]{1,0:T(8,128)(2,1)}, u32[]{:S(2)}, u32[]{:S(2)}) collective-permute-start(bf16[256,1536]{1,0:T(8,128)(2,1)S(1)} %get-tuple-element.342), channel_id=1, source_target_pairs={{4,0},{5,1},{0,2},{1,3},{6,4},{7,5},{2,6},{3,7},{12,8},{13,9},{8,1... | collective-permute-start | bytes 2359304 | tf_op jit(solution)/shard_map/ppermute | solution.py:369
  738.5 25.3 %collective-permute-start.48 = (bf16[200,1536]{1,0:T(8,128)(2,1)S(1)}, bf16[200,1536]{1,0:T(8,128)(2,1)}, u32[]{:S(2)}, u32[]{:S(2)}) collective-permute-start(bf16[200,1536]{1,0:T(8,128)(2,1)S(1)} %maximum_select_fusion.14), channel_id=1, source_target_pairs={{0,1},{1,0},{2,3},{3,2},{4,5},{5,4},{6,7},{7,6},{8,9},{9,8},{10,11... | collective-permute-start | bytes 1843208 | tf_op jit(solution)/shard_map/ppermute | solution.py:359
  765.7 4.4 collective-permute-start.54
  (79 other events, 825.0 us)
Sparse Core Ops, SparseCore 0:
  68.1 49.6 all-gather.3
  119.6 54.5 all-gather.5
  180.7 60.1 all-gather.7
  262.0 69.0 reduce-scatter.3
  379.7 43.5 reduce-scatter.5
  426.7 55.1 reduce-scatter.7
  535.5 111.1 all-reduce.7

commit v2 on v1

--- a/solution.py
+++ b/solution.py
@@ -439,23 +439,19 @@
     return flip(send_x, 2), flip(send_y, 4)
 
 
-def halve(field, bit_value, bit):
+def split_rows(field, which):
     size = field.shape[0] // 2
-    own = lax.dynamic_slice_in_dim(field, bit_value * size, size, 0)
-    other = lax.dynamic_slice_in_dim(field, (1 - bit_value) * size, size, 0)
-    return add_half(own, cross(other, bit))
-
-
-def join(field, bit_value, bit):
-    return pick_order(bit_value == 1, field, cross(field, bit))
+    own = lax.dynamic_slice_in_dim(field, which * size, size, 0)
+    return own, lax.dynamic_slice_in_dim(field, (1 - which) * size, size, 0)
 
 
 def prepare_kernel(core_ref, gate_mine, gate_theirs, up_mine, up_theirs, mine_ref, theirs_ref):
     for gate, up, out in ((gate_mine, up_mine, mine_ref), (gate_theirs, up_theirs, theirs_ref)):
         part = gate.shape[1] // 2
         for group in range(2):
-            out[group, :, :part] = gate[:, group * part : (group + 1) * part]
-            out[group, :, part:] = up[:, group * part : (group + 1) * part]
+            for offset, field in ((0, gate), (part, up)):
+                start = 2 * part * group + offset
+                out[:, start : start + part] = field[:, group * part : (group + 1) * part]
 
 
 def prepare_ffn(gate_weight, up_weight, core):
@@ -463,8 +459,8 @@
     piece = columns // 8
     mine = pl.BlockSpec((rows, piece), lambda j, c: (0, 2 * j + c[0]))
     theirs = pl.BlockSpec((rows, piece), lambda j, c: (0, 2 * j + 1 - c[0]))
-    out = pl.BlockSpec((2, rows, piece), lambda j, c: (0, 0, j))
-    shape = jax.ShapeDtypeStruct((2, rows, columns // 2), jnp.bfloat16)
+    out = pl.BlockSpec((rows, 2 * piece), lambda j, c: (0, j))
+    shape = jax.ShapeDtypeStruct((rows, columns), jnp.bfloat16)
     return pl.pallas_call(
         prepare_kernel,
         out_shape=(shape, shape),
@@ -510,7 +506,7 @@
 
 def hint(flops, bytes_accessed, transcendentals=0):
     return pl.CostEstimate(
-        flops=flops // 8, transcendentals=transcendentals // 8, bytes_accessed=bytes_accessed // 8
+        flops=flops // 64, transcendentals=transcendentals // 64, bytes_accessed=bytes_accessed // 64
     )
 
 
@@ -544,9 +540,9 @@
         grads[lines, part:] = (grad_hidden * silu_gate).astype(jnp.bfloat16)
 
 
-def hidden_stage(normed, upstream, pieces, down):
+def hidden_stage(normed, upstream, pieces, down, group):
     length, width = normed.shape
-    columns = pieces[0].shape[1]
+    columns = pieces[0].shape[1] // 2
     piece = columns // 4
     whole = pl.BlockSpec((length, width), lambda j: (0, 0), pipeline_mode=pl.Buffered(1))
     return pl.pallas_call(
@@ -557,7 +553,7 @@
         ),
         grid=(4,),
         in_specs=[whole, whole]
-        + [pl.BlockSpec((p.shape[0], piece), lambda j: (0, j)) for p in pieces]
+        + [pl.BlockSpec((p.shape[0], piece), lambda j: (0, 2 * j + group)) for p in pieces]
         + [pl.BlockSpec((piece // 2, width), lambda j: (j, 0))],
         out_specs=(
             pl.BlockSpec((length, piece // 2), lambda j: (0, j)),
@@ -619,6 +615,8 @@
     heads = columns // HEAD_SIZE
     tile = 256
     table = pl.BlockSpec((tile, LANES), lambda i: (i, 0))
+    rows, corner = width // 4, pieces[3].shape[0]
+    counts = (rows, rows, rows, corner, rows - corner)
     return pl.pallas_call(
         lambda *refs: project_kernel(width // 4, heads, *refs),
         out_shape=(
@@ -628,7 +626,8 @@
         grid=(length // tile,),
         in_specs=[pl.BlockSpec((tile, width), lambda i: (i, 0)), table, table, table]
         + [
-            pl.BlockSpec(p.shape, lambda i: (0, 0), pipeline_mode=pl.Buffered(1)) for p in pieces
+            pl.BlockSpec((count, columns), lambda i: (0, 0), pipeline_mode=pl.Buffered(1))
+            for count in counts
         ],
         out_specs=(
             pl.BlockSpec((tile, heads * LANES), lambda i: (i, 0)),
@@ -778,10 +777,10 @@
 
 
 def inputs_back_kernel(rows, chip_ref, *refs):
-    weight, out = refs[-2:]
+    weight, field, out, sums = refs[-4:]
     columns = refs[0].shape[1]
     part = 0.0
-    for j, grad in enumerate(refs[:-2]):
+    for j, grad in enumerate(refs[:-4]):
         part = part + lax.dot_general(
             grad[...], weight[:, j * columns : (j + 1) * columns], (((1,), (1,)), ((), ())),
             preferred_element_type=jnp.float32,
@@ -789,28 +788,223 @@
     for r in range(4):
         where = pl.ds(pl.multiple_of((chip_ref[0] ^ r) * rows, 128), rows)
         out[:, where] = part[:, r * rows : (r + 1) * rows]
-
-
-def inputs_back_stage(backs, weight, chip):
+    total = field[...].astype(jnp.float32)
+    unit = total * lax.rsqrt(jnp.mean(total * total, axis=1, keepdims=True) + eps)
+
+    @pl.when(pl.program_id(0) == 0)
+    def _():
+        sums[...] = jnp.zeros_like(sums)
+
+    sums[...] += jnp.sum((out[...] * unit).reshape(-1, 8, total.shape[1]), axis=0)
+
+
+def inputs_back_stage(backs, weight, chip, field):
     length, columns = backs[0].shape
     width = weight.shape[0]
     tile = 256
     return pl.pallas_call(
         lambda *refs: inputs_back_kernel(width // 4, *refs),
-        out_shape=jax.ShapeDtypeStruct((length, width), jnp.float32),
+        out_shape=(
+            jax.ShapeDtypeStruct((length, width), jnp.float32),
+            jax.ShapeDtypeStruct((8, width), jnp.float32),
+        ),
         grid_spec=pltpu.PrefetchScalarGridSpec(
             num_scalar_prefetch=1,
             grid=(length // tile,),
             in_specs=[pl.BlockSpec((tile, columns), lambda i, c: (i, 0))] * len(backs)
-            + [pl.BlockSpec(weight.shape, lambda i, c: (0, 0), pipeline_mode=pl.Buffered(1))],
-            out_specs=pl.BlockSpec((tile, width), lambda i, c: (i, 0)),
+            + [
+                pl.BlockSpec(weight.shape, lambda i, c: (0, 0), pipeline_mode=pl.Buffered(1)),
+                pl.BlockSpec((tile, width), lambda i, c: (i, 0)),
+            ],
+            out_specs=(
+                pl.BlockSpec((tile, width), lambda i, c: (i, 0)),
+                pl.BlockSpec((8, width), lambda i, c: (0, 0)),
+            ),
         ),
         compiler_params=pltpu.CompilerParams(vmem_limit_bytes=VMEM_BYTES),
         cost_estimate=hint(
             2 * length * width * weight.shape[1], 2 * width * weight.shape[1] + 8 * length * width
         ),
         name="inputs_back_stage",
-    )(chip.reshape(1), *backs, weight)
+    )(chip.reshape(1), *backs, weight, field)
+
+
+def norm_kernel(with_parts, chip_ref, field, *refs):
+    total = field[...].astype(jnp.float32)
+    if with_parts:
+        part, other, gain, middle, out = refs
+        total = total + part[...] + other[...].astype(jnp.float32)
+        middle[...] = total
+    else:
+        gain, out = refs
+    inverse = lax.rsqrt(jnp.mean(total * total, axis=1, keepdims=True) + eps)
+    normed = (total * inverse * gain[...]).astype(jnp.bfloat16)
+    width = total.shape[1] // 4
+    for j in range(4):
+        columns = pl.ds(pl.multiple_of((chip_ref[0] ^ j) * width, 128), width)
+        out[:, columns] = normed[:, j * width : (j + 1) * width]
+
+
+def norm_stage(field, gain, chip, *parts):
+    length, width = field.shape
+    tile = 256
+    line = pl.BlockSpec((tile, width), lambda i, c: (i, 0))
+    shapes = [jax.ShapeDtypeStruct((length, width), jnp.bfloat16)]
+    if parts:
+        shapes = [jax.ShapeDtypeStruct((length, width), jnp.float32)] + shapes
+    return pl.pallas_call(
+        lambda *refs: norm_kernel(len(parts) > 0, *refs),
+        out_shape=tuple(shapes),
+        grid_spec=pltpu.PrefetchScalarGridSpec(
+            num_scalar_prefetch=1,
+            grid=(length // tile,),
+            in_specs=[line] * (1 + len(parts)) + [pl.BlockSpec((1, width), lambda i, c: (0, 0))],
+            out_specs=(line,) * len(shapes),
+        ),
+        compiler_params=pltpu.CompilerParams(vmem_limit_bytes=VMEM_BYTES),
+        cost_estimate=hint(16 * length * width, 12 * length * width),
+        name="norm_stage",
+    )(chip.reshape(1), field, *parts, gain[None])
+
+
+def norm_back_kernel(grad, other, middle, upstream, gain, out, out_half, sums):
+    total = middle[...]
+    inverse = lax.rsqrt(jnp.mean(total * total, axis=1, keepdims=True) + eps)
+    unit = total * inverse
+    own = grad[...]
+    scaled = (own + other[...].astype(jnp.float32)) * gain[...]
+    average = jnp.mean(scaled * unit, axis=1, keepdims=True)
+    result = upstream[...].astype(jnp.float32) + inverse * (scaled - unit * average)
+    out[...] = result
+    out_half[...] = result.astype(jnp.bfloat16)
+
+    @pl.when(pl.program_id(0) == 0)
+    def _():
+        sums[...] = jnp.zeros_like(sums)
+
+    sums[...] += jnp.sum((own * unit).reshape(-1, 8, own.shape[1]), axis=0)
+
+
+def norm_back_stage(grad, other, middle, upstream, gain):
+    length, width = grad.shape
+    tile = 256
+    line = pl.BlockSpec((tile, width), lambda i: (i, 0))
+    return pl.pallas_call(
+        norm_back_kernel,
+        out_shape=(
+            jax.ShapeDtypeStruct((length, width), jnp.float32),
+            jax.ShapeDtypeStruct((length, width), jnp.bfloat16),
+            jax.ShapeDtypeStruct((8, width), jnp.float32),
+        ),
+        grid=(length // tile,),
+        in_specs=[line] * 4 + [pl.BlockSpec((1, width), lambda i: (0, 0))],
+        out_specs=(line, line, pl.BlockSpec((8, width), lambda i: (0, 0))),
+        compiler_params=pltpu.CompilerParams(vmem_limit_bytes=VMEM_BYTES),
+        cost_estimate=hint(16 * length * width, 18 * length * width),
+        name="norm_back_stage",
+    )(grad, other, middle, upstream, gain[None])
+
+
+def outer_kernel(left, right, out):
+    out[...] = lax.dot_general(
+        left[...], right[...], (((0,), (0,)), ((), ())), preferred_element_type=jnp.float32
+    ).astype(jnp.bfloat16)
+
+
+def outer_stage(left, right):
+    length, rows = left.shape
+    columns = right.shape[1]
+    tile = 256
+    return pl.pallas_call(
+        outer_kernel,
+        out_shape=jax.ShapeDtypeStruct((rows, columns), jnp.bfloat16),
+        grid=(rows // tile,),
+        in_specs=[
+            pl.BlockSpec((length, tile), lambda i: (0, i)),
+            pl.BlockSpec((length, columns), lambda i: (0, 0), pipeline_mode=pl.Buffered(1)),
+        ],
+        out_specs=pl.BlockSpec((tile, columns), lambda i: (i, 0)),
+        compiler_params=pltpu.CompilerParams(vmem_limit_bytes=VMEM_BYTES),
+        cost_estimate=hint(2 * length * rows * columns, 2 * (rows + columns) * length),
+        name="outer_stage",
+    )(left, right)
+
+
+def down_kernel(hidden_0, hidden_1, down_0, down_1, out):
+    out[...] = jnp.dot(
+        hidden_0[...], down_0[...], preferred_element_type=jnp.float32
+    ) + jnp.dot(hidden_1[...], down_1[...], preferred_element_type=jnp.float32)
+
+
+def down_stage(hidden_0, hidden_1, down_0, down_1):
+    length, units = hidden_0.shape
+    width = down_0.shape[1]
+    tile = 256
+    line = pl.BlockSpec((tile, units), lambda i: (i, 0))
+    whole = pl.BlockSpec((units, width), lambda i: (0, 0), pipeline_mode=pl.Buffered(1))
+    return pl.pallas_call(
+        down_kernel,
+        out_shape=jax.ShapeDtypeStruct((length, width), jnp.float32),
+        grid=(length // tile,),
+        in_specs=[line, line, whole, whole],
+        out_specs=pl.BlockSpec((tile, width), lambda i: (i, 0)),
+        compiler_params=pltpu.CompilerParams(vmem_limit_bytes=VMEM_BYTES),
+        cost_estimate=hint(4 * length * units * width, 4 * units * (length + width)),
+        name="down_stage",
+    )(hidden_0, hidden_1, down_0, down_1)
+
+
+def output_back_kernel(grad, attended, weight, out, weight_grad, total):
+    step = pl.program_id(0)
+    out[...] = lax.dot_general(
+        grad[...], weight[...], (((1,), (1,)), ((), ())), preferred_element_type=jnp.float32
+    ).astype(jnp.bfloat16)
+    part = lax.dot_general(
+        attended[...], grad[...], (((0,), (0,)), ((), ())), preferred_element_type=jnp.float32
+    )
+
+    @pl.when(step == 0)
+    def _():
+        total[...] = part
+
+    @pl.when(step > 0)
+    def _():
+        total[...] += part
+
+    @pl.when(step == pl.num_programs(0) - 1)
+    def _():
+        for head in range(total.shape[0] // LANES):
+            weight_grad[pl.ds(head * HEAD_SIZE, HEAD_SIZE), :] = total[
+                pl.ds(head * LANES, HEAD_SIZE), :
+            ].astype(jnp.bfloat16)
+
+
+def output_back_stage(grad, attended, weight):
+    length, width = grad.shape
+    columns = attended.shape[1]
+    rows = columns // LANES * HEAD_SIZE
+    tile = 512
+    return pl.pallas_call(
+        output_back_kernel,
+        out_shape=(
+            jax.ShapeDtypeStruct((length, columns), jnp.bfloat16),
+            jax.ShapeDtypeStruct((rows, width), jnp.bfloat16),
+        ),
+        grid=(length // tile,),
+        in_specs=[
+            pl.BlockSpec((tile, width), lambda i: (i, 0)),
+            pl.BlockSpec((tile, columns), lambda i: (i, 0)),
+            pl.BlockSpec((columns, width), lambda i: (0, 0), pipeline_mode=pl.Buffered(1)),
+        ],
+        out_specs=(
+            pl.BlockSpec((tile, columns), lambda i: (i, 0)),
+            pl.BlockSpec((rows, width), lambda i: (0, 0), pipeline_mode=pl.Buffered(1)),
+        ),
+        scratch_shapes=[pltpu.VMEM((columns, width), jnp.float32)],
+        compiler_params=pltpu.CompilerParams(vmem_limit_bytes=VMEM_BYTES),
+        cost_estimate=hint(4 * length * width * columns, 4 * width * (length + columns)),
+        name="output_back_stage",
+    )(grad, attended, weight)
 
 
 def weight_kernel(normed, *refs):
@@ -852,10 +1046,16 @@
 
 def back_kernel(rows, with_base, chip_ref, grads, *rest):
     weight, out = rest[-1], rest[-2]
+    piece = rest[0].shape[1]
 
     @pl.when(pl.program_id(0) == 0)
     def _():
-        weight[...] = stacked(rest[:5], rows)
+        for j in range(4):
+            start = 0
+            for part in rest[5 * j : 5 * j + 5]:
+                count = part.shape[0]
+                weight[start : start + count, j * piece : (j + 1) * piece] = part[...]
+                start += count
 
     part = lax.dot_general(
         grads[...], weight[...], (((1,), (1,)), ((), ())), preferred_element_type=jnp.float32
@@ -864,16 +1064,23 @@
         columns = pl.ds(pl.multiple_of((chip_ref[0] ^ r) * rows, 128), rows)
         block = part[:, r * rows : (r + 1) * rows]
         if with_base:
-            block = block + rest[5][:, columns]
+            block = block + rest[20][:, columns]
         out[:, columns] = block
 
 
-def back_stage(grads, pieces, chip, base=None):
+def back_stage(grads, pieces, chip, group, base=None):
     length, columns = grads.shape
-    width = (pieces[0].shape[0] // 128 * 128) * 4
+    width = pieces[0].shape[0] * 4
+    piece = columns // 4
     tile = 256
     line = pl.BlockSpec((tile, width), lambda i, c: (i, 0))
-    inputs = [grads, *pieces] + ([] if base is None else [base])
+
+    def part_spec(rows, j):
+        return pl.BlockSpec(
+            (rows, piece), lambda i, c: (0, 2 * j + group), pipeline_mode=pl.Buffered(1)
+        )
+
+    inputs = [grads, *(list(pieces) * 4)] + ([] if base is None else [base])
     return pl.pallas_call(
         lambda *refs: back_kernel(width // 4, base is not None, *refs),
         out_shape=jax.ShapeDtypeStruct((length, width), jnp.float32),
@@ -881,10 +1088,7 @@
             num_scalar_prefetch=1,
             grid=(length // tile,),
             in_specs=[pl.BlockSpec((tile, columns), lambda i, c: (i, 0))]
-            + [
-                pl.BlockSpec(p.shape, lambda i, c: (0, 0), pipeline_mode=pl.Buffered(1))
-                for p in pieces
-            ]
+            + [part_spec(p.shape[0], j) for j in range(4) for p in pieces]
             + ([] if base is None else [line]),
             out_specs=line,
             scratch_shapes=[pltpu.VMEM((width, columns), jnp.bfloat16)],
@@ -961,44 +1165,60 @@
     even, odd = jnp.concatenate(even, axis=1), jnp.concatenate(odd, axis=1)
     mine, theirs = jnp.where(core == 0, even, odd), jnp.where(core == 0, odd, even)
     theirs = flip(jnp.concatenate([theirs, own_gains], axis=0), 1)
-    inputs_parts = sequence_parts(layer_input, low)
+    both_parts = sequence_parts(jnp.concatenate([layer_input, cotangent], axis=1), low)
     theirs, their_gains = theirs[:core_rows], theirs[core_rows:]
     attn_block = jnp.where(
         core == 0,
         jnp.concatenate([mine, theirs, own_gains, their_gains], axis=0),
         jnp.concatenate([theirs, mine, their_gains, own_gains], axis=0),
     )
+    part_rows = down_weight.shape[0] // 2
+    share = part_rows // 4
+    down_quarters = [
+        lax.dynamic_slice_in_dim(down_weight, g * part_rows + place * share, share, 0)
+        for g in range(2)
+    ]
+    attn_block = jnp.concatenate([attn_block, output_weight, *down_quarters], axis=0)
+    cut = attn_block.shape[0] // 32 * 16
     attn_x, attn_y = flip(attn_block, 2), flip(attn_block, 4)
     ffn_mine, ffn_theirs = prepare_ffn(gate_weight, up_weight, core)
     ffn_other = flip(ffn_theirs, 1)
-    ffn_blocks = [pick_order(core == 1, ffn_mine[g], ffn_other[g]) for g in range(2)]
-    inputs_full = both_cores(pick_order(low == 1, *inputs_parts), core)
-    resid_in = inputs_full.astype(f32)
-    inv_one = lax.rsqrt(jnp.mean(resid_in * resid_in, axis=-1, keepdims=True) + eps)
-    unit_one = resid_in * inv_one
+    ffn_block = pick_order(core == 1, ffn_mine, ffn_other)
     token, attn_x, attn_y = chain(token, attn_x, attn_y)
-    corner_x, corner_y = flip(attn_y[:core_rows], 2), flip(attn_x[core_rows:], 4)
-    token, corner_x, corner_y, ffn_0, down_in, upstream_in, output_in = chain(
-        token, corner_x, corner_y, ffn_blocks[0], down_weight, cotangent, output_weight
-    )
-    sides_0 = (flip(ffn_0, 2), flip(ffn_0, 4))
-
-    def gather_rows(field):
-        return lax.all_gather(field, "dp", axis=0, tiled=True, axis_index_groups=SAME_CORE)
-
-    part_rows = down_weight.shape[0] // 2
-    output_all = gather_rows(output_in)
-    down_0 = gather_rows(down_in[:part_rows])
-    upstream_parts = sequence_parts(upstream_in, low)
+    corner_x, corner_y = flip(attn_y[:cut], 2), flip(attn_x[cut:], 4)
+    token, corner_x, corner_y, ffn_block, *both_parts = chain(
+        token, corner_x, corner_y, ffn_block, *both_parts
+    )
+    ffn_sides = (flip(ffn_block, 2), flip(ffn_block, 4))
+    halves = [p.reshape(2, local_length, width) for p in both_parts]
+    here = pick_order(low == 1, *halves, axis=1)
+    there = flip(here, 1)
+    both = pick_order(core == 0, here, there, axis=1)
+    inputs_full, upstream = both[0], both[1]
+
 
     attn_pieces = (attn_block, attn_x, attn_y, corner_x, corner_y)
-    gain_lines = [p[-16:] for p in (attn_block, attn_x, attn_y, corner_y)]
+    extras = [p[-(16 + core_rows + 2 * share) :] for p in (attn_block, attn_x, attn_y, corner_y)]
     gains = jnp.concatenate(
-        [g[i, :chip_rows].reshape(2, core_rows) for g in gain_lines for i in (0, 8)], axis=1
-    )
+        [g[i, :chip_rows].reshape(2, core_rows) for g in extras for i in (0, 8)], axis=1
+    )
+
+    def chip_order(start, count):
+        field = jnp.stack([g[start : start + count] for g in extras])
+        return jnp.concatenate(
+            [lax.dynamic_index_in_dim(field, chip ^ r, 0, keepdims=False) for r in range(4)], axis=0
+        )
+
+    def share_quarters(field):
+        whole = lax.all_gather(field, "seq", axis=0)
+        return jnp.swapaxes(whole.reshape(4, 4, share, width), 0, 1).reshape(-1, width)
+
+    output_all = chip_order(16, core_rows)
+    down_0 = share_quarters(chip_order(16 + core_rows, share))
+    down_1 = share_quarters(chip_order(16 + core_rows + share, share))
     gains = relative_columns(gains, chip).astype(f32)
     gain_one, gain_two = gains[0], gains[1]
-    first_normed = relative_columns((unit_one * gain_one).astype(bf16), chip)
+    (first_normed,) = norm_stage(inputs_full, gain_one, chip)
     cosine_table, sine_table = rope_tables(length, 0, HEAD_SIZE)
     rest = ((0, 0), (0, LANES - HEAD_SIZE))
     first_half = jnp.arange(HEAD_SIZE)[None, :] < HEAD_SIZE // 2
@@ -1009,125 +1229,125 @@
     )
     heads = groups * kv_heads
     fields, attn_weight = project_stage(first_normed, attn_pieces, tables)
-    token, fields, *sides_0 = chain(token, fields, *sides_0)
-    half = ffn_0.shape[0] // 2
-    corners_0 = (flip(sides_0[1][:half], 2), flip(sides_0[0][half:], 4))
     attended = attention_stage(fields, heads, kv_heads)
-    token, attended, ffn_1, down_in, corner_0x, corner_0y, *upstream_parts = chain(
-        token, attended, ffn_blocks[1], down_in, *corners_0, *upstream_parts
-    )
-    sides_1 = (flip(ffn_1, 2), flip(ffn_1, 4))
-    down_1 = gather_rows(down_in[part_rows:])
+    token, attended, ffn_x, ffn_y = chain(token, attended, *ffn_sides)
+    half = ffn_block.shape[0] // 2
+    ffn_corners = (flip(ffn_y[:half], 2), flip(ffn_x[half:], 4))
     output_all = jnp.pad(
         output_all.reshape(heads, HEAD_SIZE, width), ((0, 0), (0, LANES - HEAD_SIZE), (0, 0))
     ).reshape(heads * LANES, width)
     attn_part = jnp.dot(attended, output_all, preferred_element_type=f32)
     attn_flip = flip(attn_part.astype(bf16), 1)
-    upstream = both_cores(pick_order(low == 1, *upstream_parts), core)
-    resid_mid = resid_in + attn_part + attn_flip.astype(f32)
-    inv_two = lax.rsqrt(jnp.mean(resid_mid * resid_mid, axis=-1, keepdims=True) + eps)
-    unit_two = resid_mid * inv_two
-    normed_two = relative_columns((unit_two * gain_two).astype(bf16), chip)
-    ffn_pieces_0 = (ffn_0, *sides_0, corner_0x, corner_0y)
+    token, attn_flip = chain(token, attn_flip)
+    resid_mid, normed_two = norm_stage(inputs_full, gain_two, chip, attn_part, attn_flip)
 
     def scatter_down(field):
         return lax.psum_scatter(
             field, "dp", scatter_dimension=0, tiled=True, axis_index_groups=SAME_CORE
         )
 
-    token, normed_two, down_0 = chain(token, normed_two, down_0)
-    hidden_0, grads_0 = hidden_stage(normed_two, upstream, ffn_pieces_0, down_0)
-    token, grads_0, hidden_0, *sides_1 = chain(token, grads_0, hidden_0, *sides_1)
-    corners_1 = (flip(sides_1[1][:half], 2), flip(sides_1[0][half:], 4))
-    ffn_grad_0 = transposed_times(normed_two, grads_0).astype(bf16)
+    token, normed_two, down_0, *ffn_corners = chain(token, normed_two, down_0, *ffn_corners)
+    ffn_pieces = (ffn_block, ffn_x, ffn_y, *ffn_corners)
+    hidden_0, grads_0 = hidden_stage(normed_two, upstream, ffn_pieces, down_0, 0)
+    token, grads_0, hidden_0 = chain(token, grads_0, hidden_0)
+    ffn_grad_0 = outer_stage(normed_two, grads_0)
     token, grads_0, ffn_grad_0 = chain(token, grads_0, ffn_grad_0)
     first_0 = scatter_first(ffn_grad_0)
-    grad_norm = back_stage(grads_0, ffn_pieces_0, chip)
+    grad_norm = back_stage(grads_0, ffn_pieces, chip, 0)
     token, grad_norm, hidden_0 = chain(token, grad_norm, hidden_0)
-    down_grad_0 = transposed_times(hidden_0, upstream).astype(bf16)
-    token, down_grad_0, normed_two, *first_0 = chain(token, down_grad_0, normed_two, *first_0)
+    down_grad_0 = outer_stage(hidden_0, upstream)
+    token, down_grad_0, normed_two, down_1, *first_0 = chain(
+        token, down_grad_0, normed_two, down_1, *first_0
+    )
     second_0 = scatter_second(ffn_grad_0, *first_0)
     down_grad_0 = scatter_down(down_grad_0)
-    token, normed_two, down_1, *corners_1 = chain(token, normed_two, down_1, *corners_1)
-    ffn_pieces_1 = (ffn_1, *sides_1, *corners_1)
-    hidden_1, grads_1 = hidden_stage(normed_two, upstream, ffn_pieces_1, down_1)
+    hidden_1, grads_1 = hidden_stage(normed_two, upstream, ffn_pieces, down_1, 1)
     token, grads_1, hidden_1 = chain(token, grads_1, hidden_1)
-    ffn_grad_1 = transposed_times(normed_two, grads_1).astype(bf16)
+    ffn_grad_1 = outer_stage(normed_two, grads_1)
     token, grads_1, ffn_grad_1 = chain(token, grads_1, ffn_grad_1)
     first_1 = scatter_first(ffn_grad_1)
-    grad_norm = back_stage(grads_1, ffn_pieces_1, chip, grad_norm)
-    token, grad_norm, hidden_1, down_grad_0, *second_0 = chain(
-        token, grad_norm, hidden_1, down_grad_0, *second_0
-    )
+    grad_norm = back_stage(grads_1, ffn_pieces, chip, 1, grad_norm)
+    token, grad_norm, hidden_1 = chain(token, grad_norm, hidden_1)
+    norm_flip = flip(grad_norm.astype(bf16), 1)
+    down_grad_1 = outer_stage(hidden_1, upstream)
+    token, down_grad_1, hidden_1, *second_0 = chain(token, down_grad_1, hidden_1, *second_0)
     ffn_sum_0 = add_half(ffn_grad_0[:chip_rows], *second_0)
-    low_high = place % 2, place // 2
-    ffn_pair_0 = halve(ffn_sum_0, low_high[0], 1)
-    norm_flip = flip(grad_norm.astype(bf16), 1)
-    down_grad_1 = transposed_times(hidden_1, upstream).astype(bf16)
-    token, down_grad_1, grad_norm, norm_flip, *first_1 = chain(
-        token, down_grad_1, grad_norm, norm_flip, *first_1
+    own_0, other_0 = split_rows(ffn_sum_0, low)
+    near_0 = cross(other_0, 1)
+    down_total = down_stage(hidden_0, hidden_1, down_0, down_1)
+    token, down_grad_0, down_grad_1, down_total, grad_norm, norm_flip, near_0, *first_1 = chain(
+        token, down_grad_0, down_grad_1, down_total, grad_norm, norm_flip, near_0, *first_1
     )
     second_1 = scatter_second(ffn_grad_1, *first_1)
     down_grad_1 = scatter_down(down_grad_1)
-    grad_norm_two = grad_norm + norm_flip.astype(f32)
-    ffn_gain_grad = jnp.sum(grad_norm * unit_two, axis=0)
-    grad_mid = upstream.astype(f32) + norm_backward(grad_norm_two, unit_two, gain_two, inv_two)
-    grad_mid_half = grad_mid.astype(bf16)
-    token, grad_mid_half, ffn_pair_0 = chain(token, grad_mid_half, ffn_pair_0)
-    ffn_total_0 = halve(ffn_pair_0, low_high[1], 2)
-    grad_att = times_transposed(grad_mid_half, output_all).astype(bf16)
-    out_grad = transposed_times(attended, grad_mid_half).astype(bf16)
-    out_grad = out_grad.reshape(heads, LANES, width)[:, :HEAD_SIZE].reshape(-1, width)
-    token, grad_att, out_grad, ffn_total_0 = chain(token, grad_att, out_grad, ffn_total_0)
+    pair_0 = add_half(own_0, near_0)
+    far_0 = cross(pair_0, 2)
+    down_flip = flip(other_rows(down_total).astype(bf16), 1)
+    grad_mid, grad_mid_half, gain_sums_two = norm_back_stage(
+        grad_norm, norm_flip, resid_mid, upstream, gain_two
+    )
+    ffn_gain_grad = jnp.sum(gain_sums_two, axis=0)
+    token, grad_mid_half, down_flip = chain(token, grad_mid_half, down_flip)
+    layer_half = (half_rows(resid_mid + down_total) + down_flip.astype(f32)).astype(bf16)
+    grad_att, out_grad = output_back_stage(grad_mid_half, attended, output_all)
+    token, grad_att, out_grad, layer_half, far_0 = chain(
+        token, grad_att, out_grad, layer_half, far_0
+    )
     out_grad = scatter_down(out_grad)
-    ffn_pair_0 = join(ffn_total_0, low_high[1], 2)
+    total_0 = add_half(pair_0, far_0)
+    last_0 = cross(total_0, 1)
+    layer_parts = slice_parts(layer_half, low)
     backs = attention_back_stage(fields, attended, grad_att, tables, kv_heads)
-    token, down_grad_1, ffn_pair_0, *rest = chain(
-        token, down_grad_1, ffn_pair_0, *second_1, *backs
-    )
-    second_1, backs = rest[:2], rest[2:]
+    token, last_0, down_grad_1, *rest = chain(
+        token, last_0, down_grad_1, *second_1, *layer_parts, *backs
+    )
+    second_1, layer_parts, backs = rest[:2], rest[2:4], rest[4:]
     ffn_sum_1 = add_half(ffn_grad_1[:chip_rows], *second_1)
-    ffn_sum_0 = join(ffn_pair_0, low_high[0], 1)
-    ffn_pair = halve(ffn_sum_1, low_high[0], 1)
-    part_one = inputs_back_stage(backs, attn_weight, chip)
-    attn_gain_grad = jnp.sum(part_one * unit_one, axis=0)
+    own_1, other_1 = split_rows(ffn_sum_1, low)
+    near_1 = cross(other_1, 1)
+    part_one, gain_sums_one = inputs_back_stage(backs, attn_weight, chip, inputs_full)
+    attn_gain_grad = jnp.sum(gain_sums_one, axis=0)
     gain_grads = relative_columns(jnp.stack([attn_gain_grad, ffn_gain_grad]), chip).astype(bf16)
     gain_grads = jnp.transpose(gain_grads.reshape(2, 8, core_rows), (1, 0, 2))
     gain_grads = jnp.pad(
         gain_grads.reshape(8, 1, chip_rows), ((0, 0), (0, 7), (0, width - chip_rows))
     ).reshape(64, width)
-    token, gain_grads, part_one, out_grad, ffn_pair, ffn_sum_0 = chain(
-        token, gain_grads, part_one, out_grad, ffn_pair, ffn_sum_0
-    )
-    row_grad = lax.psum(jnp.concatenate([down_grad_0, down_grad_1, out_grad], axis=0), "seq")
-    ffn_total = halve(ffn_pair, low_high[1], 2)
+    token, gain_grads, part_one, out_grad, near_1 = chain(
+        token, gain_grads, part_one, out_grad, near_1
+    )
+    row_sum = lax.psum(jnp.concatenate([down_grad_0, down_grad_1, out_grad], axis=0), "seq")
+    pair_1 = add_half(own_1, near_1)
+    far_1 = cross(pair_1, 2)
     attn_grad = weight_stage(first_normed, backs, gain_grads)
-    token, attn_grad, part_one, hidden_0, hidden_1, ffn_total = chain(
-        token, attn_grad, part_one, hidden_0, hidden_1, ffn_total
-    )
+    token, attn_grad, part_one = chain(token, attn_grad, part_one)
     first_2 = scatter_first(attn_grad)
-    ffn_pair = join(ffn_total, low_high[1], 2)
     part_flip = flip(other_rows(part_one).astype(bf16), 1)
-    down_total = jnp.dot(hidden_0, down_0, preferred_element_type=f32) + jnp.dot(
-        hidden_1, down_1, preferred_element_type=f32
-    )
-    token, down_total, part_flip, *first_2 = chain(token, down_total, part_flip, *first_2)
+    layer_output = join_slices(layer_parts, low)
+    ffn_sum_0 = pick_order(low == 1, total_0, last_0)
+    token, layer_output, ffn_sum_0, part_flip, far_1, *first_2 = chain(
+        token, layer_output, ffn_sum_0, part_flip, far_1, *first_2
+    )
     second_2 = scatter_second(attn_grad, *first_2)
-    down_flip = flip(other_rows(down_total).astype(bf16), 1)
+    total_1 = add_half(pair_1, far_1)
+    last_1 = cross(total_1, 1)
     grad_norm_one = half_rows(part_one) + part_flip.astype(f32)
-    unit_half = half_rows(unit_one)
+    resid_in = half_rows(inputs_full).astype(f32)
+    inverse = lax.rsqrt(jnp.mean(resid_in * resid_in, axis=-1, keepdims=True) + eps)
     input_grad = half_rows(grad_mid) + norm_backward(
-        grad_norm_one, unit_half, gain_one, half_rows(inv_one)
-    )
+        grad_norm_one, resid_in * inverse, gain_one, inverse
+    )
+    token, input_grad, last_1, *second_2 = chain(token, input_grad, last_1, *second_2)
+    attn_grad = add_half(attn_grad[: chip_rows + 16], *second_2)
+    tail_own, tail_other = split_rows(attn_grad, low)
+    tail_near = cross(tail_other, 1)
+    token, tail_near, row_sum = chain(token, tail_near, row_sum)
+    tail = add_half(tail_own, tail_near)
+    tail_far = cross(tail, 2)
     input_parts = slice_parts(input_grad.astype(bf16), low)
-    layer_half = (half_rows(resid_mid + down_total) + down_flip.astype(f32)).astype(bf16)
-    layer_parts = slice_parts(layer_half, low)
-    token, ffn_pair, *second_2 = chain(token, ffn_pair, *second_2)
-    attn_grad = add_half(attn_grad[: chip_rows + 16], *second_2)
-    ffn_sum_1 = join(ffn_pair, low_high[0], 1)
-    tail = halve(attn_grad, low_high[0], 1)
-    token, tail, ffn_sum_1 = chain(token, tail, ffn_sum_1)
-    tail = halve(tail, low_high[1], 2)
+    token, tail_far = chain(token, tail_far)
+    tail = add_half(tail, tail_far)
+    tail_last = cross(tail, 1)
+    ffn_sum_1 = pick_order(low == 1, total_1, last_1)
 
     def settle(field, size, extra=None):
         own = lax.dynamic_slice_in_dim(field, core * size, size, 0)
@@ -1141,18 +1361,14 @@
         return own, flip(other, 1)
 
     settled = settle(ffn_sum_0, core_rows) + settle(ffn_sum_1, core_rows)
-    token, tail, *settled = chain(token, tail, *settled)
-    tail = join(tail, low_high[1], 2)
+    token, *settled = chain(token, *settled)
     gate_grad, up_grad = merge_ffn(*settled, core)
-    token, tail, gate_grad, up_grad = chain(token, tail, gate_grad, up_grad)
-    tail = join(tail, low_high[0], 1)
-    layer_output = join_slices(layer_parts, low)
-    input_grad = join_slices(input_parts, low).astype(f32)
-    row_grad = row_grad.astype(f32)
-    down_grad, out_grad = row_grad[: 2 * part_rows], row_grad[2 * part_rows :]
-    token, tail, layer_output, input_grad, down_grad, out_grad = chain(
-        token, tail, layer_output, input_grad, down_grad, out_grad
-    )
+    row_sum = row_sum.astype(f32)
+    down_grad, out_grad = row_sum[: 2 * part_rows], row_sum[2 * part_rows :]
+    token, tail_last, gate_grad, up_grad, down_grad, out_grad = chain(
+        token, tail_last, gate_grad, up_grad, down_grad, out_grad
+    )
+    tail = pick_order(low == 1, tail, tail_last)
     (attn_own, gains_own), attn_other = settle(
         tail[:chip_rows], core_rows, tail[chip_rows:]
     )
@@ -1162,6 +1378,7 @@
         + attn_other[core_rows, :chip_rows].astype(f32)
     )
     attn_other = attn_other[:core_rows]
+    input_grad = join_slices(input_parts, low).astype(f32)
     cuts = (0, groups * kv_width, (groups + 1) * kv_width, (groups + 2) * kv_width)
     query_grad, key_grad, value_grad = [
         interleave(

time: 789 us -> 780 us (0.989)
  Pallas kernels: 157 us -> 242 us
  matrix products: 55.5 us -> 5.88 us
  starting transfers between devices: 66.9 us -> 31.2 us
  other arithmetic: 115 us -> 86.3 us
  waiting for transfers between devices: 285 us -> 300 us
    pallas_call x0 -> x9, Pallas kernels: none -> 83 us  [the longest x4 37.1 us: outer_stage(): pl.pallas_call(outer_kernel, out_shape=jax.ShapeDtypeStruct((rows, column...]
    ppermute x35 -> x30, waiting for transfers between devices: 150 us -> 99.2 us  [flip(): return lax.ppermute(field, 'dp', [(i, i ^ bit) for i in range(count)])]
    dot_general x8 -> x0, matrix products: 49.8 us -> none  [the longest x5 34 us: transposed_times(): lax.dot_general(left, right, (((0,), (0,)), ((), ())), preferred_element_...]
    ppermute x12 -> x9, waiting for transfers between devices: 127 us -> 174 us  [cross(): return lax.ppermute(field, 'seq', [(i, i ^ bit) for i in range(4)])]
    ppermute x12 -> x9, starting transfers between devices: 25.5 us -> 1.14 us  [cross(): return lax.ppermute(field, 'seq', [(i, i ^ bit) for i in range(4)])]
    ppermute x8 -> x6, waiting for transfers between devices: 8.41 us -> 27.2 us  [column_swap(): return lax.ppermute(field, ('dp', 'seq'), pairs)]
    reduce_sum x3 -> x2, other arithmetic: 18.8 us -> 0.05 us  [the longest x1 0.03 us: paired_body(): ffn_gain_grad = jnp.sum(gain_sums_two, axis=0)]
    another operation x1 -> x6, local copies, waits for them, and re-layouts: 0.65 us -> 9.14 us  [chip_order(): field = jnp.stack([g[start:start + count] for g in extras])]
  transfers between devices with their start and end apart: 62 -> 51, of which waited for: 32 -> 23; matrix products, arithmetic and copies ran while one was open for 28% -> 19% of each run, Pallas kernels for 20% -> 30%
where the time goes in v2:
time: 780 us; the launch traced here: 772 us
  waiting for transfers between devices  300 us (38%)
  Pallas kernels  242 us (31%)
  local copies, waits for them, and re-layouts  91.1 us (12%)
  other arithmetic  86.3 us (11%)
  starting transfers between devices  31.2 us (4%)
  between operations  15.6 us (2%)
    ppermute x9, waiting for transfers between devices, cross(): return lax.ppermute(field, 'seq', [(i, i ^ bit) for i in range(4)])  174 us
    ppermute x30, waiting for transfers between devices, flip(): return lax.ppermute(field, 'dp', [(i, i ^ bit) for i in range(count)])  99.2 us
    pallas_call x4, Pallas kernels, outer_stage(): pl.pallas_call(outer_kernel, out_shape=jax.ShapeDtypeStruct((rows, column...  37.1 us
    pallas_call x2, Pallas kernels, hidden_stage(): pl.pallas_call(lambda *refs: hidden_kernel(width // 4, *refs), out_shape=...  32.1 us
    pallas_call x1, Pallas kernels, attention_back_stage(): pl.pallas_call(lambda *refs: attention_back_kernel(tile, *refs), out_shap...  31.6 us
    ppermute x6, waiting for transfers between devices, column_swap(): return lax.ppermute(field, ('dp', 'seq'), pairs)  27.2 us
    pallas_call x2, Pallas kernels, back_stage(): pl.pallas_call(lambda *refs: back_kernel(width // 4, base is not None, *r...  25.3 us
    convert_element_type x12, other arithmetic, add_half(): return total.astype(jnp.bfloat16)  23.5 us
  transfers between devices with their start and end apart: 51, of which 23 were waited for; matrix products, arithmetic and copies ran while one was open for 19% of the time, Pallas kernels for 30%

profile of v2, /device:TPU:0, one launch (start us, length us, event | category | flops | bytes accessed | tf_op | source)
XLA Modules:
  0.0 772.4 jit_solution(16059029350561877231)
XLA Ops:
  17.2 2.9 collective-permute-start.2
  21.6 4.3 prepare_ffn.1
  31.5 2.1 collective-permute-start.6
  35.0 33.6 %collective-permute-done.2.refs_6_ = bf16[720,1536]{1,0:T(8,128)(2,1)} collective-permute-done((bf16[720,1536]{1,0:T(8,128)(2,1)S(1)}, bf16[720,1536]{1,0:T(8,128)(2,1)}, u32[]{:S(2)}, u32[]{:S(2)}) %collective-permute-start.2) | collective-permute-done | bytes 2211872 | tf_op jit(solution)/shard_map/ppermute | solution.py:355
  74.8 3.7 maximum_select_fusion.1.refs_2_.refs_7_.refs_12_.refs_17_
  82.0 20.1 %collective-permute-done.6 = bf16[512,1536]{1,0:T(8,128)(2,1)} collective-permute-done((bf16[512,1536]{1,0:T(8,128)(2,1)}, bf16[512,1536]{1,0:T(8,128)(2,1)}, u32[]{:S(2)}, u32[]{:S(2)}) %collective-permute-start.6) | collective-permute-done | bytes 1572896 | tf_op jit(solution)/shard_map/ppermute | solution.py:369
  106.2 2.1 fusion.12
  114.1 4.8 maximum_select_fusion.2
  130.0 6.1 maximum_select_fusion
  136.2 3.9 fusion.24
  140.1 3.6 norm_stage.2.refs_0_.normed
  145.4 15.5 %project_stage.1 = (bf16[1024,2048]{1,0:T(8,128)(2,1)}, bf16[1536,2048]{1,0:T(8,128)(2,1)}) custom-call(bf16[1024,1536]{1,0:T(8,128)(2,1)} %copy-done.5, f32[1024,128]{1,0:T(8,128)S(1)} %copy-done.17, f32[1024,128]{1,0:T(8,128)S(1)} %pad.24.refs_2_.refs_9_, f32[1024,128]{1,0:T(8,128)S(1)} %pad.25.refs_3_.refs_10_, ...), custom_call_target="tpu_custom_call" | custom-call | flops 100663296 | bytes 245760 | tf_op jit(solution)/shard_map/project_stage/pallas_call | solution.py:620
  160.8 19.3 %attention_stage.1.attended.refs_4_.refs_5_ = bf16[1024,1024]{1,0:T(8,128)(2,1)S(1)} custom-call(bf16[1024,2048]{1,0:T(8,128)(2,1)} %get-tuple-element.157.refs_0_.refs_1_.refs_2_.refs_3_, bf16[1024,2048]{1,0:T(8,128)(2,1)} %get-tuple-element.157.refs_0_.refs_1_.refs_2_.refs_3_, bf16[1024,2048]{1,0:T(8,128)(2,1)} %get-tuple-element.157.refs_0_.refs_1_.refs_2_.refs_3_), custom_call_target="tpu_custom_call" | custom-call | flops 33554432 | bytes 98304 | tf_op jit(solution)/shard_map/attention_stage/pallas_call | solution.py:692
  180.1 11.5 %collective-permute-done.10.refs_4_.refs_9_.refs_14_.refs_19_ = bf16[384,4096]{1,0:T(8,128)(2,1)} collective-permute-done((bf16[384,4096]{1,0:T(8,128)(2,1)}, bf16[384,4096]{1,0:T(8,128)(2,1)}, u32[]{:S(2)}, u32[]{:S(2)}) %collective-permute-start.10) | collective-permute-done | bytes 3145760 | tf_op jit(solution)/shard_map/ppermute | solution.py:355
  191.8 5.9 fusion.32
  197.7 2.7 slice.396
  200.4 2.8 slice.397
  205.3 3.8 copy.22
  209.1 7.9 %norm_stage.3 = (f32[1024,1536]{1,0:T(8,128)}, bf16[1024,1536]{1,0:T(8,128)(2,1)S(1)}) custom-call(s32[1]{0:T(128)} %bitcast.4.refs_0_, bf16[1024,1536]{1,0:T(8,128)(2,1)} %get-tuple-element.292.refs_1_.refs_6_, f32[1024,1536]{1,0:T(8,128)} %get-tuple-element.393.refs_2_, bf16[1024,1536]{1,0:T(8,128)(2,1)} %collective-permute-done.11.refs_3_, ...), custom_call_target="tpu_custom_call" | custom-call | flops 393216 | bytes 294912 | tf_op jit(solution)/shard_map/norm_stage/pallas_call | solution.py:855
  218.8 21.5 %collective-permute-done.13.refs_6_.refs_11_.refs_16_.refs_21_ = bf16[192,4096]{1,0:T(8,128)(2,1)S(1)} collective-permute-done((bf16[192,4096]{1,0:T(8,128)(2,1)}, bf16[192,4096]{1,0:T(8,128)(2,1)S(1)}, u32[]{:S(2)}, u32[]{:S(2)}) %collective-permute-start.13) | collective-permute-done | bytes 1572896 | tf_op jit(solution)/shard_map/ppermute | solution.py:355
  241.5 16.1 %hidden_stage.2 = (bf16[1024,1024]{1,0:T(8,128)(2,1)S(1)}, bf16[1024,2048]{1,0:T(8,128)(2,1)}) custom-call(bf16[1024,1536]{1,0:T(8,128)(2,1)} %copy-done, bf16[1024,1536]{1,0:T(8,128)(2,1)} %get-tuple-element.293.refs_1_.right.upstream, bf16[384,4096]{1,0:T(8,128)(2,1)} %maximum_select_fusion.1.refs_2_.refs_7_.refs_12_.refs_17_, ...), custom_call_target="tpu_custom_call" | custom-call | flops 150994944 | bytes 344064 | tf_op jit(solution)/shard_map/hidden_stage/pallas_call | solution.py:548
  257.6 11.8 %outer_stage.4 = bf16[1536,2048]{1,0:T(8,128)(2,1)} custom-call(bf16[1024,1536]{1,0:T(8,128)(2,1)S(1)} %copy-done.1, bf16[1024,2048]{1,0:T(8,128)(2,1)} %get-tuple-element.176.right.refs_1_), custom_call_target="tpu_custom_call" | custom-call | flops 100663296 | bytes 114688 | tf_op jit(solution)/shard_map/outer_stage/pallas_call | solution.py:918
  269.4 3.6 fusion.26
  274.1 3.8 copy.23
  277.8 12.2 %back_stage.2.refs_22_ = f32[1024,1536]{1,0:T(8,128)} custom-call(s32[1]{0:T(128)} %bitcast.4.refs_0_, bf16[1024,2048]{1,0:T(8,128)(2,1)} %get-tuple-element.176.right.refs_1_, bf16[384,4096]{1,0:T(8,128)(2,1)} %maximum_select_fusion.1.refs_2_.refs_7_.refs_12_.refs_17_, bf16[384,4096]{1,0:T(8,128)(2,1)} %collective-permute-done.9.refs_3_.refs_8_.refs_13_.refs_18_, ...), custom_call_target="tpu_custom_call" | custom-call | flops 100663296 | bytes 262144 | tf_op jit(solution)/shard_map/back_stage/pallas_call | solution.py:1084
  290.0 6.2 outer_stage.5
  298.0 2.5 add_convert_fusion.9
  306.2 16.1 %hidden_stage.3 = (bf16[1024,1024]{1,0:T(8,128)(2,1)S(1)}, bf16[1024,2048]{1,0:T(8,128)(2,1)}) custom-call(bf16[1024,1536]{1,0:T(8,128)(2,1)} %copy-done, bf16[1024,1536]{1,0:T(8,128)(2,1)} %get-tuple-element.293.refs_1_.right.upstream, bf16[384,4096]{1,0:T(8,128)(2,1)} %maximum_select_fusion.1.refs_2_.refs_7_.refs_12_.refs_17_, ...), custom_call_target="tpu_custom_call" | custom-call | flops 150994944 | bytes 344064 | tf_op jit(solution)/shard_map/hidden_stage/pallas_call | solution.py:548
  322.3 12.0 %outer_stage.6 = bf16[1536,2048]{1,0:T(8,128)(2,1)} custom-call(bf16[1024,1536]{1,0:T(8,128)(2,1)S(1)} %copy-done.2, bf16[1024,2048]{1,0:T(8,128)(2,1)} %get-tuple-element.189.right.refs_1_), custom_call_target="tpu_custom_call" | custom-call | flops 100663296 | bytes 114688 | tf_op jit(solution)/shard_map/outer_stage/pallas_call | solution.py:918
  334.3 13.1 %back_stage.3.grad = f32[1024,1536]{1,0:T(8,128)} custom-call(s32[1]{0:T(128)} %bitcast.4.refs_0_, bf16[1024,2048]{1,0:T(8,128)(2,1)} %get-tuple-element.189.right.refs_1_, bf16[384,4096]{1,0:T(8,128)(2,1)} %maximum_select_fusion.1.refs_2_.refs_7_.refs_12_.refs_17_, bf16[384,4096]{1,0:T(8,128)(2,1)} %collective-permute-done.9.refs_3_.refs_8_.refs_13_.refs_18_, ...), custom_call_target="tpu_custom_call" | custom-call | flops 100663296 | bytes 262144 | tf_op jit(solution)/shard_map/back_stage/pallas_call | solution.py:1084
  347.4 4.8 convert_element_type.244
  352.2 3.5 fusion.25
  357.4 7.1 outer_stage.7
  365.6 3.5 add_convert_fusion.1
  369.2 11.6 %down_stage.1 = f32[1024,1536]{1,0:T(8,128)} custom-call(bf16[1024,1024]{1,0:T(8,128)(2,1)S(1)} %copy-done.10, bf16[1024,1024]{1,0:T(8,128)(2,1)S(1)} %copy-done.12, bf16[1024,1536]{1,0:T(8,128)(2,1)} %bitcast.89, bf16[1024,1536]{1,0:T(8,128)(2,1)} %bitcast.91), custom_call_target="tpu_custom_call" | custom-call | flops 100663296 | bytes 163840 | tf_op jit(solution)/shard_map/down_stage/pallas_call | solution.py:945
  381.6 6.2 collective-permute-done.19
  387.8 3.2 dynamic-slice_convert_fusion.1
  391.1 2.7 add_convert_fusion.8
  393.7 10.9 %norm_back_stage.1 = (f32[1024,1536]{1,0:T(8,128)}, bf16[1024,1536]{1,0:T(8,128)(2,1)S(1)}, f32[8,1536]{1,0:T(8,128)S(1)}) custom-call(f32[1024,1536]{1,0:T(8,128)} %back_stage.3.grad, bf16[1024,1536]{1,0:T(8,128)(2,1)} %collective-permute-done.18.other, f32[1024,1536]{1,0:T(8,128)} %get-tuple-element.207.middle, ...), custom_call_target="tpu_custom_call" | custom-call | flops 393216 | bytes 442368 | tf_op jit(solution)/shard_map/norm_back_stage/pallas_call | solution.py:892
  406.3 11.9 %output_back_stage.1 = (bf16[1024,1024]{1,0:T(8,128)(2,1)S(1)}, bf16[768,1536]{1,0:T(8,128)(2,1)}) custom-call(bf16[1024,1536]{1,0:T(8,128)(2,1)} %copy-done.24, bf16[1024,1024]{1,0:T(8,128)(2,1)S(1)} %copy-done.4, bf16[1024,1536]{1,0:T(8,128)(2,1)} %bitcast.94), custom_call_target="tpu_custom_call" | custom-call | flops 100663296 | bytes 196608 | tf_op jit(solution)/shard_map/output_back_stage/pallas_call | solution.py:987
  418.3 5.1 fusion.8
  423.4 8.1 %collective-permute-done.23 = bf16[192,2048]{1,0:T(8,128)(2,1)} collective-permute-done((bf16[192,2048]{1,0:T(8,128)(2,1)}, bf16[192,2048]{1,0:T(8,128)(2,1)}, u32[]{:S(2)}, u32[]{:S(2)}) %collective-permute-start.23) | collective-permute-done | bytes 786464 | tf_op jit(solution)/shard_map/ppermute | solution.py:359
  431.6 2.5 add_convert_fusion.5
  443.2 31.6 %attention_back_stage.1 = (bf16[1024,512]{1,0:T(8,128)(2,1)S(1)}, bf16[1024,512]{1,0:T(8,128)(2,1)S(1)}, bf16[1024,512]{1,0:T(8,128)(2,1)S(1)}, bf16[1024,512]{1,0:T(8,128)(2,1)S(1)}) custom-call(bf16[1024,2048]{1,0:T(8,128)(2,1)} %get-tuple-element.157.refs_0_.refs_1_.refs_2_.refs_3_, bf16[1024,2048]{1,0:T(8,128)(2,1)} %get-tuple-element.157.refs_0_.refs_1_.refs_2_.refs_3_, ...), custom_call_target="tpu_custom_call" | custom-call | flops 83886080 | bytes 245760 | tf_op jit(solution)/shard_map/attention_back_stage/pallas_call | solution.py:760
  475.7 15.3 %collective-permute-done.25 = bf16[384,2048]{1,0:T(8,128)(2,1)} collective-permute-done((bf16[384,2048]{1,0:T(8,128)(2,1)}, bf16[384,2048]{1,0:T(8,128)(2,1)}, u32[]{:S(2)}, u32[]{:S(2)}) %collective-permute-start.25) | collective-permute-done | bytes 1572896 | tf_op jit(solution)/shard_map/ppermute | solution.py:355
  494.8 3.3 add_convert_fusion
  503.2 12.6 %inputs_back_stage.1 = (f32[1024,1536]{1,0:T(8,128)}, f32[8,1536]{1,0:T(8,128)S(1)}) custom-call(s32[1]{0:T(128)} %bitcast.4.refs_0_, bf16[1024,512]{1,0:T(8,128)(2,1)S(1)} %get-tuple-element.228.refs_1_.refs_0_, bf16[1024,512]{1,0:T(8,128)(2,1)S(1)} %get-tuple-element.229.refs_2_.refs_1_, bf16[1024,512]{1,0:T(8,128)(2,1)S(1)} %get-tuple-element.230.refs_3_.refs_2_, ...), custom_call_target="tpu_custom_call" | custom-call | flops 100663296 | bytes 294912 | tf_op jit(solution)/shard_map/inputs_back_stage/pallas_call | solution.py:805
  516.5 2.4 collective-permute-done.29
  520.1 10.4 %weight_stage.1 = bf16[1600,1536]{1,0:T(8,128)(2,1)} custom-call(bf16[1024,1536]{1,0:T(8,128)(2,1)} %copy-done.5, bf16[1024,512]{1,0:T(8,128)(2,1)S(1)} %get-tuple-element.228.refs_1_.refs_0_, bf16[1024,512]{1,0:T(8,128)(2,1)S(1)} %get-tuple-element.229.refs_2_.refs_1_, bf16[1024,512]{1,0:T(8,128)(2,1)S(1)} %get-tuple-element.230.refs_3_.refs_2_, ...), custom_call_target="tpu_custom_call" | custom-call | flops 75497472 | bytes 172032 | tf_op jit(solution)/shard_map/weight_stage/pallas_call | solution.py:1030
  530.5 3.4 dynamic-slice_convert_fusion
  540.9 2.9 maximum_select_fusion.3
  545.4 8.3 %collective-permute-done.33 = bf16[200,1536]{1,0:T(8,128)(2,1)} collective-permute-done((bf16[200,1536]{1,0:T(8,128)(2,1)}, bf16[200,1536]{1,0:T(8,128)(2,1)}, u32[]{:S(2)}, u32[]{:S(2)}) %collective-permute-start.33) | collective-permute-done | bytes 614432 | tf_op jit(solution)/shard_map/ppermute | solution.py:355
  555.1 52.2 %collective-permute-done.31 = bf16[192,2048]{1,0:T(8,128)(2,1)} collective-permute-done((bf16[192,2048]{1,0:T(8,128)(2,1)S(1)}, bf16[192,2048]{1,0:T(8,128)(2,1)}, u32[]{:S(2)}, u32[]{:S(2)}) %collective-permute-start.31) | collective-permute-done | bytes 786464 | tf_op jit(solution)/shard_map/ppermute | solution.py:359
  614.5 2.6 fusion.2
  617.1 4.6 fusion.5
  621.7 46.1 %collective-permute-done.34 = bf16[192,2048]{1,0:T(8,128)(2,1)S(1)} collective-permute-done((bf16[192,2048]{1,0:T(8,128)(2,1)S(1)}, bf16[192,2048]{1,0:T(8,128)(2,1)S(1)}, u32[]{:S(2)}, u32[]{:S(2)}) %collective-permute-start.34) | collective-permute-done | bytes 786464 | tf_op jit(solution)/shard_map/ppermute | solution.py:359
  670.7 15.6 %collective-permute-done.39 = bf16[200,1536]{1,0:T(8,128)(2,1)S(1)} collective-permute-done((bf16[200,1536]{1,0:T(8,128)(2,1)}, bf16[200,1536]{1,0:T(8,128)(2,1)S(1)}, u32[]{:S(2)}, u32[]{:S(2)}) %collective-permute-start.39) | collective-permute-done | bytes 614432 | tf_op jit(solution)/shard_map/ppermute | solution.py:359
  690.3 24.8 %collective-permute-done.40 = bf16[200,1536]{1,0:T(8,128)(2,1)S(1)} collective-permute-done((bf16[200,1536]{1,0:T(8,128)(2,1)S(1)}, bf16[200,1536]{1,0:T(8,128)(2,1)S(1)}, u32[]{:S(2)}, u32[]{:S(2)}) %collective-permute-start.40) | collective-permute-done | bytes 614432 | tf_op jit(solution)/shard_map/ppermute | solution.py:359
  715.4 2.6 constant_dynamic-slice_fusion.13
  720.2 2.1 slice.458
  722.2 7.9 %merge_ffn.1 = (f32[192,4096]{1,0:T(8,128)}, f32[192,4096]{1,0:T(8,128)}) custom-call(s32[1]{0:T(128)} %bitcast.1.core_ref, bf16[192,2048]{1,0:T(8,128)(2,1)} %get-tuple-element.270.own_0, bf16[192,2048]{1,0:T(8,128)(2,1)} %collective-permute-done.41.other_0, bf16[192,2048]{1,0:T(8,128)(2,1)} %get-tuple-element.272.own_1, ...), custom_call_target="tpu_custom_call" | custom-call | tf_op jit(solution)/shard_map/merge_ffn/pallas_call | solution.py:494
  730.2 18.5 %collective-permute-done.43 = bf16[200,1536]{1,0:T(8,128)(2,1)S(1)} collective-permute-done((bf16[200,1536]{1,0:T(8,128)(2,1)S(1)}, bf16[200,1536]{1,0:T(8,128)(2,1)S(1)}, u32[]{:S(2)}, u32[]{:S(2)}) %collective-permute-start.43) | collective-permute-done | bytes 614432 | tf_op jit(solution)/shard_map/ppermute | solution.py:359
  749.4 7.1 collective-permute-done.37
  756.5 3.8 fusion.9
  (337 shorter events, 122.3 us)
Async XLA Ops:
  7.2 198.1 %all-gather.5.cloned.1.call-start = ((), (), s32[]{:S(2)}) async-start(), calls=%async_computation.7 | async-start | bytes 3932160 | tf_op jit(solution)/shard_map/all_gather | solution.py:1213
  13.4 2.3 collective-permute-start
  17.2 51.4 %collective-permute-start.2 = (bf16[720,1536]{1,0:T(8,128)(2,1)S(1)}, bf16[720,1536]{1,0:T(8,128)(2,1)}, u32[]{:S(2)}, u32[]{:S(2)}) collective-permute-start(bf16[720,1536]{1,0:T(8,128)(2,1)S(1)} %pad_maximum_fusion.2.refs_4_), channel_id=1, source_target_pairs={{0,16},{4,20},{8,24},{12,28},{16,0},{20,4},{24,8},{28,12},{1,17},{... | collective-permute-start | bytes 6635528 | tf_op jit(solution)/shard_map/ppermute | solution.py:355
  20.1 50.0 %collective-permute-start.1 = (bf16[720,1536]{1,0:T(8,128)(2,1)S(1)}, bf16[720,1536]{1,0:T(8,128)(2,1)}, u32[]{:S(2)}, u32[]{:S(2)}) collective-permute-start(bf16[720,1536]{1,0:T(8,128)(2,1)S(1)} %pad_maximum_fusion.2.refs_4_), channel_id=1, source_target_pairs={{0,8},{4,12},{8,0},{12,4},{16,24},{20,28},{24,16},{28,20},{1,9},{5... | collective-permute-start | bytes 6635528 | tf_op jit(solution)/shard_map/ppermute | solution.py:355
  25.9 48.9 %collective-permute-start.5 = (bf16[192,4096]{1,0:T(8,128)(2,1)}, bf16[192,4096]{1,0:T(8,128)(2,1)}, u32[]{:S(2)}, u32[]{:S(2)}) collective-permute-start(bf16[192,4096]{1,0:T(8,128)(2,1)} %get-tuple-element.150), channel_id=1, source_target_pairs={{0,4},{4,0},{8,12},{12,8},{16,20},{20,16},{24,28},{28,24},{1,5},{5... | collective-permute-start | bytes 4718600 | tf_op jit(solution)/shard_map/ppermute | solution.py:355
  29.8 52.2 %collective-permute-start.7 = (bf16[512,1536]{1,0:T(8,128)(2,1)}, bf16[512,1536]{1,0:T(8,128)(2,1)}, u32[]{:S(2)}, u32[]{:S(2)}) collective-permute-start(bf16[512,1536]{1,0:T(8,128)(2,1)} %get-tuple-element.312), channel_id=1, source_target_pairs={{0,5},{1,4},{2,1},{3,0},{4,7},{5,6},{6,3},{7,2},{8,13},{9,12},{10,... | collective-permute-start | bytes 4718600 | tf_op jit(solution)/shard_map/ppermute | solution.py:369
  31.5 70.6 %collective-permute-start.6 = (bf16[512,1536]{1,0:T(8,128)(2,1)}, bf16[512,1536]{1,0:T(8,128)(2,1)}, u32[]{:S(2)}, u32[]{:S(2)}) collective-permute-start(bf16[512,1536]{1,0:T(8,128)(2,1)} %get-tuple-element.313), channel_id=1, source_target_pairs={{0,4},{1,5},{2,0},{3,1},{4,6},{5,7},{6,2},{7,3},{8,12},{9,13},{10,... | collective-permute-start | bytes 4718600 | tf_op jit(solution)/shard_map/ppermute | solution.py:369
  33.6 41.2 %copy-start.46 = (bf16[192,4096]{1,0:T(8,128)(2,1)S(1)}, bf16[192,4096]{1,0:T(8,128)(2,1)}, u32[]{:S(2)}) copy-start(bf16[192,4096]{1,0:T(8,128)(2,1)} %get-tuple-element.151) | copy-start | bytes 4718596
  71.4 30.7 %collective-permute-start.3 = (bf16[352,1536]{1,0:T(8,128)(2,1)S(1)}, bf16[352,1536]{1,0:T(8,128)(2,1)S(1)}, u32[]{:S(2)}, u32[]{:S(2)}) collective-permute-start(bf16[352,1536]{1,0:T(8,128)(2,1)S(1)} %slice.377), channel_id=1, source_target_pairs={{0,8},{4,12},{8,0},{12,4},{16,24},{20,28},{24,16},{28,20},{1,9},{5... | collective-permute-start | bytes 3244040 | tf_op jit(solution)/shard_map/ppermute | solution.py:355
  74.3 28.8 %collective-permute-start.4 = (bf16[368,1536]{1,0:T(8,128)(2,1)S(1)}, bf16[368,1536]{1,0:T(8,128)(2,1)S(1)}, u32[]{:S(2)}, u32[]{:S(2)}) collective-permute-start(bf16[368,1536]{1,0:T(8,128)(2,1)S(1)} %slice.378), channel_id=1, source_target_pairs={{0,16},{4,20},{8,24},{12,28},{16,0},{20,4},{24,8},{28,12},{1,17},{... | collective-permute-start | bytes 3391496 | tf_op jit(solution)/shard_map/ppermute | solution.py:355
  106.0 168.1 %all-gather.7.cloned.1.call-start = ((), (), s32[]{:S(2)}) async-start(), calls=%async_computation.8 | async-start | bytes 3932160 | tf_op jit(solution)/shard_map/all_gather | solution.py:1213
  108.4 35.3 %copy-start.13 = (f32[1024,128]{1,0:T(8,128)}, f32[1024,128]{1,0:T(8,128)S(1)}, u32[]{:S(2)}) copy-start(f32[1024,128]{1,0:T(8,128)S(1)} %pad.25.refs_3_.refs_10_) | copy-start | bytes 1572868
  108.4 35.3 %copy-start.15 = (f32[1024,128]{1,0:T(8,128)}, f32[1024,128]{1,0:T(8,128)S(1)}, u32[]{:S(2)}) copy-start(f32[1024,128]{1,0:T(8,128)S(1)} %pad.24.refs_2_.refs_9_) | copy-start | bytes 1572868
  118.9 11.2 %collective-permute-start.8 = (bf16[2,512,1536]{2,1,0:T(8,128)(2,1)}, bf16[2,512,1536]{2,1,0:T(8,128)(2,1)}, u32[]{:S(2)}, u32[]{:S(2)}) collective-permute-start(bf16[2,512,1536]{2,1,0:T(8,128)(2,1)} %maximum_select_fusion.2), channel_id=1, source_target_pairs={{0,4},{4,0},{8,12},{12,8},{16,20},{20,16},{24,28},{28,24},{1,5},{5... | collective-permute-start | bytes 9437192 | tf_op jit(solution)/shard_map/ppermute | solution.py:355
  120.8 70.8 %collective-permute-start.10 = (bf16[384,4096]{1,0:T(8,128)(2,1)}, bf16[384,4096]{1,0:T(8,128)(2,1)}, u32[]{:S(2)}, u32[]{:S(2)}) collective-permute-start(bf16[384,4096]{1,0:T(8,128)(2,1)} %maximum_select_fusion.1.refs_2_.refs_7_.refs_12_.refs_17_), channel_id=1, source_target_pairs={{0,16},{4,20},{8,24},{12,28},{16,0},{20,4},{24,8},{28,12},{1,17},{... | collective-permute-start | bytes 9437192 | tf_op jit(solution)/shard_map/ppermute | solution.py:355
  121.3 70.5 %collective-permute-start.9 = (bf16[384,4096]{1,0:T(8,128)(2,1)}, bf16[384,4096]{1,0:T(8,128)(2,1)}, u32[]{:S(2)}, u32[]{:S(2)}) collective-permute-start(bf16[384,4096]{1,0:T(8,128)(2,1)} %maximum_select_fusion.1.refs_2_.refs_7_.refs_12_.refs_17_), channel_id=1, source_target_pairs={{0,8},{4,12},{8,0},{12,4},{16,24},{20,28},{24,16},{28,20},{1,9},{5... | collective-permute-start | bytes 9437192 | tf_op jit(solution)/shard_map/ppermute | solution.py:355
  129.0 258.8 %reduce-scatter.4.cloned.1.call-start = ((), (), s32[]{:S(2)}) async-start(), calls=%async_computation.3 | async-start | bytes 3932160 | tf_op jit(solution)/shard_map/reduce_scatter | solution.py:1245
  160.8 31.0 %copy-start.29 = (bf16[8,128,1536]{2,1,0:T(8,128)(2,1)S(1)}, bf16[8,128,1536]{2,1,0:T(8,128)(2,1)}, u32[]{:S(2)}) copy-start(bf16[8,128,1536]{2,1,0:T(8,128)(2,1)} %pad.26) | copy-start | bytes 9437188
  180.1 17.6 %copy-start.3 = (bf16[1024,1024]{1,0:T(8,128)(2,1)}, bf16[1024,1024]{1,0:T(8,128)(2,1)S(1)}, u32[]{:S(2)}) copy-start(bf16[1024,1024]{1,0:T(8,128)(2,1)S(1)} %attention_stage.1.attended.refs_4_.refs_5_) | copy-start | bytes 6291460
  197.7 11.4 %collective-permute-start.11 = (bf16[1024,1536]{1,0:T(8,128)(2,1)}, bf16[1024,1536]{1,0:T(8,128)(2,1)}, u32[]{:S(2)}, u32[]{:S(2)}) collective-permute-start(bf16[1024,1536]{1,0:T(8,128)(2,1)} %get-tuple-element.392), channel_id=1, source_target_pairs={{0,4},{4,0},{8,12},{12,8},{16,20},{20,16},{24,28},{28,24},{1,5},{5... | collective-permute-start | bytes 9437192 | tf_op jit(solution)/shard_map/ppermute | solution.py:355
  203.2 37.0 %collective-permute-start.13 = (bf16[192,4096]{1,0:T(8,128)(2,1)}, bf16[192,4096]{1,0:T(8,128)(2,1)S(1)}, u32[]{:S(2)}, u32[]{:S(2)}) collective-permute-start(bf16[192,4096]{1,0:T(8,128)(2,1)} %slice.397), channel_id=1, source_target_pairs={{0,16},{4,20},{8,24},{12,28},{16,0},{20,4},{24,8},{28,12},{1,17},{... | collective-permute-start | bytes 4718600 | tf_op jit(solution)/shard_map/ppermute | solution.py:355
  204.8 36.7 %collective-permute-start.12 = (bf16[192,4096]{1,0:T(8,128)(2,1)}, bf16[192,4096]{1,0:T(8,128)(2,1)S(1)}, u32[]{:S(2)}, u32[]{:S(2)}) collective-permute-start(bf16[192,4096]{1,0:T(8,128)(2,1)} %slice.396), channel_id=1, source_target_pairs={{0,8},{4,12},{8,0},{12,4},{16,24},{20,28},{24,16},{28,20},{1,9},{5... | collective-permute-start | bytes 4718600 | tf_op jit(solution)/shard_map/ppermute | solution.py:355
  273.0 24.9 %collective-permute-start.15 = (bf16[192,2048]{1,0:T(8,128)(2,1)}, bf16[192,2048]{1,0:T(8,128)(2,1)}, u32[]{:S(2)}, u32[]{:S(2)}) collective-permute-start(bf16[192,2048]{1,0:T(8,128)(2,1)} %get-tuple-element.304), channel_id=1, source_target_pairs={{0,16},{4,20},{8,24},{12,28},{16,0},{20,4},{24,8},{28,12},{1,17},{... | collective-permute-start | bytes 2359304 | tf_op jit(solution)/shard_map/ppermute | solution.py:355
  273.5 24.4 %collective-permute-start.14 = (bf16[192,2048]{1,0:T(8,128)(2,1)}, bf16[192,2048]{1,0:T(8,128)(2,1)}, u32[]{:S(2)}, u32[]{:S(2)}) collective-permute-start(bf16[192,2048]{1,0:T(8,128)(2,1)} %get-tuple-element.305), channel_id=1, source_target_pairs={{0,8},{4,12},{8,0},{12,4},{16,24},{20,28},{24,16},{28,20},{1,9},{5... | collective-permute-start | bytes 2359304 | tf_op jit(solution)/shard_map/ppermute | solution.py:355
  297.9 196.8 %reduce-scatter.6.cloned.1.call-start = ((), (), s32[]{:S(2)}) async-start(), calls=%async_computation.4 | async-start | bytes 3932160 | tf_op jit(solution)/shard_map/reduce_scatter | solution.py:1245
  301.9 62.6 %collective-permute-start.16 = (bf16[384,2048]{1,0:T(8,128)(2,1)}, bf16[384,2048]{1,0:T(8,128)(2,1)}, u32[]{:S(2)}, u32[]{:S(2)}) collective-permute-start(bf16[384,2048]{1,0:T(8,128)(2,1)} %pad_maximum_fusion.4), channel_id=1, source_target_pairs={{0,8},{4,12},{8,0},{12,4},{16,24},{20,28},{24,16},{28,20},{1,9},{5... | collective-permute-start | bytes 4718600 | tf_op jit(solution)/shard_map/ppermute | solution.py:355
  304.6 17.6 %copy-start.2 = (bf16[1024,1536]{1,0:T(8,128)(2,1)S(1)}, bf16[1024,1536]{1,0:T(8,128)(2,1)}, u32[]{:S(2)}) copy-start(bf16[1024,1536]{1,0:T(8,128)(2,1)} %copy-done) | copy-start | bytes 9437188
  304.6 60.9 %collective-permute-start.17 = (bf16[384,2048]{1,0:T(8,128)(2,1)}, bf16[384,2048]{1,0:T(8,128)(2,1)}, u32[]{:S(2)}, u32[]{:S(2)}) collective-permute-start(bf16[384,2048]{1,0:T(8,128)(2,1)} %pad_maximum_fusion.5), channel_id=1, source_target_pairs={{0,16},{4,20},{8,24},{12,28},{16,0},{20,4},{24,8},{28,12},{1,17},{... | collective-permute-start | bytes 4718600 | tf_op jit(solution)/shard_map/ppermute | solution.py:355
  352.2 35.6 %collective-permute-start.18 = (bf16[1024,1536]{1,0:T(8,128)(2,1)}, bf16[1024,1536]{1,0:T(8,128)(2,1)}, u32[]{:S(2)}, u32[]{:S(2)}) collective-permute-start(bf16[1024,1536]{1,0:T(8,128)(2,1)} %convert_element_type.244), channel_id=1, source_target_pairs={{0,4},{4,0},{8,12},{12,8},{16,20},{20,16},{24,28},{28,24},{1,5},{5... | collective-permute-start | bytes 9437192 | tf_op jit(solution)/shard_map/ppermute | solution.py:355
  355.7 25.8 %collective-permute-start.21 = (bf16[192,2048]{1,0:T(8,128)(2,1)}, bf16[192,2048]{1,0:T(8,128)(2,1)}, u32[]{:S(2)}, u32[]{:S(2)}) collective-permute-start(bf16[192,2048]{1,0:T(8,128)(2,1)} %get-tuple-element.298), channel_id=1, source_target_pairs={{0,16},{4,20},{8,24},{12,28},{16,0},{20,4},{24,8},{28,12},{1,17},{... | collective-permute-start | bytes 2359304 | tf_op jit(solution)/shard_map/ppermute | solution.py:355
  356.3 25.3 %collective-permute-start.20 = (bf16[192,2048]{1,0:T(8,128)(2,1)}, bf16[192,2048]{1,0:T(8,128)(2,1)}, u32[]{:S(2)}, u32[]{:S(2)}) collective-permute-start(bf16[192,2048]{1,0:T(8,128)(2,1)} %get-tuple-element.299), channel_id=1, source_target_pairs={{0,8},{4,12},{8,0},{12,4},{16,24},{20,28},{24,16},{28,20},{1,9},{5... | collective-permute-start | bytes 2359304 | tf_op jit(solution)/shard_map/ppermute | solution.py:355
  369.1 18.6 %collective-permute-start.19 = (bf16[192,2048]{1,0:T(8,128)(2,1)S(1)}, bf16[192,2048]{1,0:T(8,128)(2,1)}, u32[]{:S(2)}, u32[]{:S(2)}) collective-permute-start(bf16[192,2048]{1,0:T(8,128)(2,1)S(1)} %constant_dynamic-slice_fusion.21), channel_id=1, source_target_pairs={{0,1},{1,0},{2,3},{3,2},{4,5},{5,4},{6,7},{7,6},{8,9},{9,8},{10,11... | collective-permute-start | bytes 2359304 | tf_op jit(solution)/shard_map/ppermute | solution.py:359
  387.8 128.7 %reduce-scatter.8.cloned.1.call-start = ((), (), s32[]{:S(2)}) async-start(), calls=%async_computation.5 | async-start | bytes 2949120 | tf_op jit(solution)/shard_map/reduce_scatter | solution.py:1245
  391.1 15.2 %collective-permute-start.22 = (bf16[512,1536]{1,0:T(8,128)(2,1)}, bf16[512,1536]{1,0:T(8,128)(2,1)}, u32[]{:S(2)}, u32[]{:S(2)}) collective-permute-start(bf16[512,1536]{1,0:T(8,128)(2,1)} %dynamic-slice_convert_fusion.1), channel_id=1, source_target_pairs={{0,4},{4,0},{8,12},{12,8},{16,20},{20,16},{24,28},{28,24},{1,5},{5... | collective-permute-start | bytes 4718600 | tf_op jit(solution)/shard_map/ppermute | solution.py:355
  391.1 27.2 %slice-start = ((s8[6291456]{0:T(1024)(128)(4,1)}), s8[2097152]{0:T(1024)(128)(4,1)S(1)}, s32[]{:S(2)}) async-start(s8[6291456]{0:T(1024)(128)(4,1)} %bitcast.92), calls=%async_computation.9 | async-start | bytes 4194304
  393.7 37.7 %collective-permute-start.23 = (bf16[192,2048]{1,0:T(8,128)(2,1)}, bf16[192,2048]{1,0:T(8,128)(2,1)}, u32[]{:S(2)}, u32[]{:S(2)}) collective-permute-start(bf16[192,2048]{1,0:T(8,128)(2,1)} %add_convert_fusion.8), channel_id=1, source_target_pairs={{0,2},{1,3},{2,0},{3,1},{4,6},{5,7},{6,4},{7,5},{8,10},{9,11},{10,... | collective-permute-start | bytes 2359304 | tf_op jit(solution)/shard_map/ppermute | solution.py:359
  393.7 24.5 %slice-start.1 = ((s8[6291456]{0:T(1024)(128)(4,1)}), s8[4194304]{0:T(1024)(128)(4,1)S(1)}, s32[]{:S(2)}) async-start(s8[6291456]{0:T(1024)(128)(4,1)} %bitcast.92), calls=%async_computation.10 | async-start | bytes 8388608
  431.5 239.2 %all-reduce.8.cloned.1.call-start = ((), (), s32[]{:S(2)}) async-start(), calls=%async_computation.6 | async-start | bytes 4325376 | tf_op jit(solution)/shard_map/psum | solution.py:1318
  435.4 55.6 %collective-permute-start.25 = (bf16[384,2048]{1,0:T(8,128)(2,1)}, bf16[384,2048]{1,0:T(8,128)(2,1)}, u32[]{:S(2)}, u32[]{:S(2)}) collective-permute-start(bf16[384,2048]{1,0:T(8,128)(2,1)} %pad_maximum_fusion.6), channel_id=1, source_target_pairs={{0,8},{4,12},{8,0},{12,4},{16,24},{20,28},{24,16},{28,20},{1,9},{5... | collective-permute-start | bytes 4718600 | tf_op jit(solution)/shard_map/ppermute | solution.py:355
  437.6 55.4 %collective-permute-start.26 = (bf16[384,2048]{1,0:T(8,128)(2,1)}, bf16[384,2048]{1,0:T(8,128)(2,1)}, u32[]{:S(2)}, u32[]{:S(2)}) collective-permute-start(bf16[384,2048]{1,0:T(8,128)(2,1)} %pad_maximum_fusion.7), channel_id=1, source_target_pairs={{0,16},{4,20},{8,24},{12,28},{16,0},{20,4},{24,8},{28,12},{1,17},{... | collective-permute-start | bytes 4718600 | tf_op jit(solution)/shard_map/ppermute | solution.py:355
  441.1 33.7 %copy-start.40 = (bf16[192,2048]{1,0:T(8,128)(2,1)}, bf16[192,2048]{1,0:T(8,128)(2,1)S(1)}, u32[]{:S(2)}) copy-start(bf16[192,2048]{1,0:T(8,128)(2,1)S(1)} %add_convert_fusion.7) | copy-start | bytes 2359300
  441.1 51.9 %collective-permute-start.24 = (bf16[192,2048]{1,0:T(8,128)(2,1)S(1)}, bf16[192,2048]{1,0:T(8,128)(2,1)S(1)}, u32[]{:S(2)}, u32[]{:S(2)}) collective-permute-start(bf16[192,2048]{1,0:T(8,128)(2,1)S(1)} %add_convert_fusion.7), channel_id=1, source_target_pairs={{0,1},{1,0},{2,3},{3,2},{4,5},{5,4},{6,7},{7,6},{8,9},{9,8},{10,11... | collective-permute-start | bytes 2359304 | tf_op jit(solution)/shard_map/ppermute | solution.py:359
  441.3 51.7 %collective-permute-start.28 = (bf16[256,1536]{1,0:T(8,128)(2,1)S(1)}, bf16[256,1536]{1,0:T(8,128)(2,1)S(1)}, u32[]{:S(2)}, u32[]{:S(2)}) collective-permute-start(bf16[256,1536]{1,0:T(8,128)(2,1)S(1)} %get-tuple-element.344), channel_id=1, source_target_pairs={{5,0},{4,1},{1,2},{0,3},{7,4},{6,5},{3,6},{2,7},{13,8},{12,9},{9,1... | collective-permute-start | bytes 2359304 | tf_op jit(solution)/shard_map/ppermute | solution.py:369
  442.6 52.2 %collective-permute-start.27 = (bf16[256,1536]{1,0:T(8,128)(2,1)S(1)}, bf16[256,1536]{1,0:T(8,128)(2,1)}, u32[]{:S(2)}, u32[]{:S(2)}) collective-permute-start(bf16[256,1536]{1,0:T(8,128)(2,1)S(1)} %get-tuple-element.345), channel_id=1, source_target_pairs={{4,0},{5,1},{0,2},{1,3},{6,4},{7,5},{2,6},{3,7},{12,8},{13,9},{8,1... | collective-permute-start | bytes 2359304 | tf_op jit(solution)/shard_map/ppermute | solution.py:369
  500.2 18.7 %collective-permute-start.29 = (bf16[192,2048]{1,0:T(8,128)(2,1)}, bf16[192,2048]{1,0:T(8,128)(2,1)}, u32[]{:S(2)}, u32[]{:S(2)}) collective-permute-start(bf16[192,2048]{1,0:T(8,128)(2,1)} %constant_dynamic-slice_fusion.14), channel_id=1, source_target_pairs={{0,1},{1,0},{2,3},{3,2},{4,5},{5,4},{6,7},{7,6},{8,9},{9,8},{10,11... | collective-permute-start | bytes 2359304 | tf_op jit(solution)/shard_map/ppermute | solution.py:359
  533.8 73.5 %collective-permute-start.30 = (bf16[512,1536]{1,0:T(8,128)(2,1)}, bf16[512,1536]{1,0:T(8,128)(2,1)}, u32[]{:S(2)}, u32[]{:S(2)}) collective-permute-start(bf16[512,1536]{1,0:T(8,128)(2,1)} %dynamic-slice_convert_fusion), channel_id=1, source_target_pairs={{0,4},{4,0},{8,12},{12,8},{16,20},{20,16},{24,28},{28,24},{1,5},{5... | collective-permute-start | bytes 4718600 | tf_op jit(solution)/shard_map/ppermute | solution.py:355
  535.3 72.1 %collective-permute-start.31 = (bf16[192,2048]{1,0:T(8,128)(2,1)S(1)}, bf16[192,2048]{1,0:T(8,128)(2,1)}, u32[]{:S(2)}, u32[]{:S(2)}) collective-permute-start(bf16[192,2048]{1,0:T(8,128)(2,1)S(1)} %add_convert_fusion.4), channel_id=1, source_target_pairs={{0,2},{1,3},{2,0},{3,1},{4,6},{5,7},{6,4},{7,5},{8,10},{9,11},{10,... | collective-permute-start | bytes 2359304 | tf_op jit(solution)/shard_map/ppermute | solution.py:359
  537.3 16.3 %collective-permute-start.33 = (bf16[200,1536]{1,0:T(8,128)(2,1)}, bf16[200,1536]{1,0:T(8,128)(2,1)}, u32[]{:S(2)}, u32[]{:S(2)}) collective-permute-start(bf16[200,1536]{1,0:T(8,128)(2,1)} %get-tuple-element.310), channel_id=1, source_target_pairs={{0,16},{4,20},{8,24},{12,28},{16,0},{20,4},{24,8},{28,12},{1,17},{... | collective-permute-start | bytes 1843208 | tf_op jit(solution)/shard_map/ppermute | solution.py:355
  538.8 16.3 %collective-permute-start.32 = (bf16[200,1536]{1,0:T(8,128)(2,1)}, bf16[200,1536]{1,0:T(8,128)(2,1)}, u32[]{:S(2)}, u32[]{:S(2)}) collective-permute-start(bf16[200,1536]{1,0:T(8,128)(2,1)} %get-tuple-element.311), channel_id=1, source_target_pairs={{0,8},{4,12},{8,0},{12,4},{16,24},{20,28},{24,16},{28,20},{1,9},{5... | collective-permute-start | bytes 1843208 | tf_op jit(solution)/shard_map/ppermute | solution.py:355
  543.9 70.6 %slice-start.2 = ((s8[6291456]{0:T(1024)(128)(4,1)}), s8[2097152]{0:T(1024)(128)(4,1)S(1)}, s32[]{:S(2)}) async-start(s8[6291456]{0:T(1024)(128)(4,1)} %bitcast.96), calls=%async_computation.11 | async-start | bytes 4194304
  545.4 69.1 %slice-start.3 = ((s8[6291456]{0:T(1024)(128)(4,1)}), s8[4194304]{0:T(1024)(128)(4,1)S(1)}, s32[]{:S(2)}) async-start(s8[6291456]{0:T(1024)(128)(4,1)} %bitcast.96), calls=%async_computation.12 | async-start | bytes 8388608
  610.4 57.3 %collective-permute-start.35 = (bf16[400,1536]{1,0:T(8,128)(2,1)S(1)}, bf16[400,1536]{1,0:T(8,128)(2,1)S(1)}, u32[]{:S(2)}, u32[]{:S(2)}) collective-permute-start(bf16[400,1536]{1,0:T(8,128)(2,1)S(1)} %pad_maximum_fusion.8), channel_id=1, source_target_pairs={{0,8},{4,12},{8,0},{12,4},{16,24},{20,28},{24,16},{28,20},{1,9},{5... | collective-permute-start | bytes 3686408 | tf_op jit(solution)/shard_map/ppermute | solution.py:355
  611.8 55.9 %collective-permute-start.36 = (bf16[400,1536]{1,0:T(8,128)(2,1)S(1)}, bf16[400,1536]{1,0:T(8,128)(2,1)S(1)}, u32[]{:S(2)}, u32[]{:S(2)}) collective-permute-start(bf16[400,1536]{1,0:T(8,128)(2,1)S(1)} %pad_maximum_fusion.9), channel_id=1, source_target_pairs={{0,16},{4,20},{8,24},{12,28},{16,0},{20,4},{24,8},{28,12},{1,17},{... | collective-permute-start | bytes 3686408 | tf_op jit(solution)/shard_map/ppermute | solution.py:355
  614.4 53.4 %collective-permute-start.34 = (bf16[192,2048]{1,0:T(8,128)(2,1)S(1)}, bf16[192,2048]{1,0:T(8,128)(2,1)S(1)}, u32[]{:S(2)}, u32[]{:S(2)}) collective-permute-start(bf16[192,2048]{1,0:T(8,128)(2,1)S(1)} %add_convert_fusion.3), channel_id=1, source_target_pairs={{0,1},{1,0},{2,3},{3,2},{4,5},{5,4},{6,7},{7,6},{8,9},{9,8},{10,11... | collective-permute-start | bytes 2359304 | tf_op jit(solution)/shard_map/ppermute | solution.py:359
  670.7 15.6 %collective-permute-start.39 = (bf16[200,1536]{1,0:T(8,128)(2,1)}, bf16[200,1536]{1,0:T(8,128)(2,1)S(1)}, u32[]{:S(2)}, u32[]{:S(2)}) collective-permute-start(bf16[200,1536]{1,0:T(8,128)(2,1)} %constant_dynamic-slice_fusion.11), channel_id=1, source_target_pairs={{0,1},{1,0},{2,3},{3,2},{4,5},{5,4},{6,7},{7,6},{8,9},{9,8},{10,11... | collective-permute-start | bytes 1843208 | tf_op jit(solution)/shard_map/ppermute | solution.py:359
  670.7 17.1 %copy-start.57 = (bf16[192,2048]{1,0:T(8,128)(2,1)S(1)}, bf16[192,2048]{1,0:T(8,128)(2,1)}, u32[]{:S(2)}) copy-start(bf16[192,2048]{1,0:T(8,128)(2,1)} %copy-done.56) | copy-start | bytes 2359300
  686.5 28.7 %collective-permute-start.40 = (bf16[200,1536]{1,0:T(8,128)(2,1)S(1)}, bf16[200,1536]{1,0:T(8,128)(2,1)S(1)}, u32[]{:S(2)}, u32[]{:S(2)}) collective-permute-start(bf16[200,1536]{1,0:T(8,128)(2,1)S(1)} %add_convert_fusion.12), channel_id=1, source_target_pairs={{0,2},{1,3},{2,0},{3,1},{4,6},{5,7},{6,4},{7,5},{8,10},{9,11},{10,... | collective-permute-start | bytes 1843208 | tf_op jit(solution)/shard_map/ppermute | solution.py:359
  687.8 34.4 %collective-permute-start.41 = (bf16[192,2048]{1,0:T(8,128)(2,1)}, bf16[192,2048]{1,0:T(8,128)(2,1)}, u32[]{:S(2)}, u32[]{:S(2)}) collective-permute-start(bf16[192,2048]{1,0:T(8,128)(2,1)} %get-tuple-element.340), channel_id=1, source_target_pairs={{0,4},{4,0},{8,12},{12,8},{16,20},{20,16},{24,28},{28,24},{1,5},{5... | collective-permute-start | bytes 2359304 | tf_op jit(solution)/shard_map/ppermute | solution.py:355
  689.8 29.2 %copy-start.30 = (bf16[704,1536]{1,0:T(8,128)(2,1)S(1)}, bf16[704,1536]{1,0:T(8,128)(2,1)}, u32[]{:S(2)}) copy-start(bf16[704,1536]{1,0:T(8,128)(2,1)} %all-reduce.8.cloned.1.call-done) | copy-start | bytes 6488068
  689.8 32.4 %collective-permute-start.42 = (bf16[192,2048]{1,0:T(8,128)(2,1)}, bf16[192,2048]{1,0:T(8,128)(2,1)}, u32[]{:S(2)}, u32[]{:S(2)}) collective-permute-start(bf16[192,2048]{1,0:T(8,128)(2,1)} %get-tuple-element.338), channel_id=1, source_target_pairs={{0,4},{4,0},{8,12},{12,8},{16,20},{20,16},{24,28},{28,24},{1,5},{5... | collective-permute-start | bytes 2359304 | tf_op jit(solution)/shard_map/ppermute | solution.py:355
  715.3 33.3 %collective-permute-start.43 = (bf16[200,1536]{1,0:T(8,128)(2,1)S(1)}, bf16[200,1536]{1,0:T(8,128)(2,1)S(1)}, u32[]{:S(2)}, u32[]{:S(2)}) collective-permute-start(bf16[200,1536]{1,0:T(8,128)(2,1)S(1)} %add_convert_fusion.11), channel_id=1, source_target_pairs={{0,1},{1,0},{2,3},{3,2},{4,5},{5,4},{6,7},{7,6},{8,9},{9,8},{10,11... | collective-permute-start | bytes 1843208 | tf_op jit(solution)/shard_map/ppermute | solution.py:359
  718.0 38.4 %collective-permute-start.37 = (bf16[256,1536]{1,0:T(8,128)(2,1)}, bf16[256,1536]{1,0:T(8,128)(2,1)}, u32[]{:S(2)}, u32[]{:S(2)}) collective-permute-start(bf16[256,1536]{1,0:T(8,128)(2,1)} %get-tuple-element.342), channel_id=1, source_target_pairs={{5,0},{4,1},{1,2},{0,3},{7,4},{6,5},{3,6},{2,7},{13,8},{12,9},{9,1... | collective-permute-start | bytes 2359304 | tf_op jit(solution)/shard_map/ppermute | solution.py:369
  719.0 37.5 %collective-permute-start.38 = (bf16[256,1536]{1,0:T(8,128)(2,1)}, bf16[256,1536]{1,0:T(8,128)(2,1)}, u32[]{:S(2)}, u32[]{:S(2)}) collective-permute-start(bf16[256,1536]{1,0:T(8,128)(2,1)} %get-tuple-element.343), channel_id=1, source_target_pairs={{4,0},{5,1},{0,2},{1,3},{6,4},{7,5},{2,6},{3,7},{12,8},{13,9},{8,1... | collective-permute-start | bytes 2359304 | tf_op jit(solution)/shard_map/ppermute | solution.py:369
  749.3 11.0 %collective-permute-start.44 = (bf16[200,1536]{1,0:T(8,128)(2,1)S(1)}, bf16[200,1536]{1,0:T(8,128)(2,1)S(1)}, u32[]{:S(2)}, u32[]{:S(2)}) collective-permute-start(bf16[200,1536]{1,0:T(8,128)(2,1)S(1)} %pad_maximum_fusion.15), channel_id=1, source_target_pairs={{0,4},{4,0},{8,12},{12,8},{16,20},{20,16},{24,28},{28,24},{1,5},{5... | collective-permute-start | bytes 1843208 | tf_op jit(solution)/shard_map/ppermute | solution.py:355
  (52 other events, 245.5 us)
Sparse Core Ops, SparseCore 0:
  106.1 60.8 all-gather.4
  168.5 62.0 all-gather.6
  298.0 68.2 reduce-scatter.3
  387.9 42.3 reduce-scatter.5
  433.2 56.5 reduce-scatter.7
  545.5 122.6 all-reduce.7

commit v3 on v2

--- a/solution.py
+++ b/solution.py
@@ -1186,10 +1186,9 @@
     ffn_block = pick_order(core == 1, ffn_mine, ffn_other)
     token, attn_x, attn_y = chain(token, attn_x, attn_y)
     corner_x, corner_y = flip(attn_y[:cut], 2), flip(attn_x[cut:], 4)
-    token, corner_x, corner_y, ffn_block, *both_parts = chain(
-        token, corner_x, corner_y, ffn_block, *both_parts
-    )
+    token, corner_x, corner_y, ffn_block = chain(token, corner_x, corner_y, ffn_block)
     ffn_sides = (flip(ffn_block, 2), flip(ffn_block, 4))
+    token, *both_parts = chain(token, *both_parts)
     halves = [p.reshape(2, local_length, width) for p in both_parts]
     here = pick_order(low == 1, *halves, axis=1)
     there = flip(here, 1)

time: 780 us -> 774 us (level)
  waiting for transfers between devices: 300 us -> 273 us
  starting transfers between devices: 31.2 us -> 52.6 us
    ppermute x9, waiting for transfers between devices: 174 us -> 152 us  [cross(): return lax.ppermute(field, 'seq', [(i, i ^ bit) for i in range(4)])]
    ppermute x6, waiting for transfers between devices: 27.2 us -> 5.95 us  [column_swap(): return lax.ppermute(field, ('dp', 'seq'), pairs)]
    ppermute x9, starting transfers between devices: 1.14 us -> 19 us  [cross(): return lax.ppermute(field, 'seq', [(i, i ^ bit) for i in range(4)])]
    ppermute x30, waiting for transfers between devices: 99.2 us -> 114 us  [flip(): return lax.ppermute(field, 'dp', [(i, i ^ bit) for i in range(count)])]
  transfers between devices with their start and end apart: 51 -> 51, of which waited for: 23 -> 24; matrix products, arithmetic and copies ran while one was open for 19% -> 20% of each run, Pallas kernels for 30% -> 30%
where the time goes in v3:
time: 774 us; the launch traced here: 766 us
  waiting for transfers between devices  273 us (35%)
  Pallas kernels  241 us (31%)
  local copies, waits for them, and re-layouts  91 us (12%)
  other arithmetic  86.6 us (11%)
  starting transfers between devices  52.6 us (7%)
  between operations  15.5 us (2%)
    ppermute x9, waiting for transfers between devices, cross(): return lax.ppermute(field, 'seq', [(i, i ^ bit) for i in range(4)])  152 us
    ppermute x30, waiting for transfers between devices, flip(): return lax.ppermute(field, 'dp', [(i, i ^ bit) for i in range(count)])  114 us
    pallas_call x4, Pallas kernels, outer_stage(): pl.pallas_call(outer_kernel, out_shape=jax.ShapeDtypeStruct((rows, column...  36.9 us
    pallas_call x2, Pallas kernels, hidden_stage(): pl.pallas_call(lambda *refs: hidden_kernel(width // 4, *refs), out_shape=...  32.1 us
    pallas_call x1, Pallas kernels, attention_back_stage(): pl.pallas_call(lambda *refs: attention_back_kernel(tile, *refs), out_shap...  31.6 us
    pallas_call x2, Pallas kernels, back_stage(): pl.pallas_call(lambda *refs: back_kernel(width // 4, base is not None, *r...  25.3 us
    convert_element_type x12, other arithmetic, add_half(): return total.astype(jnp.bfloat16)  23.4 us
    ppermute x30, starting transfers between devices, flip(): return lax.ppermute(field, 'dp', [(i, i ^ bit) for i in range(count)])  22.5 us
  transfers between devices with their start and end apart: 51, of which 24 were waited for; matrix products, arithmetic and copies ran while one was open for 20% of the time, Pallas kernels for 30%

profile of v3, /device:TPU:0, one launch (start us, length us, event | category | flops | bytes accessed | tf_op | source)
XLA Modules:
  0.0 766.1 jit_solution(3602524023546426231)
XLA Ops:
  17.2 2.9 collective-permute-start.2
  21.6 4.3 prepare_ffn.1
  35.0 33.6 %collective-permute-done.2.refs_6_ = bf16[720,1536]{1,0:T(8,128)(2,1)} collective-permute-done((bf16[720,1536]{1,0:T(8,128)(2,1)S(1)}, bf16[720,1536]{1,0:T(8,128)(2,1)}, u32[]{:S(2)}, u32[]{:S(2)}) %collective-permute-start.2) | collective-permute-done | bytes 2211872 | tf_op jit(solution)/shard_map/ppermute | solution.py:355
  74.8 3.7 maximum_select_fusion.1.refs_2_.refs_7_.refs_12_.refs_17_
  82.0 14.2 %collective-permute-done.3.refs_7_ = bf16[352,1536]{1,0:T(8,128)(2,1)S(1)} collective-permute-done((bf16[352,1536]{1,0:T(8,128)(2,1)S(1)}, bf16[352,1536]{1,0:T(8,128)(2,1)S(1)}, u32[]{:S(2)}, u32[]{:S(2)}) %collective-permute-start.3) | collective-permute-done | bytes 1081376 | tf_op jit(solution)/shard_map/ppermute | solution.py:355
  97.2 2.7 collective-permute-done.4.refs_8_
  110.8 4.8 maximum_select_fusion.2
  126.9 6.1 maximum_select_fusion
  133.0 3.9 fusion.24
  136.9 3.6 norm_stage.2.refs_0_.normed
  142.2 15.5 %project_stage.1 = (bf16[1024,2048]{1,0:T(8,128)(2,1)}, bf16[1536,2048]{1,0:T(8,128)(2,1)}) custom-call(bf16[1024,1536]{1,0:T(8,128)(2,1)} %copy-done.5, f32[1024,128]{1,0:T(8,128)S(1)} %copy-done.17, f32[1024,128]{1,0:T(8,128)S(1)} %pad.24.refs_2_.refs_9_, f32[1024,128]{1,0:T(8,128)S(1)} %pad.25.refs_3_.refs_10_, ...), custom_call_target="tpu_custom_call" | custom-call | flops 100663296 | bytes 245760 | tf_op jit(solution)/shard_map/project_stage/pallas_call | solution.py:620
  157.6 19.3 %attention_stage.1.attended.refs_4_.refs_5_ = bf16[1024,1024]{1,0:T(8,128)(2,1)S(1)} custom-call(bf16[1024,2048]{1,0:T(8,128)(2,1)} %get-tuple-element.159.refs_0_.refs_1_.refs_2_.refs_3_, bf16[1024,2048]{1,0:T(8,128)(2,1)} %get-tuple-element.159.refs_0_.refs_1_.refs_2_.refs_3_, bf16[1024,2048]{1,0:T(8,128)(2,1)} %get-tuple-element.159.refs_0_.refs_1_.refs_2_.refs_3_), custom_call_target="tpu_custom_call" | custom-call | flops 33554432 | bytes 98304 | tf_op jit(solution)/shard_map/attention_stage/pallas_call | solution.py:692
  176.9 11.5 %collective-permute-done.10.refs_4_.refs_9_.refs_14_.refs_19_ = bf16[384,4096]{1,0:T(8,128)(2,1)} collective-permute-done((bf16[384,4096]{1,0:T(8,128)(2,1)}, bf16[384,4096]{1,0:T(8,128)(2,1)}, u32[]{:S(2)}, u32[]{:S(2)}) %collective-permute-start.10) | collective-permute-done | bytes 3145760 | tf_op jit(solution)/shard_map/ppermute | solution.py:355
  188.7 5.9 fusion.32
  194.6 2.7 slice.396
  197.3 2.8 slice.397
  202.0 3.8 copy.22
  205.8 7.9 %norm_stage.3 = (f32[1024,1536]{1,0:T(8,128)}, bf16[1024,1536]{1,0:T(8,128)(2,1)S(1)}) custom-call(s32[1]{0:T(128)} %bitcast.4.refs_0_, bf16[1024,1536]{1,0:T(8,128)(2,1)} %get-tuple-element.294.refs_1_.refs_6_, f32[1024,1536]{1,0:T(8,128)} %get-tuple-element.395.refs_2_, bf16[1024,1536]{1,0:T(8,128)(2,1)} %collective-permute-done.11.refs_3_, ...), custom_call_target="tpu_custom_call" | custom-call | flops 393216 | bytes 294912 | tf_op jit(solution)/shard_map/norm_stage/pallas_call | solution.py:855
  215.5 21.6 %collective-permute-done.13.refs_6_.refs_11_.refs_16_.refs_21_ = bf16[192,4096]{1,0:T(8,128)(2,1)S(1)} collective-permute-done((bf16[192,4096]{1,0:T(8,128)(2,1)}, bf16[192,4096]{1,0:T(8,128)(2,1)S(1)}, u32[]{:S(2)}, u32[]{:S(2)}) %collective-permute-start.13) | collective-permute-done | bytes 1572896 | tf_op jit(solution)/shard_map/ppermute | solution.py:355
  238.3 16.1 %hidden_stage.2 = (bf16[1024,1024]{1,0:T(8,128)(2,1)S(1)}, bf16[1024,2048]{1,0:T(8,128)(2,1)}) custom-call(bf16[1024,1536]{1,0:T(8,128)(2,1)} %copy-done, bf16[1024,1536]{1,0:T(8,128)(2,1)} %get-tuple-element.295.refs_1_.right.upstream, bf16[384,4096]{1,0:T(8,128)(2,1)} %maximum_select_fusion.1.refs_2_.refs_7_.refs_12_.refs_17_, ...), custom_call_target="tpu_custom_call" | custom-call | flops 150994944 | bytes 344064 | tf_op jit(solution)/shard_map/hidden_stage/pallas_call | solution.py:548
  254.3 11.8 %outer_stage.4 = bf16[1536,2048]{1,0:T(8,128)(2,1)} custom-call(bf16[1024,1536]{1,0:T(8,128)(2,1)S(1)} %copy-done.1, bf16[1024,2048]{1,0:T(8,128)(2,1)} %get-tuple-element.178.right.refs_1_), custom_call_target="tpu_custom_call" | custom-call | flops 100663296 | bytes 114688 | tf_op jit(solution)/shard_map/outer_stage/pallas_call | solution.py:918
  266.2 3.6 fusion.26
  270.9 3.8 copy.23
  274.7 12.2 %back_stage.2.refs_22_ = f32[1024,1536]{1,0:T(8,128)} custom-call(s32[1]{0:T(128)} %bitcast.4.refs_0_, bf16[1024,2048]{1,0:T(8,128)(2,1)} %get-tuple-element.178.right.refs_1_, bf16[384,4096]{1,0:T(8,128)(2,1)} %maximum_select_fusion.1.refs_2_.refs_7_.refs_12_.refs_17_, bf16[384,4096]{1,0:T(8,128)(2,1)} %collective-permute-done.9.refs_3_.refs_8_.refs_13_.refs_18_, ...), custom_call_target="tpu_custom_call" | custom-call | flops 100663296 | bytes 262144 | tf_op jit(solution)/shard_map/back_stage/pallas_call | solution.py:1084
  286.8 6.2 outer_stage.5
  302.9 16.1 %hidden_stage.3 = (bf16[1024,1024]{1,0:T(8,128)(2,1)S(1)}, bf16[1024,2048]{1,0:T(8,128)(2,1)}) custom-call(bf16[1024,1536]{1,0:T(8,128)(2,1)} %copy-done, bf16[1024,1536]{1,0:T(8,128)(2,1)} %get-tuple-element.295.refs_1_.right.upstream, bf16[384,4096]{1,0:T(8,128)(2,1)} %maximum_select_fusion.1.refs_2_.refs_7_.refs_12_.refs_17_, ...), custom_call_target="tpu_custom_call" | custom-call | flops 150994944 | bytes 344064 | tf_op jit(solution)/shard_map/hidden_stage/pallas_call | solution.py:548
  319.0 11.8 %outer_stage.6 = bf16[1536,2048]{1,0:T(8,128)(2,1)} custom-call(bf16[1024,1536]{1,0:T(8,128)(2,1)S(1)} %copy-done.2, bf16[1024,2048]{1,0:T(8,128)(2,1)} %get-tuple-element.191.right.refs_1_), custom_call_target="tpu_custom_call" | custom-call | flops 100663296 | bytes 114688 | tf_op jit(solution)/shard_map/outer_stage/pallas_call | solution.py:918
  330.8 13.1 %back_stage.3.grad = f32[1024,1536]{1,0:T(8,128)} custom-call(s32[1]{0:T(128)} %bitcast.4.refs_0_, bf16[1024,2048]{1,0:T(8,128)(2,1)} %get-tuple-element.191.right.refs_1_, bf16[384,4096]{1,0:T(8,128)(2,1)} %maximum_select_fusion.1.refs_2_.refs_7_.refs_12_.refs_17_, bf16[384,4096]{1,0:T(8,128)(2,1)} %collective-permute-done.9.refs_3_.refs_8_.refs_13_.refs_18_, ...), custom_call_target="tpu_custom_call" | custom-call | flops 100663296 | bytes 262144 | tf_op jit(solution)/shard_map/back_stage/pallas_call | solution.py:1084
  343.9 5.4 convert_element_type.244
  349.3 3.5 fusion.25
  354.0 7.1 outer_stage.7
  363.3 3.5 add_convert_fusion.1
  368.6 11.2 %down_stage.1 = f32[1024,1536]{1,0:T(8,128)} custom-call(bf16[1024,1024]{1,0:T(8,128)(2,1)S(1)} %copy-done.10, bf16[1024,1024]{1,0:T(8,128)(2,1)S(1)} %copy-done.12, bf16[1024,1536]{1,0:T(8,128)(2,1)} %bitcast.89, bf16[1024,1536]{1,0:T(8,128)(2,1)} %bitcast.91), custom_call_target="tpu_custom_call" | custom-call | flops 100663296 | bytes 163840 | tf_op jit(solution)/shard_map/down_stage/pallas_call | solution.py:945
  379.8 4.5 collective-permute-done.19
  384.3 3.2 dynamic-slice_convert_fusion.1
  387.6 2.7 add_convert_fusion.8
  390.2 2.6 collective-permute-start.23
  392.9 10.9 %norm_back_stage.1 = (f32[1024,1536]{1,0:T(8,128)}, bf16[1024,1536]{1,0:T(8,128)(2,1)S(1)}, f32[8,1536]{1,0:T(8,128)S(1)}) custom-call(f32[1024,1536]{1,0:T(8,128)} %back_stage.3.grad, bf16[1024,1536]{1,0:T(8,128)(2,1)} %collective-permute-done.18.other, f32[1024,1536]{1,0:T(8,128)} %get-tuple-element.209.middle, ...), custom_call_target="tpu_custom_call" | custom-call | flops 393216 | bytes 442368 | tf_op jit(solution)/shard_map/norm_back_stage/pallas_call | solution.py:892
  405.4 11.9 %output_back_stage.1 = (bf16[1024,1024]{1,0:T(8,128)(2,1)S(1)}, bf16[768,1536]{1,0:T(8,128)(2,1)}) custom-call(bf16[1024,1536]{1,0:T(8,128)(2,1)} %copy-done.24, bf16[1024,1024]{1,0:T(8,128)(2,1)S(1)} %copy-done.4, bf16[1024,1536]{1,0:T(8,128)(2,1)} %bitcast.94), custom_call_target="tpu_custom_call" | custom-call | flops 100663296 | bytes 196608 | tf_op jit(solution)/shard_map/output_back_stage/pallas_call | solution.py:987
  417.4 5.1 fusion.8
  422.5 5.8 collective-permute-done.23
  438.9 2.8 collective-permute-start.28
  442.4 31.6 %attention_back_stage.1 = (bf16[1024,512]{1,0:T(8,128)(2,1)S(1)}, bf16[1024,512]{1,0:T(8,128)(2,1)S(1)}, bf16[1024,512]{1,0:T(8,128)(2,1)S(1)}, bf16[1024,512]{1,0:T(8,128)(2,1)S(1)}) custom-call(bf16[1024,2048]{1,0:T(8,128)(2,1)} %get-tuple-element.159.refs_0_.refs_1_.refs_2_.refs_3_, bf16[1024,2048]{1,0:T(8,128)(2,1)} %get-tuple-element.159.refs_0_.refs_1_.refs_2_.refs_3_, ...), custom_call_target="tpu_custom_call" | custom-call | flops 83886080 | bytes 245760 | tf_op jit(solution)/shard_map/attention_back_stage/pallas_call | solution.py:760
  474.9 12.6 %collective-permute-done.25 = bf16[384,2048]{1,0:T(8,128)(2,1)} collective-permute-done((bf16[384,2048]{1,0:T(8,128)(2,1)}, bf16[384,2048]{1,0:T(8,128)(2,1)}, u32[]{:S(2)}, u32[]{:S(2)}) %collective-permute-start.25) | collective-permute-done | bytes 1572896 | tf_op jit(solution)/shard_map/ppermute | solution.py:355
  487.5 2.8 collective-permute-done.26
  492.1 3.3 add_convert_fusion
  501.6 12.6 %inputs_back_stage.1 = (f32[1024,1536]{1,0:T(8,128)}, f32[8,1536]{1,0:T(8,128)S(1)}) custom-call(s32[1]{0:T(128)} %bitcast.4.refs_0_, bf16[1024,512]{1,0:T(8,128)(2,1)S(1)} %get-tuple-element.230.refs_1_.refs_0_, bf16[1024,512]{1,0:T(8,128)(2,1)S(1)} %get-tuple-element.231.refs_2_.refs_1_, bf16[1024,512]{1,0:T(8,128)(2,1)S(1)} %get-tuple-element.232.refs_3_.refs_2_, ...), custom_call_target="tpu_custom_call" | custom-call | flops 100663296 | bytes 294912 | tf_op jit(solution)/shard_map/inputs_back_stage/pallas_call | solution.py:805
  517.0 10.4 %weight_stage.1 = bf16[1600,1536]{1,0:T(8,128)(2,1)} custom-call(bf16[1024,1536]{1,0:T(8,128)(2,1)} %copy-done.5, bf16[1024,512]{1,0:T(8,128)(2,1)S(1)} %get-tuple-element.230.refs_1_.refs_0_, bf16[1024,512]{1,0:T(8,128)(2,1)S(1)} %get-tuple-element.231.refs_2_.refs_1_, bf16[1024,512]{1,0:T(8,128)(2,1)S(1)} %get-tuple-element.232.refs_3_.refs_2_, ...), custom_call_target="tpu_custom_call" | custom-call | flops 75497472 | bytes 172032 | tf_op jit(solution)/shard_map/weight_stage/pallas_call | solution.py:1030
  527.4 3.4 dynamic-slice_convert_fusion
  532.2 3.0 collective-permute-start.31
  540.1 2.9 maximum_select_fusion.3
  544.6 8.2 %collective-permute-done.33 = bf16[200,1536]{1,0:T(8,128)(2,1)} collective-permute-done((bf16[200,1536]{1,0:T(8,128)(2,1)}, bf16[200,1536]{1,0:T(8,128)(2,1)}, u32[]{:S(2)}, u32[]{:S(2)}) %collective-permute-start.33) | collective-permute-done | bytes 614432 | tf_op jit(solution)/shard_map/ppermute | solution.py:355
  553.6 50.1 %collective-permute-done.31 = bf16[192,2048]{1,0:T(8,128)(2,1)} collective-permute-done((bf16[192,2048]{1,0:T(8,128)(2,1)S(1)}, bf16[192,2048]{1,0:T(8,128)(2,1)}, u32[]{:S(2)}, u32[]{:S(2)}) %collective-permute-start.31) | collective-permute-done | bytes 786464 | tf_op jit(solution)/shard_map/ppermute | solution.py:359
  614.7 4.7 fusion.5
  619.3 43.4 %collective-permute-done.34 = bf16[192,2048]{1,0:T(8,128)(2,1)S(1)} collective-permute-done((bf16[192,2048]{1,0:T(8,128)(2,1)S(1)}, bf16[192,2048]{1,0:T(8,128)(2,1)S(1)}, u32[]{:S(2)}, u32[]{:S(2)}) %collective-permute-start.34) | collective-permute-done | bytes 786464 | tf_op jit(solution)/shard_map/ppermute | solution.py:359
  666.5 10.8 %collective-permute-done.39 = bf16[200,1536]{1,0:T(8,128)(2,1)S(1)} collective-permute-done((bf16[200,1536]{1,0:T(8,128)(2,1)}, bf16[200,1536]{1,0:T(8,128)(2,1)S(1)}, u32[]{:S(2)}, u32[]{:S(2)}) %collective-permute-start.39) | collective-permute-done | bytes 614432 | tf_op jit(solution)/shard_map/ppermute | solution.py:359
  677.4 7.2 collective-permute-start.40
  688.4 21.3 %collective-permute-done.40 = bf16[200,1536]{1,0:T(8,128)(2,1)S(1)} collective-permute-done((bf16[200,1536]{1,0:T(8,128)(2,1)S(1)}, bf16[200,1536]{1,0:T(8,128)(2,1)S(1)}, u32[]{:S(2)}, u32[]{:S(2)}) %collective-permute-start.40) | collective-permute-done | bytes 614432 | tf_op jit(solution)/shard_map/ppermute | solution.py:359
  710.6 2.6 constant_dynamic-slice_fusion.13
  713.3 2.8 collective-permute-start.37
  719.9 7.9 %merge_ffn.1 = (f32[192,4096]{1,0:T(8,128)}, f32[192,4096]{1,0:T(8,128)}) custom-call(s32[1]{0:T(128)} %bitcast.1.core_ref, bf16[192,2048]{1,0:T(8,128)(2,1)} %get-tuple-element.272.own_0, bf16[192,2048]{1,0:T(8,128)(2,1)} %collective-permute-done.41.other_0, bf16[192,2048]{1,0:T(8,128)(2,1)} %get-tuple-element.274.own_1, ...), custom_call_target="tpu_custom_call" | custom-call | tf_op jit(solution)/shard_map/merge_ffn/pallas_call | solution.py:494
  727.8 15.6 %collective-permute-done.43 = bf16[200,1536]{1,0:T(8,128)(2,1)S(1)} collective-permute-done((bf16[200,1536]{1,0:T(8,128)(2,1)S(1)}, bf16[200,1536]{1,0:T(8,128)(2,1)S(1)}, u32[]{:S(2)}, u32[]{:S(2)}) %collective-permute-start.43) | collective-permute-done | bytes 614432 | tf_op jit(solution)/shard_map/ppermute | solution.py:359
  744.1 5.9 collective-permute-done.37
  750.1 3.8 fusion.9
  (337 shorter events, 138.2 us)
Async XLA Ops:
  7.2 194.9 %all-gather.5.cloned.1.call-start = ((), (), s32[]{:S(2)}) async-start(), calls=%async_computation.7 | async-start | bytes 3932160 | tf_op jit(solution)/shard_map/all_gather | solution.py:1212
  13.4 2.3 collective-permute-start
  17.2 51.4 %collective-permute-start.2 = (bf16[720,1536]{1,0:T(8,128)(2,1)S(1)}, bf16[720,1536]{1,0:T(8,128)(2,1)}, u32[]{:S(2)}, u32[]{:S(2)}) collective-permute-start(bf16[720,1536]{1,0:T(8,128)(2,1)S(1)} %pad_maximum_fusion.2.refs_4_), channel_id=1, source_target_pairs={{0,16},{4,20},{8,24},{12,28},{16,0},{20,4},{24,8},{28,12},{1,17},{... | collective-permute-start | bytes 6635528 | tf_op jit(solution)/shard_map/ppermute | solution.py:355
  20.1 50.0 %collective-permute-start.1 = (bf16[720,1536]{1,0:T(8,128)(2,1)S(1)}, bf16[720,1536]{1,0:T(8,128)(2,1)}, u32[]{:S(2)}, u32[]{:S(2)}) collective-permute-start(bf16[720,1536]{1,0:T(8,128)(2,1)S(1)} %pad_maximum_fusion.2.refs_4_), channel_id=1, source_target_pairs={{0,8},{4,12},{8,0},{12,4},{16,24},{20,28},{24,16},{28,20},{1,9},{5... | collective-permute-start | bytes 6635528 | tf_op jit(solution)/shard_map/ppermute | solution.py:355
  25.9 48.9 %collective-permute-start.5 = (bf16[192,4096]{1,0:T(8,128)(2,1)}, bf16[192,4096]{1,0:T(8,128)(2,1)}, u32[]{:S(2)}, u32[]{:S(2)}) collective-permute-start(bf16[192,4096]{1,0:T(8,128)(2,1)} %get-tuple-element.151), channel_id=1, source_target_pairs={{0,4},{4,0},{8,12},{12,8},{16,20},{20,16},{24,28},{28,24},{1,5},{5... | collective-permute-start | bytes 4718600 | tf_op jit(solution)/shard_map/ppermute | solution.py:355
  29.8 81.0 %collective-permute-start.7 = (bf16[512,1536]{1,0:T(8,128)(2,1)}, bf16[512,1536]{1,0:T(8,128)(2,1)}, u32[]{:S(2)}, u32[]{:S(2)}) collective-permute-start(bf16[512,1536]{1,0:T(8,128)(2,1)} %get-tuple-element.314), channel_id=1, source_target_pairs={{0,5},{1,4},{2,1},{3,0},{4,7},{5,6},{6,3},{7,2},{8,13},{9,12},{10,... | collective-permute-start | bytes 4718600 | tf_op jit(solution)/shard_map/ppermute | solution.py:369
  31.5 79.3 %collective-permute-start.6 = (bf16[512,1536]{1,0:T(8,128)(2,1)}, bf16[512,1536]{1,0:T(8,128)(2,1)}, u32[]{:S(2)}, u32[]{:S(2)}) collective-permute-start(bf16[512,1536]{1,0:T(8,128)(2,1)} %get-tuple-element.315), channel_id=1, source_target_pairs={{0,4},{1,5},{2,0},{3,1},{4,6},{5,7},{6,2},{7,3},{8,12},{9,13},{10,... | collective-permute-start | bytes 4718600 | tf_op jit(solution)/shard_map/ppermute | solution.py:369
  33.6 41.2 %copy-start.46 = (bf16[192,4096]{1,0:T(8,128)(2,1)S(1)}, bf16[192,4096]{1,0:T(8,128)(2,1)}, u32[]{:S(2)}) copy-start(bf16[192,4096]{1,0:T(8,128)(2,1)} %get-tuple-element.152) | copy-start | bytes 4718596
  71.4 24.8 %collective-permute-start.3 = (bf16[352,1536]{1,0:T(8,128)(2,1)S(1)}, bf16[352,1536]{1,0:T(8,128)(2,1)S(1)}, u32[]{:S(2)}, u32[]{:S(2)}) collective-permute-start(bf16[352,1536]{1,0:T(8,128)(2,1)S(1)} %slice.377), channel_id=1, source_target_pairs={{0,8},{4,12},{8,0},{12,4},{16,24},{20,28},{24,16},{28,20},{1,9},{5... | collective-permute-start | bytes 3244040 | tf_op jit(solution)/shard_map/ppermute | solution.py:355
  74.3 25.6 %collective-permute-start.4 = (bf16[368,1536]{1,0:T(8,128)(2,1)S(1)}, bf16[368,1536]{1,0:T(8,128)(2,1)S(1)}, u32[]{:S(2)}, u32[]{:S(2)}) collective-permute-start(bf16[368,1536]{1,0:T(8,128)(2,1)S(1)} %slice.378), channel_id=1, source_target_pairs={{0,16},{4,20},{8,24},{12,28},{16,0},{20,4},{24,8},{28,12},{1,17},{... | collective-permute-start | bytes 3391496 | tf_op jit(solution)/shard_map/ppermute | solution.py:355
  102.7 168.1 %all-gather.7.cloned.1.call-start = ((), (), s32[]{:S(2)}) async-start(), calls=%async_computation.8 | async-start | bytes 3932160 | tf_op jit(solution)/shard_map/all_gather | solution.py:1212
  105.1 35.3 %copy-start.13 = (f32[1024,128]{1,0:T(8,128)}, f32[1024,128]{1,0:T(8,128)S(1)}, u32[]{:S(2)}) copy-start(f32[1024,128]{1,0:T(8,128)S(1)} %pad.25.refs_3_.refs_10_) | copy-start | bytes 1572868
  105.2 35.3 %copy-start.15 = (f32[1024,128]{1,0:T(8,128)}, f32[1024,128]{1,0:T(8,128)S(1)}, u32[]{:S(2)}) copy-start(f32[1024,128]{1,0:T(8,128)S(1)} %pad.24.refs_2_.refs_9_) | copy-start | bytes 1572868
  115.6 11.2 %collective-permute-start.8 = (bf16[2,512,1536]{2,1,0:T(8,128)(2,1)}, bf16[2,512,1536]{2,1,0:T(8,128)(2,1)}, u32[]{:S(2)}, u32[]{:S(2)}) collective-permute-start(bf16[2,512,1536]{2,1,0:T(8,128)(2,1)} %maximum_select_fusion.2), channel_id=1, source_target_pairs={{0,4},{4,0},{8,12},{12,8},{16,20},{20,16},{24,28},{28,24},{1,5},{5... | collective-permute-start | bytes 9437192 | tf_op jit(solution)/shard_map/ppermute | solution.py:355
  117.5 70.8 %collective-permute-start.10 = (bf16[384,4096]{1,0:T(8,128)(2,1)}, bf16[384,4096]{1,0:T(8,128)(2,1)}, u32[]{:S(2)}, u32[]{:S(2)}) collective-permute-start(bf16[384,4096]{1,0:T(8,128)(2,1)} %maximum_select_fusion.1.refs_2_.refs_7_.refs_12_.refs_17_), channel_id=1, source_target_pairs={{0,16},{4,20},{8,24},{12,28},{16,0},{20,4},{24,8},{28,12},{1,17},{... | collective-permute-start | bytes 9437192 | tf_op jit(solution)/shard_map/ppermute | solution.py:355
  118.1 70.5 %collective-permute-start.9 = (bf16[384,4096]{1,0:T(8,128)(2,1)}, bf16[384,4096]{1,0:T(8,128)(2,1)}, u32[]{:S(2)}, u32[]{:S(2)}) collective-permute-start(bf16[384,4096]{1,0:T(8,128)(2,1)} %maximum_select_fusion.1.refs_2_.refs_7_.refs_12_.refs_17_), channel_id=1, source_target_pairs={{0,8},{4,12},{8,0},{12,4},{16,24},{20,28},{24,16},{28,20},{1,9},{5... | collective-permute-start | bytes 9437192 | tf_op jit(solution)/shard_map/ppermute | solution.py:355
  125.8 258.4 %reduce-scatter.4.cloned.1.call-start = ((), (), s32[]{:S(2)}) async-start(), calls=%async_computation.3 | async-start | bytes 3932160 | tf_op jit(solution)/shard_map/reduce_scatter | solution.py:1244
  157.6 31.0 %copy-start.29 = (bf16[8,128,1536]{2,1,0:T(8,128)(2,1)S(1)}, bf16[8,128,1536]{2,1,0:T(8,128)(2,1)}, u32[]{:S(2)}) copy-start(bf16[8,128,1536]{2,1,0:T(8,128)(2,1)} %pad.26) | copy-start | bytes 9437188
  194.6 11.3 %collective-permute-start.11 = (bf16[1024,1536]{1,0:T(8,128)(2,1)}, bf16[1024,1536]{1,0:T(8,128)(2,1)}, u32[]{:S(2)}, u32[]{:S(2)}) collective-permute-start(bf16[1024,1536]{1,0:T(8,128)(2,1)} %get-tuple-element.394), channel_id=1, source_target_pairs={{0,4},{4,0},{8,12},{12,8},{16,20},{20,16},{24,28},{28,24},{1,5},{5... | collective-permute-start | bytes 9437192 | tf_op jit(solution)/shard_map/ppermute | solution.py:355
  200.1 37.0 %collective-permute-start.13 = (bf16[192,4096]{1,0:T(8,128)(2,1)}, bf16[192,4096]{1,0:T(8,128)(2,1)S(1)}, u32[]{:S(2)}, u32[]{:S(2)}) collective-permute-start(bf16[192,4096]{1,0:T(8,128)(2,1)} %slice.397), channel_id=1, source_target_pairs={{0,16},{4,20},{8,24},{12,28},{16,0},{20,4},{24,8},{28,12},{1,17},{... | collective-permute-start | bytes 4718600 | tf_op jit(solution)/shard_map/ppermute | solution.py:355
  201.5 36.7 %collective-permute-start.12 = (bf16[192,4096]{1,0:T(8,128)(2,1)}, bf16[192,4096]{1,0:T(8,128)(2,1)S(1)}, u32[]{:S(2)}, u32[]{:S(2)}) collective-permute-start(bf16[192,4096]{1,0:T(8,128)(2,1)} %slice.396), channel_id=1, source_target_pairs={{0,8},{4,12},{8,0},{12,4},{16,24},{20,28},{24,16},{28,20},{1,9},{5... | collective-permute-start | bytes 4718600 | tf_op jit(solution)/shard_map/ppermute | solution.py:355
  269.8 24.9 %collective-permute-start.15 = (bf16[192,2048]{1,0:T(8,128)(2,1)}, bf16[192,2048]{1,0:T(8,128)(2,1)}, u32[]{:S(2)}, u32[]{:S(2)}) collective-permute-start(bf16[192,2048]{1,0:T(8,128)(2,1)} %get-tuple-element.306), channel_id=1, source_target_pairs={{0,16},{4,20},{8,24},{12,28},{16,0},{20,4},{24,8},{28,12},{1,17},{... | collective-permute-start | bytes 2359304 | tf_op jit(solution)/shard_map/ppermute | solution.py:355
  270.3 24.4 %collective-permute-start.14 = (bf16[192,2048]{1,0:T(8,128)(2,1)}, bf16[192,2048]{1,0:T(8,128)(2,1)}, u32[]{:S(2)}, u32[]{:S(2)}) collective-permute-start(bf16[192,2048]{1,0:T(8,128)(2,1)} %get-tuple-element.307), channel_id=1, source_target_pairs={{0,8},{4,12},{8,0},{12,4},{16,24},{20,28},{24,16},{28,20},{1,9},{5... | collective-permute-start | bytes 2359304 | tf_op jit(solution)/shard_map/ppermute | solution.py:355
  294.7 197.4 %reduce-scatter.6.cloned.1.call-start = ((), (), s32[]{:S(2)}) async-start(), calls=%async_computation.4 | async-start | bytes 3932160 | tf_op jit(solution)/shard_map/reduce_scatter | solution.py:1244
  298.7 62.4 %collective-permute-start.16 = (bf16[384,2048]{1,0:T(8,128)(2,1)}, bf16[384,2048]{1,0:T(8,128)(2,1)}, u32[]{:S(2)}, u32[]{:S(2)}) collective-permute-start(bf16[384,2048]{1,0:T(8,128)(2,1)} %pad_maximum_fusion.4), channel_id=1, source_target_pairs={{0,8},{4,12},{8,0},{12,4},{16,24},{20,28},{24,16},{28,20},{1,9},{5... | collective-permute-start | bytes 4718600 | tf_op jit(solution)/shard_map/ppermute | solution.py:355
  301.4 61.9 %collective-permute-start.17 = (bf16[384,2048]{1,0:T(8,128)(2,1)}, bf16[384,2048]{1,0:T(8,128)(2,1)}, u32[]{:S(2)}, u32[]{:S(2)}) collective-permute-start(bf16[384,2048]{1,0:T(8,128)(2,1)} %pad_maximum_fusion.5), channel_id=1, source_target_pairs={{0,16},{4,20},{8,24},{12,28},{16,0},{20,4},{24,8},{28,12},{1,17},{... | collective-permute-start | bytes 4718600 | tf_op jit(solution)/shard_map/ppermute | solution.py:355
  349.3 35.0 %collective-permute-start.18 = (bf16[1024,1536]{1,0:T(8,128)(2,1)}, bf16[1024,1536]{1,0:T(8,128)(2,1)}, u32[]{:S(2)}, u32[]{:S(2)}) collective-permute-start(bf16[1024,1536]{1,0:T(8,128)(2,1)} %convert_element_type.244), channel_id=1, source_target_pairs={{0,4},{4,0},{8,12},{12,8},{16,20},{20,16},{24,28},{28,24},{1,5},{5... | collective-permute-start | bytes 9437192 | tf_op jit(solution)/shard_map/ppermute | solution.py:355
  352.8 27.0 %collective-permute-start.21 = (bf16[192,2048]{1,0:T(8,128)(2,1)}, bf16[192,2048]{1,0:T(8,128)(2,1)}, u32[]{:S(2)}, u32[]{:S(2)}) collective-permute-start(bf16[192,2048]{1,0:T(8,128)(2,1)} %get-tuple-element.300), channel_id=1, source_target_pairs={{0,16},{4,20},{8,24},{12,28},{16,0},{20,4},{24,8},{28,12},{1,17},{... | collective-permute-start | bytes 2359304 | tf_op jit(solution)/shard_map/ppermute | solution.py:355
  353.7 26.0 %collective-permute-start.20 = (bf16[192,2048]{1,0:T(8,128)(2,1)}, bf16[192,2048]{1,0:T(8,128)(2,1)}, u32[]{:S(2)}, u32[]{:S(2)}) collective-permute-start(bf16[192,2048]{1,0:T(8,128)(2,1)} %get-tuple-element.301), channel_id=1, source_target_pairs={{0,8},{4,12},{8,0},{12,4},{16,24},{20,28},{24,16},{28,20},{1,9},{5... | collective-permute-start | bytes 2359304 | tf_op jit(solution)/shard_map/ppermute | solution.py:355
  366.9 17.3 %collective-permute-start.19 = (bf16[192,2048]{1,0:T(8,128)(2,1)S(1)}, bf16[192,2048]{1,0:T(8,128)(2,1)}, u32[]{:S(2)}, u32[]{:S(2)}) collective-permute-start(bf16[192,2048]{1,0:T(8,128)(2,1)S(1)} %constant_dynamic-slice_fusion.21), channel_id=1, source_target_pairs={{0,1},{1,0},{2,3},{3,2},{4,5},{5,4},{6,7},{7,6},{8,9},{9,8},{10,11... | collective-permute-start | bytes 2359304 | tf_op jit(solution)/shard_map/ppermute | solution.py:359
  384.3 130.5 %reduce-scatter.8.cloned.1.call-start = ((), (), s32[]{:S(2)}) async-start(), calls=%async_computation.5 | async-start | bytes 2949120 | tf_op jit(solution)/shard_map/reduce_scatter | solution.py:1244
  387.6 17.9 %collective-permute-start.22 = (bf16[512,1536]{1,0:T(8,128)(2,1)}, bf16[512,1536]{1,0:T(8,128)(2,1)}, u32[]{:S(2)}, u32[]{:S(2)}) collective-permute-start(bf16[512,1536]{1,0:T(8,128)(2,1)} %dynamic-slice_convert_fusion.1), channel_id=1, source_target_pairs={{0,4},{4,0},{8,12},{12,8},{16,20},{20,16},{24,28},{28,24},{1,5},{5... | collective-permute-start | bytes 4718600 | tf_op jit(solution)/shard_map/ppermute | solution.py:355
  387.6 29.8 %slice-start = ((s8[6291456]{0:T(1024)(128)(4,1)}), s8[2097152]{0:T(1024)(128)(4,1)S(1)}, s32[]{:S(2)}) async-start(s8[6291456]{0:T(1024)(128)(4,1)} %bitcast.92), calls=%async_computation.9 | async-start | bytes 4194304
  390.2 38.0 %collective-permute-start.23 = (bf16[192,2048]{1,0:T(8,128)(2,1)}, bf16[192,2048]{1,0:T(8,128)(2,1)}, u32[]{:S(2)}, u32[]{:S(2)}) collective-permute-start(bf16[192,2048]{1,0:T(8,128)(2,1)} %add_convert_fusion.8), channel_id=1, source_target_pairs={{0,2},{1,3},{2,0},{3,1},{4,6},{5,7},{6,4},{7,5},{8,10},{9,11},{10,... | collective-permute-start | bytes 2359304 | tf_op jit(solution)/shard_map/ppermute | solution.py:359
  392.9 24.5 %slice-start.1 = ((s8[6291456]{0:T(1024)(128)(4,1)}), s8[4194304]{0:T(1024)(128)(4,1)S(1)}, s32[]{:S(2)}) async-start(s8[6291456]{0:T(1024)(128)(4,1)} %bitcast.92), calls=%async_computation.10 | async-start | bytes 8388608
  428.3 238.2 %all-reduce.8.cloned.1.call-start = ((), (), s32[]{:S(2)}) async-start(), calls=%async_computation.6 | async-start | bytes 4325376 | tf_op jit(solution)/shard_map/psum | solution.py:1317
  432.2 55.3 %collective-permute-start.25 = (bf16[384,2048]{1,0:T(8,128)(2,1)}, bf16[384,2048]{1,0:T(8,128)(2,1)}, u32[]{:S(2)}, u32[]{:S(2)}) collective-permute-start(bf16[384,2048]{1,0:T(8,128)(2,1)} %pad_maximum_fusion.6), channel_id=1, source_target_pairs={{0,8},{4,12},{8,0},{12,4},{16,24},{20,28},{24,16},{28,20},{1,9},{5... | collective-permute-start | bytes 4718600 | tf_op jit(solution)/shard_map/ppermute | solution.py:355
  435.3 55.0 %collective-permute-start.26 = (bf16[384,2048]{1,0:T(8,128)(2,1)}, bf16[384,2048]{1,0:T(8,128)(2,1)}, u32[]{:S(2)}, u32[]{:S(2)}) collective-permute-start(bf16[384,2048]{1,0:T(8,128)(2,1)} %pad_maximum_fusion.7), channel_id=1, source_target_pairs={{0,16},{4,20},{8,24},{12,28},{16,0},{20,4},{24,8},{28,12},{1,17},{... | collective-permute-start | bytes 4718600 | tf_op jit(solution)/shard_map/ppermute | solution.py:355
  438.0 35.9 %copy-start.40 = (bf16[192,2048]{1,0:T(8,128)(2,1)}, bf16[192,2048]{1,0:T(8,128)(2,1)S(1)}, u32[]{:S(2)}) copy-start(bf16[192,2048]{1,0:T(8,128)(2,1)S(1)} %add_convert_fusion.7) | copy-start | bytes 2359300
  438.0 52.3 %collective-permute-start.24 = (bf16[192,2048]{1,0:T(8,128)(2,1)S(1)}, bf16[192,2048]{1,0:T(8,128)(2,1)S(1)}, u32[]{:S(2)}, u32[]{:S(2)}) collective-permute-start(bf16[192,2048]{1,0:T(8,128)(2,1)S(1)} %add_convert_fusion.7), channel_id=1, source_target_pairs={{0,1},{1,0},{2,3},{3,2},{4,5},{5,4},{6,7},{7,6},{8,9},{9,8},{10,11... | collective-permute-start | bytes 2359304 | tf_op jit(solution)/shard_map/ppermute | solution.py:359
  438.9 51.4 %collective-permute-start.28 = (bf16[256,1536]{1,0:T(8,128)(2,1)S(1)}, bf16[256,1536]{1,0:T(8,128)(2,1)S(1)}, u32[]{:S(2)}, u32[]{:S(2)}) collective-permute-start(bf16[256,1536]{1,0:T(8,128)(2,1)S(1)} %get-tuple-element.346), channel_id=1, source_target_pairs={{5,0},{4,1},{1,2},{0,3},{7,4},{6,5},{3,6},{2,7},{13,8},{12,9},{9,1... | collective-permute-start | bytes 2359304 | tf_op jit(solution)/shard_map/ppermute | solution.py:369
  441.8 50.3 %collective-permute-start.27 = (bf16[256,1536]{1,0:T(8,128)(2,1)S(1)}, bf16[256,1536]{1,0:T(8,128)(2,1)}, u32[]{:S(2)}, u32[]{:S(2)}) collective-permute-start(bf16[256,1536]{1,0:T(8,128)(2,1)S(1)} %get-tuple-element.347), channel_id=1, source_target_pairs={{4,0},{5,1},{0,2},{1,3},{6,4},{7,5},{2,6},{3,7},{12,8},{13,9},{8,1... | collective-permute-start | bytes 2359304 | tf_op jit(solution)/shard_map/ppermute | solution.py:369
  497.5 18.3 %collective-permute-start.29 = (bf16[192,2048]{1,0:T(8,128)(2,1)}, bf16[192,2048]{1,0:T(8,128)(2,1)}, u32[]{:S(2)}, u32[]{:S(2)}) collective-permute-start(bf16[192,2048]{1,0:T(8,128)(2,1)} %constant_dynamic-slice_fusion.14), channel_id=1, source_target_pairs={{0,1},{1,0},{2,3},{3,2},{4,5},{5,4},{6,7},{7,6},{8,9},{9,8},{10,11... | collective-permute-start | bytes 2359304 | tf_op jit(solution)/shard_map/ppermute | solution.py:359
  530.8 72.9 %collective-permute-start.30 = (bf16[512,1536]{1,0:T(8,128)(2,1)}, bf16[512,1536]{1,0:T(8,128)(2,1)}, u32[]{:S(2)}, u32[]{:S(2)}) collective-permute-start(bf16[512,1536]{1,0:T(8,128)(2,1)} %dynamic-slice_convert_fusion), channel_id=1, source_target_pairs={{0,4},{4,0},{8,12},{12,8},{16,20},{20,16},{24,28},{28,24},{1,5},{5... | collective-permute-start | bytes 4718600 | tf_op jit(solution)/shard_map/ppermute | solution.py:355
  532.2 71.4 %collective-permute-start.31 = (bf16[192,2048]{1,0:T(8,128)(2,1)S(1)}, bf16[192,2048]{1,0:T(8,128)(2,1)}, u32[]{:S(2)}, u32[]{:S(2)}) collective-permute-start(bf16[192,2048]{1,0:T(8,128)(2,1)S(1)} %add_convert_fusion.4), channel_id=1, source_target_pairs={{0,2},{1,3},{2,0},{3,1},{4,6},{5,7},{6,4},{7,5},{8,10},{9,11},{10,... | collective-permute-start | bytes 2359304 | tf_op jit(solution)/shard_map/ppermute | solution.py:359
  536.5 16.3 %collective-permute-start.33 = (bf16[200,1536]{1,0:T(8,128)(2,1)}, bf16[200,1536]{1,0:T(8,128)(2,1)}, u32[]{:S(2)}, u32[]{:S(2)}) collective-permute-start(bf16[200,1536]{1,0:T(8,128)(2,1)} %get-tuple-element.312), channel_id=1, source_target_pairs={{0,16},{4,20},{8,24},{12,28},{16,0},{20,4},{24,8},{28,12},{1,17},{... | collective-permute-start | bytes 1843208 | tf_op jit(solution)/shard_map/ppermute | solution.py:355
  537.6 16.0 %collective-permute-start.32 = (bf16[200,1536]{1,0:T(8,128)(2,1)}, bf16[200,1536]{1,0:T(8,128)(2,1)}, u32[]{:S(2)}, u32[]{:S(2)}) collective-permute-start(bf16[200,1536]{1,0:T(8,128)(2,1)} %get-tuple-element.313), channel_id=1, source_target_pairs={{0,8},{4,12},{8,0},{12,4},{16,24},{20,28},{24,16},{28,20},{1,9},{5... | collective-permute-start | bytes 1843208 | tf_op jit(solution)/shard_map/ppermute | solution.py:355
  543.1 69.1 %slice-start.2 = ((s8[6291456]{0:T(1024)(128)(4,1)}), s8[2097152]{0:T(1024)(128)(4,1)S(1)}, s32[]{:S(2)}) async-start(s8[6291456]{0:T(1024)(128)(4,1)} %bitcast.96), calls=%async_computation.11 | async-start | bytes 4194304
  544.6 67.6 %slice-start.3 = ((s8[6291456]{0:T(1024)(128)(4,1)}), s8[4194304]{0:T(1024)(128)(4,1)S(1)}, s32[]{:S(2)}) async-start(s8[6291456]{0:T(1024)(128)(4,1)} %bitcast.96), calls=%async_computation.12 | async-start | bytes 8388608
  606.8 56.0 %collective-permute-start.35 = (bf16[400,1536]{1,0:T(8,128)(2,1)S(1)}, bf16[400,1536]{1,0:T(8,128)(2,1)S(1)}, u32[]{:S(2)}, u32[]{:S(2)}) collective-permute-start(bf16[400,1536]{1,0:T(8,128)(2,1)S(1)} %pad_maximum_fusion.8), channel_id=1, source_target_pairs={{0,8},{4,12},{8,0},{12,4},{16,24},{20,28},{24,16},{28,20},{1,9},{5... | collective-permute-start | bytes 3686408 | tf_op jit(solution)/shard_map/ppermute | solution.py:355
  607.4 55.4 %collective-permute-start.36 = (bf16[400,1536]{1,0:T(8,128)(2,1)S(1)}, bf16[400,1536]{1,0:T(8,128)(2,1)S(1)}, u32[]{:S(2)}, u32[]{:S(2)}) collective-permute-start(bf16[400,1536]{1,0:T(8,128)(2,1)S(1)} %pad_maximum_fusion.9), channel_id=1, source_target_pairs={{0,16},{4,20},{8,24},{12,28},{16,0},{20,4},{24,8},{28,12},{1,17},{... | collective-permute-start | bytes 3686408 | tf_op jit(solution)/shard_map/ppermute | solution.py:355
  610.4 52.4 %collective-permute-start.34 = (bf16[192,2048]{1,0:T(8,128)(2,1)S(1)}, bf16[192,2048]{1,0:T(8,128)(2,1)S(1)}, u32[]{:S(2)}, u32[]{:S(2)}) collective-permute-start(bf16[192,2048]{1,0:T(8,128)(2,1)S(1)} %add_convert_fusion.3), channel_id=1, source_target_pairs={{0,1},{1,0},{2,3},{3,2},{4,5},{5,4},{6,7},{7,6},{8,9},{9,8},{10,11... | collective-permute-start | bytes 2359304 | tf_op jit(solution)/shard_map/ppermute | solution.py:359
  664.8 19.9 %copy-start.35 = (bf16[384,2048]{1,0:T(8,128)(2,1)S(1)}, bf16[384,2048]{1,0:T(8,128)(2,1)}, u32[]{:S(2)}) copy-start(bf16[384,2048]{1,0:T(8,128)(2,1)} %maximum_select_fusion.4) | copy-start | bytes 4718596
  665.7 11.6 %collective-permute-start.39 = (bf16[200,1536]{1,0:T(8,128)(2,1)}, bf16[200,1536]{1,0:T(8,128)(2,1)S(1)}, u32[]{:S(2)}, u32[]{:S(2)}) collective-permute-start(bf16[200,1536]{1,0:T(8,128)(2,1)} %constant_dynamic-slice_fusion.11), channel_id=1, source_target_pairs={{0,1},{1,0},{2,3},{3,2},{4,5},{5,4},{6,7},{7,6},{8,9},{9,8},{10,11... | collective-permute-start | bytes 1843208 | tf_op jit(solution)/shard_map/ppermute | solution.py:359
  666.5 19.5 %copy-start.43 = (bf16[192,2048]{1,0:T(8,128)(2,1)S(1)}, bf16[192,2048]{1,0:T(8,128)(2,1)}, u32[]{:S(2)}) copy-start(bf16[192,2048]{1,0:T(8,128)(2,1)} %copy-done.42) | copy-start | bytes 2359300
  666.5 19.5 %copy-start.57 = (bf16[192,2048]{1,0:T(8,128)(2,1)S(1)}, bf16[192,2048]{1,0:T(8,128)(2,1)}, u32[]{:S(2)}) copy-start(bf16[192,2048]{1,0:T(8,128)(2,1)} %copy-done.56) | copy-start | bytes 2359300
  677.4 32.2 %collective-permute-start.40 = (bf16[200,1536]{1,0:T(8,128)(2,1)S(1)}, bf16[200,1536]{1,0:T(8,128)(2,1)S(1)}, u32[]{:S(2)}, u32[]{:S(2)}) collective-permute-start(bf16[200,1536]{1,0:T(8,128)(2,1)S(1)} %add_convert_fusion.12), channel_id=1, source_target_pairs={{0,2},{1,3},{2,0},{3,1},{4,6},{5,7},{6,4},{7,5},{8,10},{9,11},{10,... | collective-permute-start | bytes 1843208 | tf_op jit(solution)/shard_map/ppermute | solution.py:359
  685.9 33.9 %collective-permute-start.41 = (bf16[192,2048]{1,0:T(8,128)(2,1)}, bf16[192,2048]{1,0:T(8,128)(2,1)}, u32[]{:S(2)}, u32[]{:S(2)}) collective-permute-start(bf16[192,2048]{1,0:T(8,128)(2,1)} %get-tuple-element.342), channel_id=1, source_target_pairs={{0,4},{4,0},{8,12},{12,8},{16,20},{20,16},{24,28},{28,24},{1,5},{5... | collective-permute-start | bytes 2359304 | tf_op jit(solution)/shard_map/ppermute | solution.py:355
  687.9 28.7 %copy-start.30 = (bf16[704,1536]{1,0:T(8,128)(2,1)S(1)}, bf16[704,1536]{1,0:T(8,128)(2,1)}, u32[]{:S(2)}) copy-start(bf16[704,1536]{1,0:T(8,128)(2,1)} %all-reduce.8.cloned.1.call-done) | copy-start | bytes 6488068
  687.9 32.0 %collective-permute-start.42 = (bf16[192,2048]{1,0:T(8,128)(2,1)}, bf16[192,2048]{1,0:T(8,128)(2,1)}, u32[]{:S(2)}, u32[]{:S(2)}) collective-permute-start(bf16[192,2048]{1,0:T(8,128)(2,1)} %get-tuple-element.340), channel_id=1, source_target_pairs={{0,4},{4,0},{8,12},{12,8},{16,20},{20,16},{24,28},{28,24},{1,5},{5... | collective-permute-start | bytes 2359304 | tf_op jit(solution)/shard_map/ppermute | solution.py:355
  709.9 33.5 %collective-permute-start.43 = (bf16[200,1536]{1,0:T(8,128)(2,1)S(1)}, bf16[200,1536]{1,0:T(8,128)(2,1)S(1)}, u32[]{:S(2)}, u32[]{:S(2)}) collective-permute-start(bf16[200,1536]{1,0:T(8,128)(2,1)S(1)} %add_convert_fusion.11), channel_id=1, source_target_pairs={{0,1},{1,0},{2,3},{3,2},{4,5},{5,4},{6,7},{7,6},{8,9},{9,8},{10,11... | collective-permute-start | bytes 1843208 | tf_op jit(solution)/shard_map/ppermute | solution.py:359
  713.3 36.8 %collective-permute-start.37 = (bf16[256,1536]{1,0:T(8,128)(2,1)}, bf16[256,1536]{1,0:T(8,128)(2,1)}, u32[]{:S(2)}, u32[]{:S(2)}) collective-permute-start(bf16[256,1536]{1,0:T(8,128)(2,1)} %get-tuple-element.344), channel_id=1, source_target_pairs={{5,0},{4,1},{1,2},{0,3},{7,4},{6,5},{3,6},{2,7},{13,8},{12,9},{9,1... | collective-permute-start | bytes 2359304 | tf_op jit(solution)/shard_map/ppermute | solution.py:369
  716.1 34.0 %collective-permute-start.38 = (bf16[256,1536]{1,0:T(8,128)(2,1)}, bf16[256,1536]{1,0:T(8,128)(2,1)}, u32[]{:S(2)}, u32[]{:S(2)}) collective-permute-start(bf16[256,1536]{1,0:T(8,128)(2,1)} %get-tuple-element.345), channel_id=1, source_target_pairs={{4,0},{5,1},{0,2},{1,3},{6,4},{7,5},{2,6},{3,7},{12,8},{13,9},{8,1... | collective-permute-start | bytes 2359304 | tf_op jit(solution)/shard_map/ppermute | solution.py:369
  744.1 9.9 %collective-permute-start.44 = (bf16[200,1536]{1,0:T(8,128)(2,1)S(1)}, bf16[200,1536]{1,0:T(8,128)(2,1)S(1)}, u32[]{:S(2)}, u32[]{:S(2)}) collective-permute-start(bf16[200,1536]{1,0:T(8,128)(2,1)S(1)} %pad_maximum_fusion.15), channel_id=1, source_target_pairs={{0,4},{4,0},{8,12},{12,8},{16,20},{20,16},{24,28},{28,24},{1,5},{5... | collective-permute-start | bytes 1843208 | tf_op jit(solution)/shard_map/ppermute | solution.py:355
  (52 other events, 267.9 us)
Sparse Core Ops, SparseCore 0:
  102.8 62.9 all-gather.4
  167.4 62.1 all-gather.6
  294.8 70.4 reduce-scatter.3
  384.4 44.9 reduce-scatter.5
  432.3 56.4 reduce-scatter.7
  544.7 121.6 all-reduce.7
